TPU v7x, 128 devices: a whole 4x4x4 slice. The times are simulated.
128 devices in a mesh: rows: 16 (over y, z), seq: 8 (over x, core).
Axes of the slice: x: 4, y: 4, z: 4, core: 2. Of those that a mesh axis runs over, the one named last changes fastest.
Arguments:
- residual_in: bfloat16 [16, 2048, 3200], P('rows', 'seq'), may hold values from -6 to 6
- norm_gain: float32 [3200], replicated, may hold values from 0.1 to 1.9
- qkv_weight: bfloat16 [3200, 6144], P(None, 'seq')
- qk_gain: float32 [2, 2048], P(None, 'seq')
- out_weight: bfloat16 [2048, 3200], P('seq'), may hold values from -0.125 to 0.125
- layer_scale: float32 [3200], replicated, may hold values from 1 to 6
- segment_ids: int32 [16, 2048], P('rows', 'seq'), may hold values from 0 to 2, as said below
- pad_mask: int32 [16, 2048], P('rows', 'seq'), may hold values from 0 to 1, as said below
- ln_weight: float32 [12800], replicated, may hold values from 0.1 to 1.9
- ln_bias: float32 [12800], replicated, may hold values from -3 to 3
- fc_weight: bfloat16 [12800, 6144], P('rows'), may hold values from -0.0546875 to 0.0546875
- fc_bias: float32 [6144], replicated, may hold values from -3 to 3
- owner: int32 [16], replicated, may hold values from 0 to 15, each once
Outputs:
- features: bfloat16 [16, 512, 6144], P('rows', 'seq')
Inputs may be any that keep to these rules, and one draw needn't show every extreme that they name: `segment_ids`: within a row, segment ids never fall and change only at multiples of 1024 tokens; picture tokens carry ids below 2, padding tokens carry 2 and stand at the end of the row; the first tile is never padding. pad_mask is 0 exactly where segment_ids equals 2. `owner`: each index of rows owns exactly one row.
All inputs are finite; a program needn't handle non-finite values.
Results may differ from a plain program's by a relative error of at most 0.025.
Values may be sent and summed in bfloat16 or wider, within the bound.
A program may use at most 128 MiB of HBM per device.

v0:
```python
import functools

import jax
import jax.numpy as jnp
from jax import lax
from jax.experimental import pallas as pl
from jax.experimental.pallas import tpu as pltpu
from jax.sharding import PartitionSpec as P

MESH = pl.DeviceIdType.MESH

D = 3200
HEAD_DIM = 128
HEADS = 16
GRID = 32
MASK_SHIFT = 1e6


def seq_sum_kernel(part_ref, out_ref, slots, send_sem, recv_sem):
    n = slots.shape[0]
    me = lax.axis_index("seq")
    row = lax.axis_index("rows")
    barrier = pltpu.get_barrier_semaphore()
    for k in range(1, n):
        peer = lax.rem(me + k, n)
        pl.semaphore_signal(barrier, inc=1, device_id=(row, peer), device_id_type=MESH)
    pl.semaphore_wait(barrier, n - 1)
    sends = []
    for k in range(1, n):
        peer = lax.rem(me + k, n)
        copy = pltpu.make_async_remote_copy(
            src_ref=part_ref,
            dst_ref=slots.at[me],
            send_sem=send_sem.at[k],
            recv_sem=recv_sem.at[me],
            device_id=(row, peer),
            device_id_type=MESH,
        )
        copy.start()
        sends.append(copy)
    for k in range(1, n):
        src = lax.rem(me + n - k, n)
        pltpu.make_async_remote_copy(
            src_ref=part_ref,
            dst_ref=slots.at[src],
            send_sem=send_sem.at[k],
            recv_sem=recv_sem.at[src],
            device_id=(row, src),
            device_id_type=MESH,
        ).wait_recv()
    for copy in sends:
        copy.wait_send()
    total = jnp.zeros(out_ref.shape, jnp.float32)
    for s in range(n):
        total = total + jnp.where(s == me, part_ref[...], slots[s])
    out_ref[...] = total


def seq_sum(part):
    n = lax.axis_size("seq")
    return pl.pallas_call(
        seq_sum_kernel,
        out_shape=jax.ShapeDtypeStruct(part.shape, jnp.float32),
        in_specs=[pl.BlockSpec(memory_space=pltpu.VMEM)],
        out_specs=pl.BlockSpec(memory_space=pltpu.VMEM),
        scratch_shapes=[
            pltpu.VMEM((n,) + part.shape, jnp.float32),
            pltpu.SemaphoreType.DMA((n,)),
            pltpu.SemaphoreType.DMA((n,)),
        ],
        compiler_params=pltpu.CompilerParams(collective_id=0, has_side_effects=True),
    )(part)


def attention_kernel(scale, q_ref, k_ref, v_ref, qseg_ref, kseg_ref, o_ref):
    scores = (
        lax.dot_general(
            q_ref[...], k_ref[...], (((1,), (1,)), ((), ())), preferred_element_type=jnp.float32
        )
        * scale
    )
    scores = jnp.where(qseg_ref[...] == kseg_ref[...], scores, -1e30)
    peak_val = jnp.max(scores, axis=-1, keepdims=True)
    exp_terms = jnp.exp(scores - peak_val)
    total = jnp.sum(exp_terms, axis=-1, keepdims=True)
    probs = (exp_terms / total).astype(jnp.bfloat16)
    o_ref[...] = jnp.dot(probs, v_ref[...], preferred_element_type=jnp.float32).astype(o_ref.dtype)


def attend_kernel(query_norm, key_norm, value_half, row_segments, block_len, scale):
    length, width = query_norm.shape
    heads_here = width // HEAD_DIM
    q2, k2, v2 = query_norm, key_norm, value_half
    flops = 4 * length * length * width
    return pl.pallas_call(
        functools.partial(attention_kernel, scale),
        out_shape=jax.ShapeDtypeStruct((length, width), jnp.bfloat16),
        grid=(heads_here, length // block_len),
        in_specs=[
            pl.BlockSpec((block_len, HEAD_DIM), lambda h, i: (i, h)),
            pl.BlockSpec((length, HEAD_DIM), lambda h, i: (0, h)),
            pl.BlockSpec((length, HEAD_DIM), lambda h, i: (0, h)),
            pl.BlockSpec((block_len, 1), lambda h, i: (i, 0)),
            pl.BlockSpec((1, length), lambda h, i: (0, 0)),
        ],
        out_specs=pl.BlockSpec((block_len, HEAD_DIM), lambda h, i: (i, h)),
        cost_estimate=pl.CostEstimate(
            flops=flops, transcendentals=length * length * heads_here, bytes_accessed=8 * length * width
        ),
    )(q2, k2, v2, row_segments.reshape(length, 1), row_segments.reshape(1, length))


def per_device(
    residual_in,
    norm_gain,
    qkv_weight,
    qk_gain,
    out_weight,
    layer_scale,
    segment_ids,
    pad_mask,
    ln_weight,
    ln_bias,
    fc_weight,
    fc_bias,
    owner,
):
    seq_count = lax.axis_size("seq")
    seq_me = lax.axis_index("seq")
    tokens = residual_in[0].astype(jnp.float32)
    shard_rows = tokens.shape[0]
    normed = (
        tokens * lax.rsqrt(jnp.mean(tokens * tokens, axis=-1, keepdims=True) + 1e-06) * norm_gain
    ).astype(jnp.bfloat16)
    row_tokens = lax.all_gather(normed, "seq", axis=0, tiled=True)
    length = row_tokens.shape[0]
    heads_here = qkv_weight.shape[1] // (3 * HEAD_DIM)
    weight_parts = qkv_weight.reshape(qkv_weight.shape[0], heads_here, 3, HEAD_DIM)
    query_raw, key_raw, value_raw = (
        jnp.dot(
            row_tokens,
            weight_parts[:, :, c].reshape(qkv_weight.shape[0], heads_here * HEAD_DIM),
            preferred_element_type=jnp.float32,
        )
        for c in range(3)
    )
    value_half = value_raw.astype(jnp.bfloat16)
    seg_spread = lax.dynamic_update_slice_in_dim(
        jnp.zeros((length,), jnp.float32),
        segment_ids[0].astype(jnp.float32),
        seq_me * shard_rows,
        0,
    )
    stats = seq_sum(
        jnp.stack(
            [
                jnp.sum(query_raw * query_raw, axis=1),
                jnp.sum(key_raw * key_raw, axis=1),
                seg_spread,
            ]
        )
    )
    query_sq, key_sq, row_segments = stats[0], stats[1], stats[2]
    norm_width = HEADS * HEAD_DIM
    query_norm = (
        query_raw * lax.rsqrt(query_sq / norm_width + 1e-06)[:, None] * qk_gain[0]
    ).astype(jnp.bfloat16)
    key_norm = (
        key_raw * lax.rsqrt(key_sq / norm_width + 1e-06)[:, None] * qk_gain[1]
    ).astype(jnp.bfloat16)
    scale = HEAD_DIM ** (-0.5)
    attended = attend_kernel(query_norm, key_norm, value_half, row_segments, 256, scale)
    group_width = attended.shape[1]
    own_heads = lax.all_to_all(
        attended.reshape(seq_count, shard_rows, group_width), "seq", 0, 0
    )
    full_out_weight = lax.all_gather(out_weight, "seq", axis=0, tiled=False)
    group_terms = jnp.einsum(
        "gtc,gcd->gtd", own_heads, full_out_weight, preferred_element_type=jnp.float32
    ).astype(jnp.bfloat16)
    attn = jnp.sum(group_terms.astype(jnp.float32), axis=0)
    hidden = tokens + layer_scale * attn
    half_grid = GRID // 2
    lines = shard_rows // (2 * GRID)
    merged_count = shard_rows // 4
    merged = jnp.transpose(hidden.reshape(lines, 2, half_grid, 2, D), (0, 2, 1, 3, 4)).reshape(
        merged_count, 4 * D
    )
    centre = merged - jnp.mean(merged, axis=-1, keepdims=True)
    spread = jnp.mean(centre * centre, axis=-1, keepdims=True)
    merged_norm = (centre * lax.rsqrt(spread + 1e-05) * ln_weight + ln_bias).astype(jnp.bfloat16)
    merged_mask = (
        pad_mask[0]
        .reshape(lines, 2, half_grid, 2)[:, 0, :, 0]
        .reshape(merged_count)
        .astype(jnp.float32)
    )
    row_count = lax.axis_size("rows")
    row_me = lax.axis_index("rows")
    slabs = lax.all_to_all(merged_norm, "rows", split_axis=1, concat_axis=0, tiled=True)
    owner_hot = (owner[None, :] == jnp.arange(row_count, dtype=jnp.int32)[:, None]).astype(
        jnp.bfloat16
    )
    ordered = jnp.einsum(
        "jp,pms->jms",
        owner_hot,
        slabs.reshape(row_count, merged_count, -1),
        preferred_element_type=jnp.float32,
    ).astype(jnp.bfloat16)
    ordered = ordered.reshape(row_count * merged_count, -1)
    partial = jnp.dot(ordered, fc_weight, preferred_element_type=jnp.float32).reshape(
        row_count, merged_count, -1
    )
    own_slot = (jnp.arange(row_count, dtype=jnp.int32) == owner[row_me]).astype(jnp.float32)
    shift = own_slot[:, None] * ((merged_mask - 1.0) * MASK_SHIFT)[None, :]
    partial = (partial + shift[:, :, None]).astype(jnp.bfloat16)
    summed = lax.psum_scatter(
        partial.reshape(row_count * merged_count, -1),
        "rows",
        scatter_dimension=0,
        tiled=True,
    ).astype(jnp.float32)
    result = jax.nn.gelu(summed + fc_bias, approximate=False)
    return result.astype(jnp.bfloat16)[None]


def solution(mesh):
    return jax.shard_map(
        per_device,
        mesh=mesh,
        in_specs=(
            P("rows", "seq", None),
            P(),
            P(None, "seq"),
            P(None, "seq"),
            P("seq", None),
            P(),
            P("rows", "seq"),
            P("rows", "seq"),
            P(),
            P(),
            P("rows", None),
            P(),
            P(),
        ),
        out_specs=P("rows", "seq", None),
        check_vma=False,
    )
```

profile of v0, /device:TPU:1, one launch (start us, length us, event | category | flops | bytes accessed | tf_op | source)
XLA Modules:
  0.0 364.4 jit_solution(5949711592976109138)
XLA Ops:
  6.5 0.0 all-gather.4.cloned.1.call-start
  6.5 2.0 fusion.1
  8.5 0.0 copy-done
  8.5 2.4 fusion.3
  10.9 0.0 all-gather.4.cloned.1.call-update
  10.9 0.0 all-gather.6.cloned.1.call-start
  10.9 0.7 all-gather.6.cloned.1.call-update
  11.7 0.0 copy-start.9
  11.7 0.0 copy-start.8
  11.7 7.5 %copy.28 = bf16[3200,768]{0,1:T(8,128)(2,1)} copy(bf16[3200,768]{1,0:T(8,128)(2,1)} %param.15) | data formatting | bytes 9830400 | tf_op args[2]
  19.2 0.0 copy-done.9
  19.2 0.0 copy-done.8
  19.2 4.5 %fusion.32 = (bf16[3200,2,1,128]{0,3,2,1:T(8,128)(2,1)S(1)}, bf16[3200,2,1,128]{0,3,2,1:T(8,128)(2,1)}, bf16[3200,2,1,128]{0,3,2,1:T(8,128)(2,1)}) fusion(bf16[3200,2,3,128]{0,3,2,1:T(8,128)(2,1)} %bitcast.49), kind=kLoop, calls=%fused_computation.62 | loop fusion | bytes 9830400 | tf_op jit(solution)/shard_map/slice | solution.py:142
  23.7 60.5 %all-gather.4.cloned.1.call-done = bf16[2048,3200]{1,0:T(8,128)(2,1)} async-done(((bf16[256,3200]{1,0:T(8,128)(2,1)}), bf16[2048,3200]{1,0:T(8,128)(2,1)}) %all-gather.4.cloned.1.call-update) | async-done | bytes 13107216 | tf_op jit(solution)/shard_map/all_gather | solution.py:135
  84.2 10.4 %multiply_reduce_fusion.2 = (f32[2048]{0:T(1024)S(1)}, f32[2048,256]{0,1:T(8,128)}) fusion(bf16[2048,3200]{1,0:T(8,128)(2,1)} %all-gather.4.cloned.1.call-done, bf16[3200,256]{0,1:T(8,128)(2,1)} %bitcast.53), kind=kOutput, calls=%fused_computation.16 | convolution fusion | flops 3356489728 | bytes 16850944 | tf_op jit(solution)/shard_map/dot_general | solution.py:140
  94.6 0.0 copy-done.2
  94.6 0.0 copy-done.12
  94.6 5.0 %multiply_reduce_fusion.1 = (f32[2048]{0:T(1024)S(1)}, f32[2048,256]{0,1:T(8,128)}) fusion(bf16[2048,3200]{1,0:T(8,128)(2,1)S(1)} %copy-done.12, bf16[3200,256]{0,1:T(8,128)(2,1)S(1)} %bitcast.52), kind=kOutput, calls=%fused_computation.15 | convolution fusion | flops 3356489728 | bytes 16850944 | tf_op jit(solution)/shard_map/dot_general | solution.py:140
  99.7 0.6 pad_maximum_fusion.part_ref
  100.3 11.7 %shard_map.127 = f32[3,2048]{1,0:T(4,128)} custom-call(f32[3,2048]{1,0:T(4,128)} %pad_maximum_fusion.part_ref), custom_call_target="tpu_custom_call" | custom-call | tf_op jit(solution)/shard_map/pallas_call | solution.py:61
  112.0 2.9 copy.29
  114.9 3.0 copy.30
  117.9 0.0 copy-done.3
  117.9 0.6 fusion.33
  118.5 1.4 copy.31.qseg_ref
  119.9 3.5 multiply_convert_fusion
  123.4 9.7 %convolution_convert_fusion.v_ref = bf16[2048,256]{1,0:T(8,128)(2,1)} fusion(bf16[2048,3200]{1,0:T(8,128)(2,1)} %all-gather.4.cloned.1.call-done, bf16[3200,256]{0,1:T(8,128)(2,1)S(1)} %bitcast.51), kind=kOutput, calls=%fused_computation.11 | convolution fusion | flops 3355967488 | bytes 15794176 | tf_op jit(solution)/shard_map/dot_general | solution.py:140
  133.1 23.8 %shard_map.128 = bf16[2048,256]{1,0:T(8,128)(2,1)} custom-call(bf16[2048,256]{1,0:T(8,128)(2,1)} %get-tuple-element.21.q_ref, bf16[2048,256]{1,0:T(8,128)(2,1)} %get-tuple-element.20.k_ref, bf16[2048,256]{1,0:T(8,128)(2,1)} %convolution_convert_fusion.v_ref, f32[2048,1]{1,0:T(8,128)} %copy.31.qseg_ref, f32[1,2048]{1,0:T(1,128)} %get-tuple-element.10.kseg_ref), custom_call_target="tpu_custom_call" | custom-call | flops 4294967296 | bytes 4194304 | tf_op jit(solution)/shard_map/pallas_call | solution.py:95
  156.8 3.8 %all-to-all-start = ((bf16[8,256,256]{2,1,0:T(8,128)(2,1)}), bf16[8,256,256]{2,1,0:T(8,128)(2,1)S(1)}, u32[]{:S(2)}, u32[]{:S(2)}) async-start(bf16[8,256,256]{2,1,0:T(8,128)(2,1)} %bitcast.54), calls=%async_computation | async-start | bytes 2097152 | tf_op jit(solution)/shard_map/all_to_all | solution.py:174
  160.6 2.8 reshape.174
  163.4 0.0 copy-done.4
  163.5 0.1 add.92
  163.5 0.0 copy-done.5
  163.6 0.1 mul.165
  163.7 0.0 all-gather.6.cloned.1.call-done
  163.7 12.1 %all-to-all-done = bf16[8,256,256]{2,1,0:T(8,128)(2,1)S(1)} async-done(((bf16[8,256,256]{2,1,0:T(8,128)(2,1)}), bf16[8,256,256]{2,1,0:T(8,128)(2,1)S(1)}, u32[]{:S(2)}, u32[]{:S(2)}) %all-to-all-start) | async-done | bytes 1048608 | tf_op jit(solution)/shard_map/all_to_all | solution.py:174
  175.7 10.6 %convert_reduce_fusion = f32[256,3200]{1,0:T(8,128)} fusion(bf16[8,256,256]{2,1,0:T(8,128)(2,1)S(1)} %all-to-all-done, bf16[8,256,3200]{2,1,0:T(8,128)(2,1)} %bitcast.61), kind=kOutput, calls=%fused_computation | convolution fusion | flops 3374284800 | bytes 17432576 | tf_op jit(solution)/shard_map/gtc,gcd->gtd/dot_general | solution.py:178
  186.3 5.3 %reduce_sum.60 = f32[4,2,16,2,3200]{4,3,2,1,0:T(2,128)} reshape(f32[256,3200]{1,0:T(8,128)} %convert_reduce_fusion) | data formatting | bytes 6553600 | tf_op jit(solution)/shard_map/reduce_sum | solution.py:181
  191.6 0.0 copy-done.1
  191.6 4.2 %fusion.31 = (f32[4,16]{1,0:T(4,128)S(1)}, f32[4,16,2,2,3200]{4,3,1,2,0:T(2,128)S(1)}) fusion(f32[4,2,16,2,3200]{4,3,2,1,0:T(2,128)S(1)} %copy-done.1, f32[4,2,16,2,3200]{4,3,2,1,0:T(2,128)} %reduce_sum.60, f32[3200]{0:T(1024)S(1)} %copy-done.7), kind=kLoop, calls=%fused_computation.61 | loop fusion | flops 2457536 | bytes 9843456 | tf_op jit(solution)/shard_map/reduce_sum | solution.py:189
  195.9 0.3 copy.32
  196.2 1.9 multiply_reduce_fusion
  198.1 0.1 div.25
  198.2 0.1 rsqrt.45
  198.2 4.5 %reshape.172 = f32[64,16,800]{2,1,0:T(8,128)} reshape(f32[4,16,2,2,3200]{4,3,2,1,0:T(2,128)S(1)} %copy.32) | data formatting | bytes 6553600 | tf_op jit(solution)/shard_map/reshape | solution.py:186
  202.7 2.7 add_convert_fusion.1
  205.5 1.7 copy.33
  207.1 6.8 %all-to-all-start.1 = ((bf16[64,16,800]{2,0,1:T(8,128)(2,1)}), bf16[64,16,800]{2,0,1:T(8,128)(2,1)S(1)}, u32[]{:S(2)}, u32[]{:S(2)}) async-start(bf16[64,16,800]{2,0,1:T(8,128)(2,1)} %copy.33), calls=%async_computation.1 | async-start | bytes 3670016 | tf_op jit(solution)/shard_map/all_to_all | solution.py:200
  213.9 0.0 reduce-scatter.2.cloned.1.call-start
  214.0 0.5 broadcast.149
  214.5 0.7 reduce.7
  215.2 0.1 reshape_squeeze.20
  215.3 0.1 fusion.27
  215.4 0.1 mul.171
  215.5 0.0 copy-done.11
  215.5 0.6 dynamic_slice.3
  216.1 0.6 compare_convert_fusion
  216.7 0.1 broadcast_multiply_fusion
  216.8 20.2 %all-to-all-done.1 = bf16[64,16,800]{2,0,1:T(8,128)(2,1)S(1)} async-done(((bf16[64,16,800]{2,0,1:T(8,128)(2,1)}), bf16[64,16,800]{2,0,1:T(8,128)(2,1)S(1)}, u32[]{:S(2)}, u32[]{:S(2)}) %all-to-all-start.1) | async-done | bytes 1638432 | tf_op jit(solution)/shard_map/all_to_all | solution.py:200
  237.0 1.3 fusion.8
  238.3 19.2 %add_convert_fusion = bf16[16,64,6144]{2,1,0:T(8,128)(2,1)} fusion(f32[16,64]{1,0:T(8,128)S(1)} %broadcast_multiply_fusion, bf16[800,6144]{1,0:T(8,128)(2,1)} %param.23, bf16[16,64,800]{2,0,1:T(8,128)(2,1)S(1)} %fusion.8), kind=kOutput, calls=%fused_computation.1 | convolution fusion | flops 10078912512 | bytes 24055808 | tf_op jit(solution)/shard_map/dot_general | solution.py:211
  257.5 0.0 reduce-scatter.2.cloned.1.call-update
  257.5 95.1 %reduce-scatter.2.cloned.1.call-done = bf16[64,6144]{1,0:T(8,128)(2,1)} async-done(((bf16[1024,6144]{1,0:T(8,128)(2,1)}), bf16[64,6144]{1,0:T(8,128)(2,1)}) %reduce-scatter.2.cloned.1.call-update) | async-done | bytes 786448 | tf_op jit(solution)/shard_map/reduce_scatter | solution.py:217
  352.6 5.2 %fusion.24 = bf16[1,64,6144]{2,1,0:T(8,128)(2,1)} fusion(bf16[64,6144]{1,0:T(8,128)(2,1)} %reduce-scatter.2.cloned.1.call-done, f32[6144]{0:T(1024)S(1)} %copy-done.6), kind=kLoop, calls=%fused_computation.43 | loop fusion | flops 26345472 | bytes 1597440 | tf_op jit(solution)/shard_map/broadcast_in_dim | solution.py:224
  (20 shorter events, 0.1 us)
Async XLA Ops:
  6.5 2.0 copy-start
  6.5 77.7 %all-gather.4.cloned.1.call-start = ((), (), s32[]{:S(2)}) async-start(), calls=%async_computation.3 | async-start | bytes 14745600 | tf_op jit(solution)/shard_map/all_gather | solution.py:135
  10.9 152.8 %all-gather.6.cloned.1.call-start = ((), (), s32[]{:S(2)}) async-start(), calls=%async_computation.5 | async-start | bytes 14745600 | tf_op jit(solution)/shard_map/all_gather | solution.py:177
  11.7 7.5 %copy-start.9 = (s32[1,256]{1,0:T(1,128)S(1)}, s32[1,256]{1,0:T(1,128)}, u32[]{:S(2)}) copy-start(s32[1,256]{1,0:T(1,128)} %param.19) | copy-start | bytes 3076
  11.7 7.5 %copy-start.8 = (f32[2,256]{1,0:T(2,128)S(1)}, f32[2,256]{1,0:T(2,128)}, u32[]{:S(2)}) copy-start(f32[2,256]{1,0:T(2,128)} %param.16) | copy-start | bytes 6148
  84.2 10.4 %copy-start.2 = (bf16[3200,2,1,128]{0,3,2,1:T(8,128)(2,1)S(1)}, bf16[3200,2,1,128]{0,3,2,1:T(8,128)(2,1)}, u32[]{:S(2)}) copy-start(bf16[3200,2,1,128]{0,3,2,1:T(8,128)(2,1)} %get-tuple-element.8) | copy-start | bytes 4915204
  84.2 10.4 %copy-start.12 = (bf16[2048,3200]{1,0:T(8,128)(2,1)S(1)}, bf16[2048,3200]{1,0:T(8,128)(2,1)}, u32[]{:S(2)}) copy-start(bf16[2048,3200]{1,0:T(8,128)(2,1)} %all-gather.4.cloned.1.call-done) | copy-start | bytes 39321604
  114.9 3.0 copy-start.3
  156.8 18.9 %all-to-all-start = ((bf16[8,256,256]{2,1,0:T(8,128)(2,1)}), bf16[8,256,256]{2,1,0:T(8,128)(2,1)S(1)}, u32[]{:S(2)}, u32[]{:S(2)}) async-start(bf16[8,256,256]{2,1,0:T(8,128)(2,1)} %bitcast.54), calls=%async_computation | async-start | bytes 2097152 | tf_op jit(solution)/shard_map/all_to_all | solution.py:174
  160.6 2.8 copy-start.4
  160.6 2.9 copy-start.5
  186.3 5.3 %copy-start.1 = (f32[4,2,16,2,3200]{4,3,2,1,0:T(2,128)S(1)}, f32[4,2,16,2,3200]{4,3,2,1,0:T(2,128)}, u32[]{:S(2)}) copy-start(f32[4,2,16,2,3200]{4,3,2,1,0:T(2,128)} %reshape.174) | copy-start | bytes 9830404
  186.3 5.3 %copy-start.7 = (f32[3200]{0:T(1024)S(1)}, f32[3200]{0:T(1024)}, u32[]{:S(2)}) copy-start(f32[3200]{0:T(1024)} %param.18) | copy-start | bytes 38404
  207.1 7.4 %copy-start.10 = (s32[1,256]{1,0:T(1,128)S(1)}, s32[1,256]{1,0:T(1,128)}, u32[]{:S(2)}) copy-start(s32[1,256]{1,0:T(1,128)} %param.20) | copy-start | bytes 3076
  207.1 8.4 %copy-start.11 = (s32[16]{0:T(128)S(1)}, s32[16]{0:T(128)}, u32[]{:S(2)}) copy-start(s32[16]{0:T(128)} %param.25) | copy-start | bytes 196
  207.1 29.9 %all-to-all-start.1 = ((bf16[64,16,800]{2,0,1:T(8,128)(2,1)}), bf16[64,16,800]{2,0,1:T(8,128)(2,1)S(1)}, u32[]{:S(2)}, u32[]{:S(2)}) async-start(bf16[64,16,800]{2,0,1:T(8,128)(2,1)} %copy.33), calls=%async_computation.1 | async-start | bytes 3670016 | tf_op jit(solution)/shard_map/all_to_all | solution.py:200
  213.9 138.7 %reduce-scatter.2.cloned.1.call-start = ((), (), s32[]{:S(2)}) async-start(), calls=%async_computation.4 | async-start | bytes 13369344 | tf_op jit(solution)/shard_map/reduce_scatter | solution.py:217
  257.5 95.2 %copy-start.6 = (f32[6144]{0:T(1024)S(1)}, f32[6144]{0:T(1024)}, u32[]{:S(2)}) copy-start(f32[6144]{0:T(1024)} %param.24) | copy-start | bytes 73732
Sparse Core Ops, SparseCore 0:
  11.0 73.1 all-gather.3
  85.9 72.7 all-gather.5
  257.6 94.9 reduce-scatter.1
where the time goes:
time: 365 us; the launch traced here: 364 us
  waiting for transfers between devices  189 us (52%)
  matrix products  56.2 us (15%)
  local copies, waits for them, and re-layouts  35.5 us (10%)
  Pallas kernels  35.5 us (10%)
  other arithmetic  24.6 us (7%)
  between operations  13.3 us (4%)
  starting transfers between devices  10.7 us (3%)
    reduce_scatter x1, waiting for transfers between devices, per_device(): lax.psum_scatter(partial.reshape(row_count * merged_count, -1), 'rows', s...  95.1 us
    all_gather x1, waiting for transfers between devices, per_device(): row_tokens = lax.all_gather(normed, 'seq', axis=0, tiled=True)  60.5 us
    dot_general x3, matrix products, per_device(): jnp.dot(row_tokens, weight_parts[:, :, c].reshape(qkv_weight.shape[0], he...  25.1 us
    pallas_call x1, Pallas kernels, attend_kernel(): pl.pallas_call(functools.partial(attention_kernel, scale), out_shape=jax....  23.8 us
    all_to_all x1, waiting for transfers between devices, per_device(): lax.all_to_all(merged_norm, 'rows', split_axis=1, concat_axis=0, tiled=True)  20.2 us
    dot_general x1, matrix products, per_device(): jnp.dot(ordered, fc_weight, preferred_element_type=jnp.float32)  19.2 us
    all_to_all x1, waiting for transfers between devices, per_device(): lax.all_to_all(attended.reshape(seq_count, shard_rows, group_width), 'seq...  12.1 us
    pallas_call x1, Pallas kernels, seq_sum(): pl.pallas_call(seq_sum_kernel, out_shape=jax.ShapeDtypeStruct(part.shape,...  11.7 us
  transfers between devices with their start and end apart: 5, of which 4 were waited for; matrix products, arithmetic and copies ran while one was open for 15% of the time, Pallas kernels for 10%

commit v1 on v0

--- a/solution.py
+++ b/solution.py
@@ -72,10 +72,18 @@
     )(part)
 
 
-def attention_kernel(scale, q_ref, k_ref, v_ref, qseg_ref, kseg_ref, o_ref):
+def attention_kernel(scale, q_ref, k_ref, v_ref, qrs_ref, krs_ref, qg_ref, kg_ref, qseg_ref,
+                     kseg_ref, o_ref, key_norm):
+    @pl.when(pl.program_id(1) == 0)
+    def _():
+        key_norm[...] = jnp.transpose(
+            (k_ref[...] * krs_ref[...] * kg_ref[...]).astype(jnp.bfloat16)
+        )
+
+    query_norm = jnp.transpose((q_ref[...] * qrs_ref[...] * qg_ref[...]).astype(jnp.bfloat16))
     scores = (
         lax.dot_general(
-            q_ref[...], k_ref[...], (((1,), (1,)), ((), ())), preferred_element_type=jnp.float32
+            query_norm, key_norm[...], (((1,), (1,)), ((), ())), preferred_element_type=jnp.float32
         )
         * scale
     )
@@ -87,27 +95,43 @@
     o_ref[...] = jnp.dot(probs, v_ref[...], preferred_element_type=jnp.float32).astype(o_ref.dtype)
 
 
-def attend_kernel(query_norm, key_norm, value_half, row_segments, block_len, scale):
-    length, width = query_norm.shape
+def attend_kernel(query_raw, key_raw, value_half, query_rs, key_rs, qk_gain, row_segments,
+                  block_len, scale):
+    length, width = query_raw.shape
     heads_here = width // HEAD_DIM
-    q2, k2, v2 = query_norm, key_norm, value_half
     flops = 4 * length * length * width
+    gain_block = pl.BlockSpec((HEAD_DIM, 1), lambda h, i: (h, 0))
     return pl.pallas_call(
         functools.partial(attention_kernel, scale),
         out_shape=jax.ShapeDtypeStruct((length, width), jnp.bfloat16),
         grid=(heads_here, length // block_len),
         in_specs=[
-            pl.BlockSpec((block_len, HEAD_DIM), lambda h, i: (i, h)),
+            pl.BlockSpec((HEAD_DIM, block_len), lambda h, i: (h, i)),
+            pl.BlockSpec((HEAD_DIM, length), lambda h, i: (h, 0)),
             pl.BlockSpec((length, HEAD_DIM), lambda h, i: (0, h)),
-            pl.BlockSpec((length, HEAD_DIM), lambda h, i: (0, h)),
+            pl.BlockSpec((1, block_len), lambda h, i: (0, i)),
+            pl.BlockSpec((1, length), lambda h, i: (0, 0)),
+            gain_block,
+            gain_block,
             pl.BlockSpec((block_len, 1), lambda h, i: (i, 0)),
             pl.BlockSpec((1, length), lambda h, i: (0, 0)),
         ],
         out_specs=pl.BlockSpec((block_len, HEAD_DIM), lambda h, i: (i, h)),
+        scratch_shapes=[pltpu.VMEM((length, HEAD_DIM), jnp.bfloat16)],
         cost_estimate=pl.CostEstimate(
-            flops=flops, transcendentals=length * length * heads_here, bytes_accessed=8 * length * width
+            flops=flops, transcendentals=length * length * heads_here, bytes_accessed=12 * length * width
         ),
-    )(q2, k2, v2, row_segments.reshape(length, 1), row_segments.reshape(1, length))
+    )(
+        query_raw.T,
+        key_raw.T,
+        value_half,
+        query_rs.reshape(1, length),
+        key_rs.reshape(1, length),
+        qk_gain[0].reshape(width, 1),
+        qk_gain[1].reshape(width, 1),
+        row_segments.reshape(length, 1),
+        row_segments.reshape(1, length),
+    )
 
 
 def per_device(
@@ -162,14 +186,18 @@
     )
     query_sq, key_sq, row_segments = stats[0], stats[1], stats[2]
     norm_width = HEADS * HEAD_DIM
-    query_norm = (
-        query_raw * lax.rsqrt(query_sq / norm_width + 1e-06)[:, None] * qk_gain[0]
-    ).astype(jnp.bfloat16)
-    key_norm = (
-        key_raw * lax.rsqrt(key_sq / norm_width + 1e-06)[:, None] * qk_gain[1]
-    ).astype(jnp.bfloat16)
     scale = HEAD_DIM ** (-0.5)
-    attended = attend_kernel(query_norm, key_norm, value_half, row_segments, 256, scale)
+    attended = attend_kernel(
+        query_raw,
+        key_raw,
+        value_half,
+        lax.rsqrt(query_sq / norm_width + 1e-06),
+        lax.rsqrt(key_sq / norm_width + 1e-06),
+        qk_gain,
+        row_segments,
+        256,
+        scale,
+    )
     group_width = attended.shape[1]
     own_heads = lax.all_to_all(
         attended.reshape(seq_count, shard_rows, group_width), "seq", 0, 0

time: 365 us -> 363 us (level)
    dot_general x2 -> x0, local copies, waits for them, and re-layouts: 5.88 us -> none  [per_device(): jnp.dot(row_tokens, weight_parts[:, :, c].reshape(qkv_weight.shape[0], he...]
    unnamed x28 -> x24, local copies, waits for them, and re-layouts: 8.05 us -> 8.07 us
  transfers between devices with their start and end apart: 5 -> 5, of which waited for: 4 -> 5; matrix products, arithmetic and copies ran while one was open for 15% -> 13% of each run, Pallas kernels for 10% -> 11%
where the time goes in v1:
time: 363 us; the launch traced here: 362 us
  waiting for transfers between devices  187 us (52%)
  matrix products  56.1 us (15%)
  Pallas kernels  38.3 us (11%)
  local copies, waits for them, and re-layouts  34.3 us (9%)
  other arithmetic  23 us (6%)
  between operations  13.3 us (4%)
  starting transfers between devices  10.8 us (3%)
    reduce_scatter x1, waiting for transfers between devices, per_device(): lax.psum_scatter(partial.reshape(row_count * merged_count, -1), 'rows', s...  95.1 us
    all_gather x1, waiting for transfers between devices, per_device(): row_tokens = lax.all_gather(normed, 'seq', axis=0, tiled=True)  58.8 us
    pallas_call x1, Pallas kernels, attend_kernel(): pl.pallas_call(functools.partial(attention_kernel, scale), out_shape=jax....  26.7 us
    dot_general x3, matrix products, per_device(): jnp.dot(row_tokens, weight_parts[:, :, c].reshape(qkv_weight.shape[0], he...  25.2 us
    all_to_all x1, waiting for transfers between devices, per_device(): lax.all_to_all(merged_norm, 'rows', split_axis=1, concat_axis=0, tiled=True)  20 us
    dot_general x1, matrix products, per_device(): jnp.dot(ordered, fc_weight, preferred_element_type=jnp.float32)  19.2 us
    pallas_call x1, Pallas kernels, seq_sum(): pl.pallas_call(seq_sum_kernel, out_shape=jax.ShapeDtypeStruct(part.shape,...  11.6 us
    all_to_all x1, waiting for transfers between devices, per_device(): lax.all_to_all(attended.reshape(seq_count, shard_rows, group_width), 'seq...  11.2 us
  transfers between devices with their start and end apart: 5, of which 5 were waited for; matrix products, arithmetic and copies ran while one was open for 13% of the time, Pallas kernels for 11%

profile of v1, /device:TPU:1, one launch (start us, length us, event | category | flops | bytes accessed | tf_op | source)
XLA Modules:
  0.0 362.5 jit_solution(13411488173613936738)
XLA Ops:
  6.5 0.0 all-gather.4.cloned.1.call-start
  6.5 2.0 fusion.1
  8.5 0.0 copy-done
  8.5 2.4 fusion.3
  10.9 0.0 all-gather.4.cloned.1.call-update
  10.9 0.0 all-gather.6.cloned.1.call-start
  10.9 0.7 all-gather.6.cloned.1.call-update
  11.7 0.0 copy-start.6
  11.7 0.0 copy-start.7
  11.7 7.5 %copy.26 = bf16[3200,768]{0,1:T(8,128)(2,1)} copy(bf16[3200,768]{1,0:T(8,128)(2,1)} %param.15) | data formatting | bytes 9830400 | tf_op args[2]
  19.2 0.0 copy-done.6
  19.2 0.8 copy.27.qg_ref
  20.0 0.8 copy.28.kg_ref
  20.8 0.0 copy-done.7
  20.8 4.6 %fusion.32 = (bf16[3200,2,1,128]{0,3,2,1:T(8,128)(2,1)S(1)}, bf16[3200,2,1,128]{0,3,2,1:T(8,128)(2,1)}, bf16[3200,2,1,128]{0,3,2,1:T(8,128)(2,1)}) fusion(bf16[3200,2,3,128]{0,3,2,1:T(8,128)(2,1)} %bitcast.51), kind=kLoop, calls=%fused_computation.62 | loop fusion | bytes 9830400 | tf_op jit(solution)/shard_map/slice | solution.py:166
  25.4 58.8 %all-gather.4.cloned.1.call-done = bf16[2048,3200]{1,0:T(8,128)(2,1)} async-done(((bf16[256,3200]{1,0:T(8,128)(2,1)}), bf16[2048,3200]{1,0:T(8,128)(2,1)}) %all-gather.4.cloned.1.call-update) | async-done | bytes 13107216 | tf_op jit(solution)/shard_map/all_gather | solution.py:159
  84.2 10.3 %multiply_reduce_fusion.2 = (f32[2048]{0:T(1024)S(1)}, f32[2048,256]{0,1:T(8,128)}) fusion(bf16[2048,3200]{1,0:T(8,128)(2,1)} %all-gather.4.cloned.1.call-done, bf16[3200,256]{0,1:T(8,128)(2,1)} %bitcast.55), kind=kOutput, calls=%fused_computation.14 | convolution fusion | flops 3356489728 | bytes 16850944 | tf_op jit(solution)/shard_map/dot_general | solution.py:164
  94.5 0.0 copy-done.1
  94.5 0.0 copy-done.10
  94.5 5.1 %multiply_reduce_fusion.1 = (f32[2048]{0:T(1024)S(1)}, f32[2048,256]{0,1:T(8,128)}) fusion(bf16[2048,3200]{1,0:T(8,128)(2,1)S(1)} %copy-done.10, bf16[3200,256]{0,1:T(8,128)(2,1)S(1)} %bitcast.54), kind=kOutput, calls=%fused_computation.13 | convolution fusion | flops 3356489728 | bytes 16850944 | tf_op jit(solution)/shard_map/dot_general | solution.py:164
  99.7 0.6 pad_maximum_fusion.part_ref
  100.3 11.6 %shard_map.127 = f32[3,2048]{1,0:T(4,128)} custom-call(f32[3,2048]{1,0:T(4,128)} %pad_maximum_fusion.part_ref), custom_call_target="tpu_custom_call" | custom-call | tf_op jit(solution)/shard_map/pallas_call | solution.py:61
  111.9 1.5 fusion.33
  113.4 1.4 copy.29.qseg_ref
  114.8 9.7 %convolution_convert_fusion.v_ref = bf16[2048,256]{1,0:T(8,128)(2,1)} fusion(bf16[2048,3200]{1,0:T(8,128)(2,1)} %all-gather.4.cloned.1.call-done, bf16[3200,256]{0,1:T(8,128)(2,1)S(1)} %bitcast.53), kind=kOutput, calls=%fused_computation.11 | convolution fusion | flops 3355967488 | bytes 15794176 | tf_op jit(solution)/shard_map/dot_general | solution.py:164
  124.5 26.7 %shard_map.128 = bf16[2048,256]{1,0:T(8,128)(2,1)} custom-call(f32[256,2048]{1,0:T(8,128)} %bitcast.60, f32[256,2048]{1,0:T(8,128)} %bitcast.61, bf16[2048,256]{1,0:T(8,128)(2,1)} %convolution_convert_fusion.v_ref, f32[1,2048]{1,0:T(1,128)} %get-tuple-element.13.qrs_ref, f32[1,2048]{1,0:T(1,128)} %get-tuple-element.12.krs_ref, f32[256,1]{1,0:T(8,128)} %copy.27.qg_ref, ...), custom_call_target="tpu_custom_call" | custom-call | flops 4294967296 | bytes 6291456 | tf_op jit(solution)/shard_map/pallas_call | solution.py:104
  151.2 3.7 %all-to-all-start = ((bf16[8,256,256]{2,1,0:T(8,128)(2,1)}), bf16[8,256,256]{2,1,0:T(8,128)(2,1)S(1)}, u32[]{:S(2)}, u32[]{:S(2)}) async-start(bf16[8,256,256]{2,1,0:T(8,128)(2,1)} %bitcast.56), calls=%async_computation | async-start | bytes 2097152 | tf_op jit(solution)/shard_map/all_to_all | solution.py:202
  154.9 0.0 copy-start.2
  154.9 0.0 copy-start.3
  154.9 2.8 reshape.152
  157.7 0.0 copy-done.2
  157.7 0.1 add.84
  157.8 0.0 copy-done.3
  157.8 0.1 mul.119
  157.9 0.7 all-gather.6.cloned.1.call-done
  158.7 11.2 %all-to-all-done = bf16[8,256,256]{2,1,0:T(8,128)(2,1)S(1)} async-done(((bf16[8,256,256]{2,1,0:T(8,128)(2,1)}), bf16[8,256,256]{2,1,0:T(8,128)(2,1)S(1)}, u32[]{:S(2)}, u32[]{:S(2)}) %all-to-all-start) | async-done | bytes 1048608 | tf_op jit(solution)/shard_map/all_to_all | solution.py:202
  169.9 10.6 %convert_reduce_fusion = f32[256,3200]{1,0:T(8,128)} fusion(bf16[8,256,256]{2,1,0:T(8,128)(2,1)S(1)} %all-to-all-done, bf16[8,256,3200]{2,1,0:T(8,128)(2,1)} %bitcast.59), kind=kOutput, calls=%fused_computation | convolution fusion | flops 3374284800 | bytes 17432576 | tf_op jit(solution)/shard_map/gtc,gcd->gtd/dot_general | solution.py:206
  180.5 5.2 %reduce_sum.60 = f32[4,2,16,2,3200]{4,3,2,1,0:T(2,128)} reshape(f32[256,3200]{1,0:T(8,128)} %convert_reduce_fusion) | data formatting | bytes 6553600 | tf_op jit(solution)/shard_map/reduce_sum | solution.py:209
  185.7 0.0 copy-done.5
  185.7 5.2 %fusion.31 = (f32[4,16]{1,0:T(4,128)S(1)}, f32[4,16,2,2,3200]{4,3,1,2,0:T(2,128)S(1)}) fusion(f32[4,2,16,2,3200]{4,3,2,1,0:T(2,128)} %reshape.152, f32[4,2,16,2,3200]{4,3,2,1,0:T(2,128)} %reduce_sum.60, f32[3200]{0:T(1024)S(1)} %copy-done.5), kind=kLoop, calls=%fused_computation.61 | loop fusion | flops 2457536 | bytes 9843456 | tf_op jit(solution)/shard_map/reduce_sum | solution.py:217
  190.9 2.0 copy.30
  192.9 1.9 multiply_reduce_fusion
  194.8 0.1 div.25
  194.9 0.1 rsqrt.31
  195.0 5.8 %reshape.150 = f32[64,16,800]{2,1,0:T(8,128)} reshape(f32[4,16,2,2,3200]{4,3,2,1,0:T(2,128)} %copy.30) | data formatting | bytes 6553600 | tf_op jit(solution)/shard_map/reshape | solution.py:214
  200.8 2.7 add_convert_fusion.1
  203.5 1.7 copy.31
  205.2 6.8 %all-to-all-start.1 = ((bf16[64,16,800]{2,0,1:T(8,128)(2,1)}), bf16[64,16,800]{2,0,1:T(8,128)(2,1)S(1)}, u32[]{:S(2)}, u32[]{:S(2)}) async-start(bf16[64,16,800]{2,0,1:T(8,128)(2,1)} %copy.31), calls=%async_computation.1 | async-start | bytes 3670016 | tf_op jit(solution)/shard_map/all_to_all | solution.py:228
  212.1 0.3 reduce-scatter.2.cloned.1.call-start
  212.3 0.5 broadcast.131
  212.9 0.0 copy-done.8
  212.9 0.7 reduce.7
  213.5 0.1 reshape_squeeze.28
  213.7 0.1 fusion.27
  213.8 0.1 mul.125
  213.8 0.6 dynamic_slice.3
  214.4 0.6 compare_convert_fusion
  215.1 0.1 broadcast_multiply_fusion
  215.2 20.0 %all-to-all-done.1 = bf16[64,16,800]{2,0,1:T(8,128)(2,1)S(1)} async-done(((bf16[64,16,800]{2,0,1:T(8,128)(2,1)}), bf16[64,16,800]{2,0,1:T(8,128)(2,1)S(1)}, u32[]{:S(2)}, u32[]{:S(2)}) %all-to-all-start.1) | async-done | bytes 1638432 | tf_op jit(solution)/shard_map/all_to_all | solution.py:228
  235.1 1.3 fusion.8
  236.4 19.2 %add_convert_fusion = bf16[16,64,6144]{2,1,0:T(8,128)(2,1)} fusion(f32[16,64]{1,0:T(8,128)S(1)} %broadcast_multiply_fusion, bf16[800,6144]{1,0:T(8,128)(2,1)} %param.23, bf16[16,64,800]{2,0,1:T(8,128)(2,1)S(1)} %fusion.8), kind=kOutput, calls=%fused_computation.1 | convolution fusion | flops 10078912512 | bytes 24055808 | tf_op jit(solution)/shard_map/dot_general | solution.py:239
  255.6 0.0 reduce-scatter.2.cloned.1.call-update
  255.6 95.1 %reduce-scatter.2.cloned.1.call-done = bf16[64,6144]{1,0:T(8,128)(2,1)} async-done(((bf16[1024,6144]{1,0:T(8,128)(2,1)}), bf16[64,6144]{1,0:T(8,128)(2,1)}) %reduce-scatter.2.cloned.1.call-update) | async-done | bytes 786448 | tf_op jit(solution)/shard_map/reduce_scatter | solution.py:245
  350.7 5.2 %fusion.24 = bf16[1,64,6144]{2,1,0:T(8,128)(2,1)} fusion(bf16[64,6144]{1,0:T(8,128)(2,1)} %reduce-scatter.2.cloned.1.call-done, f32[6144]{0:T(1024)S(1)} %copy-done.4), kind=kLoop, calls=%fused_computation.41 | loop fusion | flops 26345472 | bytes 1597440 | tf_op jit(solution)/shard_map/broadcast_in_dim | solution.py:252
  (15 shorter events, 0.1 us)
Async XLA Ops:
  6.5 2.0 copy-start
  6.5 77.7 %all-gather.4.cloned.1.call-start = ((), (), s32[]{:S(2)}) async-start(), calls=%async_computation.3 | async-start | bytes 14745600 | tf_op jit(solution)/shard_map/all_gather | solution.py:159
  10.9 147.8 %all-gather.6.cloned.1.call-start = ((), (), s32[]{:S(2)}) async-start(), calls=%async_computation.5 | async-start | bytes 14745600 | tf_op jit(solution)/shard_map/all_gather | solution.py:205
  11.7 7.5 %copy-start.6 = (f32[2,256]{1,0:T(2,128)S(1)}, f32[2,256]{1,0:T(2,128)}, u32[]{:S(2)}) copy-start(f32[2,256]{1,0:T(2,128)} %param.16) | copy-start | bytes 6148
  11.7 9.1 %copy-start.7 = (s32[1,256]{1,0:T(1,128)S(1)}, s32[1,256]{1,0:T(1,128)}, u32[]{:S(2)}) copy-start(s32[1,256]{1,0:T(1,128)} %param.19) | copy-start | bytes 3076
  84.2 10.3 %copy-start.1 = (bf16[3200,2,1,128]{0,3,2,1:T(8,128)(2,1)S(1)}, bf16[3200,2,1,128]{0,3,2,1:T(8,128)(2,1)}, u32[]{:S(2)}) copy-start(bf16[3200,2,1,128]{0,3,2,1:T(8,128)(2,1)} %get-tuple-element.8) | copy-start | bytes 4915204
  84.2 10.3 %copy-start.10 = (bf16[2048,3200]{1,0:T(8,128)(2,1)S(1)}, bf16[2048,3200]{1,0:T(8,128)(2,1)}, u32[]{:S(2)}) copy-start(bf16[2048,3200]{1,0:T(8,128)(2,1)} %all-gather.4.cloned.1.call-done) | copy-start | bytes 39321604
  151.2 18.7 %all-to-all-start = ((bf16[8,256,256]{2,1,0:T(8,128)(2,1)}), bf16[8,256,256]{2,1,0:T(8,128)(2,1)S(1)}, u32[]{:S(2)}, u32[]{:S(2)}) async-start(bf16[8,256,256]{2,1,0:T(8,128)(2,1)} %bitcast.56), calls=%async_computation | async-start | bytes 2097152 | tf_op jit(solution)/shard_map/all_to_all | solution.py:202
  154.9 2.8 copy-start.2
  154.9 2.9 copy-start.3
  180.5 5.2 %copy-start.5 = (f32[3200]{0:T(1024)S(1)}, f32[3200]{0:T(1024)}, u32[]{:S(2)}) copy-start(f32[3200]{0:T(1024)} %param.18) | copy-start | bytes 38404
  205.2 7.6 %copy-start.8 = (s32[1,256]{1,0:T(1,128)S(1)}, s32[1,256]{1,0:T(1,128)}, u32[]{:S(2)}) copy-start(s32[1,256]{1,0:T(1,128)} %param.20) | copy-start | bytes 3076
  205.2 8.6 %copy-start.9 = (s32[16]{0:T(128)S(1)}, s32[16]{0:T(128)}, u32[]{:S(2)}) copy-start(s32[16]{0:T(128)} %param.25) | copy-start | bytes 196
  205.2 29.9 %all-to-all-start.1 = ((bf16[64,16,800]{2,0,1:T(8,128)(2,1)}), bf16[64,16,800]{2,0,1:T(8,128)(2,1)S(1)}, u32[]{:S(2)}, u32[]{:S(2)}) async-start(bf16[64,16,800]{2,0,1:T(8,128)(2,1)} %copy.31), calls=%async_computation.1 | async-start | bytes 3670016 | tf_op jit(solution)/shard_map/all_to_all | solution.py:228
  212.1 138.7 %reduce-scatter.2.cloned.1.call-start = ((), (), s32[]{:S(2)}) async-start(), calls=%async_computation.4 | async-start | bytes 13369344 | tf_op jit(solution)/shard_map/reduce_scatter | solution.py:245
  255.6 95.2 %copy-start.4 = (f32[6144]{0:T(1024)S(1)}, f32[6144]{0:T(1024)}, u32[]{:S(2)}) copy-start(f32[6144]{0:T(1024)} %param.24) | copy-start | bytes 73732
Sparse Core Ops, SparseCore 0:
  11.0 73.1 all-gather.3
  85.9 72.7 all-gather.5
  255.7 94.9 reduce-scatter.1

commit v2 on v1

--- a/solution.py
+++ b/solution.py
@@ -73,8 +73,22 @@
 
 
 def attention_kernel(scale, q_ref, k_ref, v_ref, qrs_ref, krs_ref, qg_ref, kg_ref, qseg_ref,
-                     kseg_ref, o_ref, key_norm):
-    @pl.when(pl.program_id(1) == 0)
+                     kseg_ref, o_ref, key_norm, slots, landing, send_sem, recv_sem, local_sem):
+    head, block = pl.program_id(0), pl.program_id(1)
+    blocks = pl.num_programs(1)
+    heads = pl.num_programs(0)
+    me = lax.axis_index("seq")
+    row = lax.axis_index("rows")
+
+    @pl.when((head == 0) & (block == 0))
+    def _():
+        barrier = pltpu.get_barrier_semaphore()
+        for k in range(1, o_ref.shape[0]):
+            peer = lax.rem(me + k, o_ref.shape[0])
+            pl.semaphore_signal(barrier, inc=1, device_id=(row, peer), device_id_type=MESH)
+        pl.semaphore_wait(barrier, o_ref.shape[0] - 1)
+
+    @pl.when(block == 0)
     def _():
         key_norm[...] = jnp.transpose(
             (k_ref[...] * krs_ref[...] * kg_ref[...]).astype(jnp.bfloat16)
@@ -92,19 +106,64 @@
     exp_terms = jnp.exp(scores - peak_val)
     total = jnp.sum(exp_terms, axis=-1, keepdims=True)
     probs = (exp_terms / total).astype(jnp.bfloat16)
-    o_ref[...] = jnp.dot(probs, v_ref[...], preferred_element_type=jnp.float32).astype(o_ref.dtype)
+    step = head * blocks + block
+    slots[step] = jnp.dot(probs, v_ref[...], preferred_element_type=jnp.float32).astype(
+        slots.dtype
+    )
+
+    def remote(h, i):
+        return pltpu.make_async_remote_copy(
+            src_ref=slots.at[h * blocks + i],
+            dst_ref=landing.at[me, h],
+            send_sem=send_sem.at[h * blocks + i],
+            recv_sem=recv_sem.at[me, h],
+            device_id=(row, i),
+            device_id_type=MESH,
+        )
+
+    def local(h):
+        return pltpu.make_async_copy(
+            slots.at[h * blocks + me], landing.at[me, h], local_sem.at[h]
+        )
+
+    @pl.when(block != me)
+    def _():
+        remote(head, block).start()
+
+    @pl.when(block == me)
+    def _():
+        local(head).start()
+
+    @pl.when(step == heads * blocks - 1)
+    def _():
+        for h in range(slots.shape[0] // o_ref.shape[0]):
+            local(h).wait()
+            for i in range(o_ref.shape[0]):
+                @pl.when(i != me)
+                def _():
+                    remote(h, i).wait_send()
+                    pltpu.make_async_remote_copy(
+                        src_ref=slots.at[h * blocks + i],
+                        dst_ref=landing.at[i, h],
+                        send_sem=send_sem.at[h * blocks + i],
+                        recv_sem=recv_sem.at[i, h],
+                        device_id=(row, i),
+                        device_id_type=MESH,
+                    ).wait_recv()
+        o_ref[...] = landing[...]
 
 
 def attend_kernel(query_raw, key_raw, value_half, query_rs, key_rs, qk_gain, row_segments,
                   block_len, scale):
     length, width = query_raw.shape
     heads_here = width // HEAD_DIM
+    blocks = length // block_len
     flops = 4 * length * length * width
     gain_block = pl.BlockSpec((HEAD_DIM, 1), lambda h, i: (h, 0))
     return pl.pallas_call(
         functools.partial(attention_kernel, scale),
-        out_shape=jax.ShapeDtypeStruct((length, width), jnp.bfloat16),
-        grid=(heads_here, length // block_len),
+        out_shape=jax.ShapeDtypeStruct((blocks, heads_here, block_len, HEAD_DIM), jnp.bfloat16),
+        grid=(heads_here, blocks),
         in_specs=[
             pl.BlockSpec((HEAD_DIM, block_len), lambda h, i: (h, i)),
             pl.BlockSpec((HEAD_DIM, length), lambda h, i: (h, 0)),
@@ -116,8 +175,16 @@
             pl.BlockSpec((block_len, 1), lambda h, i: (i, 0)),
             pl.BlockSpec((1, length), lambda h, i: (0, 0)),
         ],
-        out_specs=pl.BlockSpec((block_len, HEAD_DIM), lambda h, i: (i, h)),
-        scratch_shapes=[pltpu.VMEM((length, HEAD_DIM), jnp.bfloat16)],
+        out_specs=pl.BlockSpec(memory_space=pltpu.VMEM),
+        scratch_shapes=[
+            pltpu.VMEM((length, HEAD_DIM), jnp.bfloat16),
+            pltpu.VMEM((heads_here * blocks, block_len, HEAD_DIM), jnp.bfloat16),
+            pltpu.VMEM((blocks, heads_here, block_len, HEAD_DIM), jnp.bfloat16),
+            pltpu.SemaphoreType.DMA((heads_here * blocks,)),
+            pltpu.SemaphoreType.DMA((blocks, heads_here)),
+            pltpu.SemaphoreType.DMA((heads_here,)),
+        ],
+        compiler_params=pltpu.CompilerParams(collective_id=2, has_side_effects=True),
         cost_estimate=pl.CostEstimate(
             flops=flops, transcendentals=length * length * heads_here, bytes_accessed=12 * length * width
         ),
@@ -198,13 +265,12 @@
         256,
         scale,
     )
-    group_width = attended.shape[1]
-    own_heads = lax.all_to_all(
-        attended.reshape(seq_count, shard_rows, group_width), "seq", 0, 0
-    )
     full_out_weight = lax.all_gather(out_weight, "seq", axis=0, tiled=False)
     group_terms = jnp.einsum(
-        "gtc,gcd->gtd", own_heads, full_out_weight, preferred_element_type=jnp.float32
+        "ghtd,ghdo->gto",
+        attended,
+        full_out_weight.reshape(seq_count, heads_here, HEAD_DIM, -1),
+        preferred_element_type=jnp.float32,
     ).astype(jnp.bfloat16)
     attn = jnp.sum(group_terms.astype(jnp.float32), axis=0)
     hidden = tokens + layer_scale * attn

time: 363 us -> 361 us (level)
  Pallas kernels: 38.3 us -> 48.4 us
  waiting for transfers between devices: 187 us -> 182 us
  starting transfers between devices: 10.8 us -> 6.92 us
    all_to_all x1 -> x0, waiting for transfers between devices: 11.2 us -> none  [per_device(): lax.all_to_all(attended.reshape(seq_count, shard_rows, group_width), 'seq...]
    pallas_call x1, Pallas kernels: 26.7 us -> 36.8 us  [attend_kernel(): pl.pallas_call(functools.partial(attention_kernel, scale), out_shape=jax....]
    all_gather x1, waiting for transfers between devices: 0.74 us -> 8.56 us  [per_device(): full_out_weight = lax.all_gather(out_weight, 'seq', axis=0, tiled=False)]
    all_to_all x1 -> x0, starting transfers between devices: 3.69 us -> none  [per_device(): lax.all_to_all(attended.reshape(seq_count, shard_rows, group_width), 'seq...]
  transfers between devices with their start and end apart: 5 -> 4, of which waited for: 5 -> 4; matrix products, arithmetic and copies ran while one was open for 13% -> 13% of each run, Pallas kernels for 11% -> 13%
where the time goes in v2:
time: 361 us; the launch traced here: 360 us
  waiting for transfers between devices  182 us (50%)
  matrix products  56.4 us (16%)
  Pallas kernels  48.4 us (13%)
  local copies, waits for them, and re-layouts  31.4 us (9%)
  other arithmetic  22 us (6%)
  between operations  13.2 us (4%)
  starting transfers between devices  6.92 us (2%)
    reduce_scatter x1, waiting for transfers between devices, per_device(): lax.psum_scatter(partial.reshape(row_count * merged_count, -1), 'rows', s...  93.5 us
    all_gather x1, waiting for transfers between devices, per_device(): row_tokens = lax.all_gather(normed, 'seq', axis=0, tiled=True)  55.6 us
    pallas_call x1, Pallas kernels, attend_kernel(): pl.pallas_call(functools.partial(attention_kernel, scale), out_shape=jax....  36.8 us
    dot_general x3, matrix products, per_device(): jnp.dot(row_tokens, weight_parts[:, :, c].reshape(qkv_weight.shape[0], he...  25.2 us
    all_to_all x1, waiting for transfers between devices, per_device(): lax.all_to_all(merged_norm, 'rows', split_axis=1, concat_axis=0, tiled=True)  23.4 us
    dot_general x1, matrix products, per_device(): jnp.dot(ordered, fc_weight, preferred_element_type=jnp.float32)  19.2 us
    pallas_call x1, Pallas kernels, seq_sum(): pl.pallas_call(seq_sum_kernel, out_shape=jax.ShapeDtypeStruct(part.shape,...  11.6 us
    dot_general x1, matrix products, per_device(): jnp.einsum('ghtd,ghdo->gto', attended, full_out_weight.reshape(seq_count,...  10.7 us
  transfers between devices with their start and end apart: 4, of which 4 were waited for; matrix products, arithmetic and copies ran while one was open for 13% of the time, Pallas kernels for 13%

profile of v2, /device:TPU:1, one launch (start us, length us, event | category | flops | bytes accessed | tf_op | source)
XLA Modules:
  0.0 360.3 jit_solution(14574162641705117330)
XLA Ops:
  6.5 0.0 copy-start
  6.5 0.0 all-gather.4.cloned.1.call-start
  6.5 2.0 fusion.1
  8.5 0.0 copy-done
  8.5 2.4 fusion.3
  10.9 0.0 all-gather.4.cloned.1.call-update
  10.9 0.0 all-gather.6.cloned.1.call-start
  10.9 0.7 all-gather.6.cloned.1.call-update
  11.6 2.8 reshape.152
  14.5 0.0 copy-start.6
  14.5 0.0 copy-start.2
  14.5 0.0 copy-start.3
  14.5 7.5 %copy.26 = bf16[3200,768]{0,1:T(8,128)(2,1)} copy(bf16[3200,768]{1,0:T(8,128)(2,1)} %param.15) | data formatting | bytes 9830400 | tf_op args[2]
  22.0 0.0 copy-done.6
  22.0 0.8 copy.27.qg_ref
  22.8 0.8 copy.28.kg_ref
  23.6 0.0 copy-done.2
  23.6 0.1 add.84
  23.7 0.0 copy-done.3
  23.7 0.1 mul.119
  23.8 0.0 copy-done.7
  23.9 4.7 %fusion.32 = (bf16[3200,2,1,128]{0,3,2,1:T(8,128)(2,1)S(1)}, bf16[3200,2,1,128]{0,3,2,1:T(8,128)(2,1)S(1)}, bf16[3200,2,1,128]{0,3,2,1:T(8,128)(2,1)}) fusion(bf16[3200,2,3,128]{0,3,2,1:T(8,128)(2,1)} %bitcast.55), kind=kLoop, calls=%fused_computation.63 | loop fusion | bytes 9830400 | tf_op jit(solution)/shard_map/slice | solution.py:233
  28.5 55.6 %all-gather.4.cloned.1.call-done = bf16[2048,3200]{1,0:T(8,128)(2,1)} async-done(((bf16[256,3200]{1,0:T(8,128)(2,1)}), bf16[2048,3200]{1,0:T(8,128)(2,1)}) %all-gather.4.cloned.1.call-update) | async-done | bytes 13107216 | tf_op jit(solution)/shard_map/all_gather | solution.py:226
  84.2 10.3 %multiply_reduce_fusion.2 = (f32[2048]{0:T(1024)S(1)}, f32[2048,256]{0,1:T(8,128)}) fusion(bf16[2048,3200]{1,0:T(8,128)(2,1)} %all-gather.4.cloned.1.call-done, bf16[3200,256]{0,1:T(8,128)(2,1)} %bitcast.59), kind=kOutput, calls=%fused_computation.15 | convolution fusion | flops 3356489728 | bytes 16850944 | tf_op jit(solution)/shard_map/dot_general | solution.py:231
  94.5 0.0 copy-done.10
  94.5 5.2 %multiply_reduce_fusion.1 = (f32[2048]{0:T(1024)S(1)}, f32[2048,256]{0,1:T(8,128)}) fusion(bf16[2048,3200]{1,0:T(8,128)(2,1)S(1)} %copy-done.10, bf16[3200,256]{0,1:T(8,128)(2,1)S(1)} %bitcast.58), kind=kOutput, calls=%fused_computation.14 | convolution fusion | flops 3356489728 | bytes 16850944 | tf_op jit(solution)/shard_map/dot_general | solution.py:231
  99.7 0.6 pad_maximum_fusion.part_ref
  100.3 11.6 %shard_map.127 = f32[3,2048]{1,0:T(4,128)} custom-call(f32[3,2048]{1,0:T(4,128)} %pad_maximum_fusion.part_ref), custom_call_target="tpu_custom_call" | custom-call | tf_op jit(solution)/shard_map/pallas_call | solution.py:61
  112.0 1.5 fusion.33
  113.5 1.3 copy.29.qseg_ref
  114.8 9.7 %convolution_convert_fusion.v_ref = bf16[2048,256]{1,0:T(8,128)(2,1)} fusion(bf16[2048,3200]{1,0:T(8,128)(2,1)} %all-gather.4.cloned.1.call-done, bf16[3200,256]{0,1:T(8,128)(2,1)S(1)} %bitcast.57), kind=kOutput, calls=%fused_computation.12 | convolution fusion | flops 3355967488 | bytes 15794176 | tf_op jit(solution)/shard_map/dot_general | solution.py:231
  124.5 36.8 %shard_map.128 = bf16[8,2,256,128]{3,2,1,0:T(8,128)(2,1)} custom-call(f32[256,2048]{1,0:T(8,128)} %bitcast.63, f32[256,2048]{1,0:T(8,128)} %bitcast.64, bf16[2048,256]{1,0:T(8,128)(2,1)} %convolution_convert_fusion.v_ref, f32[1,2048]{1,0:T(1,128)} %get-tuple-element.13.qrs_ref, f32[1,2048]{1,0:T(1,128)} %get-tuple-element.12.krs_ref, f32[256,1]{1,0:T(8,128)} %copy.27.qg_ref, ...), custom_call_target="tpu_custom_call" | custom-call | flops 4294967296 | bytes 6291456 | tf_op jit(solution)/shard_map/pallas_call | solution.py:163
  161.3 8.6 %all-gather.6.cloned.1.call-done = bf16[2048,3200]{1,0:T(8,128)(2,1)} async-done(((bf16[256,3200]{1,0:T(8,128)(2,1)}), bf16[2048,3200]{1,0:T(8,128)(2,1)}) %all-gather.6.cloned.1.call-update) | async-done | bytes 13107216 | tf_op jit(solution)/shard_map/all_gather | solution.py:268
  169.8 10.7 %convert_reduce_fusion = f32[256,3200]{1,0:T(8,128)} fusion(bf16[8,2,256,128]{3,2,1,0:T(8,128)(2,1)} %shard_map.128, bf16[8,2,128,3200]{3,2,1,0:T(8,128)(2,1)} %bitcast.62), kind=kOutput, calls=%fused_computation.1 | convolution fusion | flops 3374284800 | bytes 17432576 | tf_op jit(solution)/shard_map/ghtd,ghdo->gto/dot_general | solution.py:269
  180.6 5.3 %reduce_sum.60 = f32[4,2,16,2,3200]{4,3,2,1,0:T(2,128)} reshape(f32[256,3200]{1,0:T(8,128)} %convert_reduce_fusion) | data formatting | bytes 6553600 | tf_op jit(solution)/shard_map/reduce_sum | solution.py:275
  185.9 0.0 copy-done.1
  185.9 0.0 copy-done.5
  185.9 4.2 %fusion.31 = (f32[4,16]{1,0:T(4,128)S(1)}, f32[4,16,2,2,3200]{4,3,1,2,0:T(2,128)S(1)}) fusion(f32[4,2,16,2,3200]{4,3,2,1,0:T(2,128)S(1)} %copy-done.1, f32[4,2,16,2,3200]{4,3,2,1,0:T(2,128)} %reduce_sum.60, f32[3200]{0:T(1024)S(1)} %copy-done.5), kind=kLoop, calls=%fused_computation.62 | loop fusion | flops 2457536 | bytes 9843456 | tf_op jit(solution)/shard_map/reduce_sum | solution.py:283
  190.1 0.3 copy.30
  190.4 1.9 multiply_reduce_fusion
  192.3 0.1 div.25
  192.4 0.1 rsqrt.31
  192.5 4.5 %reshape.150 = f32[64,16,800]{2,1,0:T(8,128)} reshape(f32[4,16,2,2,3200]{4,3,2,1,0:T(2,128)S(1)} %copy.30) | data formatting | bytes 6553600 | tf_op jit(solution)/shard_map/reshape | solution.py:280
  197.0 2.7 add_convert_fusion.1
  199.7 1.7 copy.31
  201.4 6.8 %all-to-all-start = ((bf16[64,16,800]{2,0,1:T(8,128)(2,1)}), bf16[64,16,800]{2,0,1:T(8,128)(2,1)S(1)}, u32[]{:S(2)}, u32[]{:S(2)}) async-start(bf16[64,16,800]{2,0,1:T(8,128)(2,1)} %copy.31), calls=%async_computation | async-start | bytes 3670016 | tf_op jit(solution)/shard_map/all_to_all | solution.py:294
  208.2 0.0 reduce-scatter.2.cloned.1.call-start
  208.3 0.5 broadcast.131
  208.8 0.0 copy-done.8
  208.8 0.7 reduce.7
  209.5 0.1 reshape_squeeze.28
  209.6 0.1 fusion.27
  209.7 0.1 mul.125
  209.8 0.0 copy-done.9
  209.8 0.6 dynamic_slice.3
  210.4 0.6 compare_convert_fusion
  211.0 0.1 broadcast_multiply_fusion
  211.1 23.4 %all-to-all-done = bf16[64,16,800]{2,0,1:T(8,128)(2,1)S(1)} async-done(((bf16[64,16,800]{2,0,1:T(8,128)(2,1)}), bf16[64,16,800]{2,0,1:T(8,128)(2,1)S(1)}, u32[]{:S(2)}, u32[]{:S(2)}) %all-to-all-start) | async-done | bytes 1638432 | tf_op jit(solution)/shard_map/all_to_all | solution.py:294
  234.5 1.3 fusion.8
  235.8 19.2 %add_convert_fusion = bf16[16,64,6144]{2,1,0:T(8,128)(2,1)} fusion(f32[16,64]{1,0:T(8,128)S(1)} %broadcast_multiply_fusion, bf16[800,6144]{1,0:T(8,128)(2,1)} %param.23, bf16[16,64,800]{2,0,1:T(8,128)(2,1)S(1)} %fusion.8), kind=kOutput, calls=%fused_computation.2 | convolution fusion | flops 10078912512 | bytes 24055808 | tf_op jit(solution)/shard_map/dot_general | solution.py:305
  255.0 0.0 reduce-scatter.2.cloned.1.call-update
  255.0 93.5 %reduce-scatter.2.cloned.1.call-done = bf16[64,6144]{1,0:T(8,128)(2,1)} async-done(((bf16[1024,6144]{1,0:T(8,128)(2,1)}), bf16[64,6144]{1,0:T(8,128)(2,1)}) %reduce-scatter.2.cloned.1.call-update) | async-done | bytes 786448 | tf_op jit(solution)/shard_map/reduce_scatter | solution.py:311
  348.6 0.0 copy-done.4
  348.6 5.2 %fusion.24 = bf16[1,64,6144]{2,1,0:T(8,128)(2,1)} fusion(bf16[64,6144]{1,0:T(8,128)(2,1)} %reduce-scatter.2.cloned.1.call-done, f32[6144]{0:T(1024)S(1)} %copy-done.4), kind=kLoop, calls=%fused_computation.42 | loop fusion | flops 26345472 | bytes 1597440 | tf_op jit(solution)/shard_map/broadcast_in_dim | solution.py:318
  (13 shorter events, 0.1 us)
Async XLA Ops:
  6.5 2.0 copy-start
  6.5 77.6 %all-gather.4.cloned.1.call-start = ((), (), s32[]{:S(2)}) async-start(), calls=%async_computation.2 | async-start | bytes 14745600 | tf_op jit(solution)/shard_map/all_gather | solution.py:226
  10.9 159.0 %all-gather.6.cloned.1.call-start = ((), (), s32[]{:S(2)}) async-start(), calls=%async_computation.4 | async-start | bytes 14745600 | tf_op jit(solution)/shard_map/all_gather | solution.py:268
  14.5 7.5 %copy-start.6 = (f32[2,256]{1,0:T(2,128)S(1)}, f32[2,256]{1,0:T(2,128)}, u32[]{:S(2)}) copy-start(f32[2,256]{1,0:T(2,128)} %param.16) | copy-start | bytes 6148
  14.5 9.2 %copy-start.2 = (f32[12800]{0:T(1024)S(1)}, f32[12800]{0:T(1024)}, u32[]{:S(2)}) copy-start(f32[12800]{0:T(1024)} %param.22) | copy-start | bytes 153604
  14.5 9.3 %copy-start.3 = (f32[12800]{0:T(1024)S(1)}, f32[12800]{0:T(1024)}, u32[]{:S(2)}) copy-start(f32[12800]{0:T(1024)} %param.21) | copy-start | bytes 153604
  14.5 9.4 %copy-start.7 = (s32[1,256]{1,0:T(1,128)S(1)}, s32[1,256]{1,0:T(1,128)}, u32[]{:S(2)}) copy-start(s32[1,256]{1,0:T(1,128)} %param.19) | copy-start | bytes 3076
  84.2 10.3 %copy-start.10 = (bf16[2048,3200]{1,0:T(8,128)(2,1)S(1)}, bf16[2048,3200]{1,0:T(8,128)(2,1)}, u32[]{:S(2)}) copy-start(bf16[2048,3200]{1,0:T(8,128)(2,1)} %all-gather.4.cloned.1.call-done) | copy-start | bytes 39321604
  180.6 5.3 %copy-start.1 = (f32[4,2,16,2,3200]{4,3,2,1,0:T(2,128)S(1)}, f32[4,2,16,2,3200]{4,3,2,1,0:T(2,128)}, u32[]{:S(2)}) copy-start(f32[4,2,16,2,3200]{4,3,2,1,0:T(2,128)} %reshape.152) | copy-start | bytes 9830404
  180.6 5.3 %copy-start.5 = (f32[3200]{0:T(1024)S(1)}, f32[3200]{0:T(1024)}, u32[]{:S(2)}) copy-start(f32[3200]{0:T(1024)} %param.18) | copy-start | bytes 38404
  201.4 7.4 %copy-start.8 = (s32[1,256]{1,0:T(1,128)S(1)}, s32[1,256]{1,0:T(1,128)}, u32[]{:S(2)}) copy-start(s32[1,256]{1,0:T(1,128)} %param.20) | copy-start | bytes 3076
  201.4 8.4 %copy-start.9 = (s32[16]{0:T(128)S(1)}, s32[16]{0:T(128)}, u32[]{:S(2)}) copy-start(s32[16]{0:T(128)} %param.25) | copy-start | bytes 196
  201.4 33.1 %all-to-all-start = ((bf16[64,16,800]{2,0,1:T(8,128)(2,1)}), bf16[64,16,800]{2,0,1:T(8,128)(2,1)S(1)}, u32[]{:S(2)}, u32[]{:S(2)}) async-start(bf16[64,16,800]{2,0,1:T(8,128)(2,1)} %copy.31), calls=%async_computation | async-start | bytes 3670016 | tf_op jit(solution)/shard_map/all_to_all | solution.py:294
  208.2 140.3 %reduce-scatter.2.cloned.1.call-start = ((), (), s32[]{:S(2)}) async-start(), calls=%async_computation.3 | async-start | bytes 13369344 | tf_op jit(solution)/shard_map/reduce_scatter | solution.py:311
  255.0 93.5 %copy-start.4 = (f32[6144]{0:T(1024)S(1)}, f32[6144]{0:T(1024)}, u32[]{:S(2)}) copy-start(f32[6144]{0:T(1024)} %param.24) | copy-start | bytes 73732
Sparse Core Ops, SparseCore 0:
  11.0 73.1 all-gather.3
  85.9 83.9 all-gather.5
  255.2 93.3 reduce-scatter.1

commit v3 on v2

--- a/solution.py
+++ b/solution.py
@@ -201,6 +201,37 @@
     )
 
 
+def out_proj_kernel(att_ref, w_ref, res_ref, ls_ref, o_ref):
+    total = jnp.zeros(o_ref.shape, jnp.float32)
+    for g in range(att_ref.shape[0]):
+        term = jnp.dot(att_ref[g, 0], w_ref[g, 0], preferred_element_type=jnp.float32)
+        term = term + jnp.dot(att_ref[g, 1], w_ref[g, 1], preferred_element_type=jnp.float32)
+        total = total + term.astype(jnp.bfloat16).astype(jnp.float32)
+    o_ref[...] = res_ref[...].astype(jnp.float32) + ls_ref[...] * total
+
+
+def out_proj(attended, out_weight_groups, residual, layer_scale, tile=640):
+    groups, heads_here, tokens, _ = attended.shape
+    width = out_weight_groups.shape[-1]
+    return pl.pallas_call(
+        out_proj_kernel,
+        out_shape=jax.ShapeDtypeStruct((tokens, width), jnp.float32),
+        grid=(width // tile,),
+        in_specs=[
+            pl.BlockSpec(attended.shape, lambda j: (0, 0, 0, 0)),
+            pl.BlockSpec((groups, heads_here, HEAD_DIM, tile), lambda j: (0, 0, 0, j)),
+            pl.BlockSpec((tokens, tile), lambda j: (0, j)),
+            pl.BlockSpec((1, tile), lambda j: (0, j)),
+        ],
+        out_specs=pl.BlockSpec((tokens, tile), lambda j: (0, j)),
+        cost_estimate=pl.CostEstimate(
+            flops=2 * tokens * groups * heads_here * HEAD_DIM * width,
+            transcendentals=0,
+            bytes_accessed=groups * heads_here * HEAD_DIM * width * 2 + tokens * width * 6,
+        ),
+    )(attended, out_weight_groups, residual, layer_scale.reshape(1, width))
+
+
 def per_device(
     residual_in,
     norm_gain,
@@ -266,14 +297,12 @@
         scale,
     )
     full_out_weight = lax.all_gather(out_weight, "seq", axis=0, tiled=False)
-    group_terms = jnp.einsum(
-        "ghtd,ghdo->gto",
+    hidden = out_proj(
         attended,
         full_out_weight.reshape(seq_count, heads_here, HEAD_DIM, -1),
-        preferred_element_type=jnp.float32,
-    ).astype(jnp.bfloat16)
-    attn = jnp.sum(group_terms.astype(jnp.float32), axis=0)
-    hidden = tokens + layer_scale * attn
+        residual_in[0],
+        layer_scale,
+    )
     half_grid = GRID // 2
     lines = shard_rows // (2 * GRID)
     merged_count = shard_rows // 4

time: 361 us -> 361 us (level)
  Pallas kernels: 48.4 us -> 60.4 us
  matrix products: 56.4 us -> 45.9 us
    pallas_call x0 -> x1, Pallas kernels: none -> 12 us  [out_proj(): pl.pallas_call(out_proj_kernel, out_shape=jax.ShapeDtypeStruct((tokens, w...]
    dot_general x1 -> x0, matrix products: 10.7 us -> none  [per_device(): jnp.einsum('ghtd,ghdo->gto', attended, full_out_weight.reshape(seq_count,...]
    reshape x0 -> x3, local copies, waits for them, and re-layouts: none -> 6.43 us  [the longest x2 5.83 us: per_device(): hidden.reshape(lines, 2, half_grid, 2, D)]
    reduce_sum x1 -> x0, local copies, waits for them, and re-layouts: 5.32 us -> none  [per_device(): attn = jnp.sum(group_terms.astype(jnp.float32), axis=0)]
    unnamed x24 -> x22, local copies, waits for them, and re-layouts: 8.09 us -> 8.02 us
where the time goes in v3:
time: 361 us; the launch traced here: 360 us
  waiting for transfers between devices  185 us (51%)
  Pallas kernels  60.4 us (17%)
  matrix products  45.9 us (13%)
  local copies, waits for them, and re-layouts  30.4 us (8%)
  other arithmetic  18.5 us (5%)
  between operations  13.3 us (4%)
  starting transfers between devices  6.91 us (2%)
    reduce_scatter x1, waiting for transfers between devices, per_device(): lax.psum_scatter(partial.reshape(row_count * merged_count, -1), 'rows', s...  93.6 us
    all_gather x1, waiting for transfers between devices, per_device(): row_tokens = lax.all_gather(normed, 'seq', axis=0, tiled=True)  58.2 us
    pallas_call x1, Pallas kernels, attend_kernel(): pl.pallas_call(functools.partial(attention_kernel, scale), out_shape=jax....  36.8 us
    dot_general x3, matrix products, per_device(): jnp.dot(row_tokens, weight_parts[:, :, c].reshape(qkv_weight.shape[0], he...  25.2 us
    all_to_all x1, waiting for transfers between devices, per_device(): lax.all_to_all(merged_norm, 'rows', split_axis=1, concat_axis=0, tiled=True)  23.5 us
    dot_general x1, matrix products, per_device(): jnp.dot(ordered, fc_weight, preferred_element_type=jnp.float32)  19.4 us
    pallas_call x1, Pallas kernels, out_proj(): pl.pallas_call(out_proj_kernel, out_shape=jax.ShapeDtypeStruct((tokens, w...  12 us
    pallas_call x1, Pallas kernels, seq_sum(): pl.pallas_call(seq_sum_kernel, out_shape=jax.ShapeDtypeStruct(part.shape,...  11.6 us
  transfers between devices with their start and end apart: 4, of which 4 were waited for; matrix products, arithmetic and copies ran while one was open for 13% of the time, Pallas kernels for 13%

profile of v3, /device:TPU:1, one launch (start us, length us, event | category | flops | bytes accessed | tf_op | source)
XLA Modules:
  0.0 360.0 jit_solution(6230101657057996113)
XLA Ops:
  6.5 0.0 all-gather.4.cloned.1.call-start
  6.5 2.0 fusion.1
  8.5 0.0 copy-done
  8.5 2.4 fusion.3
  10.9 0.0 all-gather.4.cloned.1.call-update
  10.9 0.0 all-gather.6.cloned.1.call-start
  10.9 0.7 all-gather.6.cloned.1.call-update
  11.7 0.0 copy-start.5
  11.7 0.0 copy-start.4
  11.7 0.0 copy-start.1
  11.7 0.0 copy-start.2
  11.7 0.0 copy-start.6
  11.7 7.5 %copy.26 = bf16[3200,768]{0,1:T(8,128)(2,1)} copy(bf16[3200,768]{1,0:T(8,128)(2,1)} %param.15) | data formatting | bytes 9830400 | tf_op args[2]
  19.2 0.0 copy-done.5
  19.2 0.8 copy.27.qg_ref
  20.0 0.8 copy.28.kg_ref
  20.8 0.0 copy-done.4
  20.8 0.6 reshape.143.ls_ref
  21.4 0.0 copy-done.1
  21.4 0.1 add.79
  21.5 0.0 copy-done.2
  21.5 0.1 mul.108
  21.6 0.0 copy-done.6
  21.6 4.4 %fusion.32 = (bf16[3200,2,1,128]{0,3,2,1:T(8,128)(2,1)S(1)}, bf16[3200,2,1,128]{0,3,2,1:T(8,128)(2,1)S(1)}, bf16[3200,2,1,128]{0,3,2,1:T(8,128)(2,1)}) fusion(bf16[3200,2,3,128]{0,3,2,1:T(8,128)(2,1)} %bitcast.46), kind=kLoop, calls=%fused_computation.61 | loop fusion | bytes 9830400 | tf_op jit(solution)/shard_map/slice | solution.py:264
  26.0 58.2 %all-gather.4.cloned.1.call-done = bf16[2048,3200]{1,0:T(8,128)(2,1)} async-done(((bf16[256,3200]{1,0:T(8,128)(2,1)}), bf16[2048,3200]{1,0:T(8,128)(2,1)}) %all-gather.4.cloned.1.call-update) | async-done | bytes 13107216 | tf_op jit(solution)/shard_map/all_gather | solution.py:257
  84.2 10.3 %multiply_reduce_fusion.2 = (f32[2048]{0:T(1024)S(1)}, f32[2048,256]{0,1:T(8,128)}) fusion(bf16[2048,3200]{1,0:T(8,128)(2,1)} %all-gather.4.cloned.1.call-done, bf16[3200,256]{0,1:T(8,128)(2,1)} %bitcast.53), kind=kOutput, calls=%fused_computation.13 | convolution fusion | flops 3356489728 | bytes 16850944 | tf_op jit(solution)/shard_map/dot_general | solution.py:262
  94.5 0.0 copy-done.9
  94.5 5.2 %multiply_reduce_fusion.1 = (f32[2048]{0:T(1024)S(1)}, f32[2048,256]{0,1:T(8,128)}) fusion(bf16[2048,3200]{1,0:T(8,128)(2,1)S(1)} %copy-done.9, bf16[3200,256]{0,1:T(8,128)(2,1)S(1)} %bitcast.52), kind=kOutput, calls=%fused_computation.12 | convolution fusion | flops 3356489728 | bytes 16850944 | tf_op jit(solution)/shard_map/dot_general | solution.py:262
  99.7 0.6 pad_maximum_fusion.part_ref
  100.4 11.6 %shard_map.127 = f32[3,2048]{1,0:T(4,128)} custom-call(f32[3,2048]{1,0:T(4,128)} %pad_maximum_fusion.part_ref), custom_call_target="tpu_custom_call" | custom-call | tf_op jit(solution)/shard_map/pallas_call | solution.py:61
  112.0 1.5 fusion.33
  113.5 1.4 copy.29.qseg_ref
  114.9 9.7 %convolution_convert_fusion.v_ref = bf16[2048,256]{1,0:T(8,128)(2,1)} fusion(bf16[2048,3200]{1,0:T(8,128)(2,1)} %all-gather.4.cloned.1.call-done, bf16[3200,256]{0,1:T(8,128)(2,1)S(1)} %bitcast.51), kind=kOutput, calls=%fused_computation.10 | convolution fusion | flops 3355967488 | bytes 15794176 | tf_op jit(solution)/shard_map/dot_general | solution.py:262
  124.6 36.8 %shard_map.128.att_ref = bf16[8,2,256,128]{3,2,1,0:T(8,128)(2,1)} custom-call(f32[256,2048]{1,0:T(8,128)} %bitcast.56, f32[256,2048]{1,0:T(8,128)} %bitcast.57, bf16[2048,256]{1,0:T(8,128)(2,1)} %convolution_convert_fusion.v_ref, f32[1,2048]{1,0:T(1,128)} %get-tuple-element.11.qrs_ref, f32[1,2048]{1,0:T(1,128)} %get-tuple-element.10.krs_ref, ...), custom_call_target="tpu_custom_call" | custom-call | flops 4294967296 | bytes 6291456 | tf_op jit(solution)/shard_map/pallas_call | solution.py:163
  161.3 8.5 %all-gather.6.cloned.1.call-done = bf16[2048,3200]{1,0:T(8,128)(2,1)} async-done(((bf16[256,3200]{1,0:T(8,128)(2,1)}), bf16[2048,3200]{1,0:T(8,128)(2,1)}) %all-gather.6.cloned.1.call-update) | async-done | bytes 13107216 | tf_op jit(solution)/shard_map/all_gather | solution.py:299
  169.9 12.0 %shard_map.129 = f32[256,3200]{1,0:T(8,128)} custom-call(bf16[8,2,256,128]{3,2,1,0:T(8,128)(2,1)} %shard_map.128.att_ref, bf16[8,2,128,3200]{3,2,1,0:T(8,128)(2,1)} %bitcast.48, bf16[256,3200]{1,0:T(8,128)(2,1)} %bitcast.47, f32[1,3200]{1,0:T(1,128)} %reshape.143.ls_ref), custom_call_target="tpu_custom_call" | custom-call | flops 3355443200 | bytes 18022400 | tf_op jit(solution)/shard_map/pallas_call | solution.py:216
  181.9 3.8 %reshape.144 = f32[4,2,16,2,3200]{4,3,2,1,0:T(2,128)S(1)} reshape(f32[256,3200]{1,0:T(8,128)} %shard_map.129) | data formatting | bytes 6553600 | tf_op jit(solution)/shard_map/reshape | solution.py:309
  185.7 0.7 fusion.31
  186.4 1.9 multiply_reduce_fusion
  188.4 0.1 div.25
  188.4 2.0 copy.47
  190.5 0.1 rsqrt.31
  190.6 5.8 %reshape.145 = f32[64,16,800]{2,1,0:T(8,128)} reshape(f32[4,16,2,2,3200]{4,3,2,1,0:T(2,128)} %bitcast.49) | data formatting | bytes 6553600 | tf_op jit(solution)/shard_map/reshape | solution.py:309
  196.4 2.7 add_convert_fusion.1
  199.1 1.7 copy.31
  200.8 6.8 %all-to-all-start = ((bf16[64,16,800]{2,0,1:T(8,128)(2,1)}), bf16[64,16,800]{2,0,1:T(8,128)(2,1)S(1)}, u32[]{:S(2)}, u32[]{:S(2)}) async-start(bf16[64,16,800]{2,0,1:T(8,128)(2,1)} %copy.31), calls=%async_computation | async-start | bytes 3670016 | tf_op jit(solution)/shard_map/all_to_all | solution.py:323
  207.6 0.0 reduce-scatter.2.cloned.1.call-start
  207.7 0.5 broadcast.126
  208.2 0.0 copy-done.7
  208.2 0.7 reduce.7
  208.8 0.1 reshape_squeeze.28
  209.0 0.1 fusion.27
  209.1 0.1 mul.114
  209.2 0.0 copy-done.8
  209.2 0.6 dynamic_slice.3
  209.8 0.6 compare_convert_fusion
  210.4 0.1 broadcast_multiply_fusion
  210.5 23.5 %all-to-all-done = bf16[64,16,800]{2,0,1:T(8,128)(2,1)S(1)} async-done(((bf16[64,16,800]{2,0,1:T(8,128)(2,1)}), bf16[64,16,800]{2,0,1:T(8,128)(2,1)S(1)}, u32[]{:S(2)}, u32[]{:S(2)}) %all-to-all-start) | async-done | bytes 1638432 | tf_op jit(solution)/shard_map/all_to_all | solution.py:323
  234.0 1.3 fusion.8
  235.2 19.4 %add_convert_fusion = bf16[16,64,6144]{2,1,0:T(8,128)(2,1)} fusion(f32[16,64]{1,0:T(8,128)S(1)} %broadcast_multiply_fusion, bf16[800,6144]{1,0:T(8,128)(2,1)} %param.23, bf16[16,64,800]{2,0,1:T(8,128)(2,1)S(1)} %fusion.8), kind=kOutput, calls=%fused_computation | convolution fusion | flops 10078912512 | bytes 24055808 | tf_op jit(solution)/shard_map/dot_general | solution.py:334
  254.7 0.0 reduce-scatter.2.cloned.1.call-update
  254.7 93.6 %reduce-scatter.2.cloned.1.call-done = bf16[64,6144]{1,0:T(8,128)(2,1)} async-done(((bf16[1024,6144]{1,0:T(8,128)(2,1)}), bf16[64,6144]{1,0:T(8,128)(2,1)}) %reduce-scatter.2.cloned.1.call-update) | async-done | bytes 786448 | tf_op jit(solution)/shard_map/reduce_scatter | solution.py:340
  348.3 0.0 copy-done.3
  348.3 5.2 %fusion.24 = bf16[1,64,6144]{2,1,0:T(8,128)(2,1)} fusion(bf16[64,6144]{1,0:T(8,128)(2,1)} %reduce-scatter.2.cloned.1.call-done, f32[6144]{0:T(1024)S(1)} %copy-done.3), kind=kLoop, calls=%fused_computation.40 | loop fusion | flops 26345472 | bytes 1597440 | tf_op jit(solution)/shard_map/broadcast_in_dim | solution.py:347
  (11 shorter events, 0.1 us)
Async XLA Ops:
  6.5 2.0 copy-start
  6.5 77.7 %all-gather.4.cloned.1.call-start = ((), (), s32[]{:S(2)}) async-start(), calls=%async_computation.2 | async-start | bytes 14745600 | tf_op jit(solution)/shard_map/all_gather | solution.py:257
  10.9 159.0 %all-gather.6.cloned.1.call-start = ((), (), s32[]{:S(2)}) async-start(), calls=%async_computation.4 | async-start | bytes 14745600 | tf_op jit(solution)/shard_map/all_gather | solution.py:299
  11.7 7.5 %copy-start.5 = (f32[2,256]{1,0:T(2,128)S(1)}, f32[2,256]{1,0:T(2,128)}, u32[]{:S(2)}) copy-start(f32[2,256]{1,0:T(2,128)} %param.16) | copy-start | bytes 6148
  11.7 9.1 %copy-start.4 = (f32[3200]{0:T(1024)S(1)}, f32[3200]{0:T(1024)}, u32[]{:S(2)}) copy-start(f32[3200]{0:T(1024)} %param.18) | copy-start | bytes 38404
  11.7 9.7 %copy-start.1 = (f32[12800]{0:T(1024)S(1)}, f32[12800]{0:T(1024)}, u32[]{:S(2)}) copy-start(f32[12800]{0:T(1024)} %param.22) | copy-start | bytes 153604
  11.7 9.8 %copy-start.2 = (f32[12800]{0:T(1024)S(1)}, f32[12800]{0:T(1024)}, u32[]{:S(2)}) copy-start(f32[12800]{0:T(1024)} %param.21) | copy-start | bytes 153604
  11.7 9.9 %copy-start.6 = (s32[1,256]{1,0:T(1,128)S(1)}, s32[1,256]{1,0:T(1,128)}, u32[]{:S(2)}) copy-start(s32[1,256]{1,0:T(1,128)} %param.19) | copy-start | bytes 3076
  84.2 10.3 %copy-start.9 = (bf16[2048,3200]{1,0:T(8,128)(2,1)S(1)}, bf16[2048,3200]{1,0:T(8,128)(2,1)}, u32[]{:S(2)}) copy-start(bf16[2048,3200]{1,0:T(8,128)(2,1)} %all-gather.4.cloned.1.call-done) | copy-start | bytes 39321604
  200.8 7.4 %copy-start.7 = (s32[1,256]{1,0:T(1,128)S(1)}, s32[1,256]{1,0:T(1,128)}, u32[]{:S(2)}) copy-start(s32[1,256]{1,0:T(1,128)} %param.20) | copy-start | bytes 3076
  200.8 8.4 %copy-start.8 = (s32[16]{0:T(128)S(1)}, s32[16]{0:T(128)}, u32[]{:S(2)}) copy-start(s32[16]{0:T(128)} %param.25) | copy-start | bytes 196
  200.8 33.2 %all-to-all-start = ((bf16[64,16,800]{2,0,1:T(8,128)(2,1)}), bf16[64,16,800]{2,0,1:T(8,128)(2,1)S(1)}, u32[]{:S(2)}, u32[]{:S(2)}) async-start(bf16[64,16,800]{2,0,1:T(8,128)(2,1)} %copy.31), calls=%async_computation | async-start | bytes 3670016 | tf_op jit(solution)/shard_map/all_to_all | solution.py:323
  207.6 140.7 %reduce-scatter.2.cloned.1.call-start = ((), (), s32[]{:S(2)}) async-start(), calls=%async_computation.3 | async-start | bytes 13369344 | tf_op jit(solution)/shard_map/reduce_scatter | solution.py:340
  254.7 93.7 %copy-start.3 = (f32[6144]{0:T(1024)S(1)}, f32[6144]{0:T(1024)}, u32[]{:S(2)}) copy-start(f32[6144]{0:T(1024)} %param.24) | copy-start | bytes 73732
Sparse Core Ops, SparseCore 0:
  11.0 73.1 all-gather.3
  85.9 83.9 all-gather.5
  254.8 93.4 reduce-scatter.1

commit v4 on v3

--- a/solution.py
+++ b/solution.py
@@ -73,7 +73,7 @@
 
 
 def attention_kernel(scale, q_ref, k_ref, v_ref, qrs_ref, krs_ref, qg_ref, kg_ref, qseg_ref,
-                     kseg_ref, o_ref, key_norm, slots, landing, send_sem, recv_sem, local_sem):
+                     kseg_ref, o_ref, key_norm, value_half, slots, landing, send_sem, recv_sem, local_sem):
     head, block = pl.program_id(0), pl.program_id(1)
     blocks = pl.num_programs(1)
     heads = pl.num_programs(0)
@@ -93,6 +93,7 @@
         key_norm[...] = jnp.transpose(
             (k_ref[...] * krs_ref[...] * kg_ref[...]).astype(jnp.bfloat16)
         )
+        value_half[...] = jnp.transpose(v_ref[...].astype(jnp.bfloat16))
 
     query_norm = jnp.transpose((q_ref[...] * qrs_ref[...] * qg_ref[...]).astype(jnp.bfloat16))
     scores = (
@@ -107,7 +108,7 @@
     total = jnp.sum(exp_terms, axis=-1, keepdims=True)
     probs = (exp_terms / total).astype(jnp.bfloat16)
     step = head * blocks + block
-    slots[step] = jnp.dot(probs, v_ref[...], preferred_element_type=jnp.float32).astype(
+    slots[step] = jnp.dot(probs, value_half[...], preferred_element_type=jnp.float32).astype(
         slots.dtype
     )
 
@@ -153,10 +154,10 @@
         o_ref[...] = landing[...]
 
 
-def attend_kernel(query_raw, key_raw, value_half, query_rs, key_rs, qk_gain, row_segments,
-                  block_len, scale):
-    length, width = query_raw.shape
-    heads_here = width // HEAD_DIM
+def attend_kernel(projected_t, query_rs, key_rs, qk_gain, row_segments, block_len, scale):
+    length = projected_t.shape[1]
+    heads_here = projected_t.shape[0] // (3 * HEAD_DIM)
+    width = heads_here * HEAD_DIM
     blocks = length // block_len
     flops = 4 * length * length * width
     gain_block = pl.BlockSpec((HEAD_DIM, 1), lambda h, i: (h, 0))
@@ -165,9 +166,9 @@
         out_shape=jax.ShapeDtypeStruct((blocks, heads_here, block_len, HEAD_DIM), jnp.bfloat16),
         grid=(heads_here, blocks),
         in_specs=[
-            pl.BlockSpec((HEAD_DIM, block_len), lambda h, i: (h, i)),
-            pl.BlockSpec((HEAD_DIM, length), lambda h, i: (h, 0)),
-            pl.BlockSpec((length, HEAD_DIM), lambda h, i: (0, h)),
+            pl.BlockSpec((HEAD_DIM, block_len), lambda h, i: (3 * h, i)),
+            pl.BlockSpec((HEAD_DIM, length), lambda h, i: (3 * h + 1, 0)),
+            pl.BlockSpec((HEAD_DIM, length), lambda h, i: (3 * h + 2, 0)),
             pl.BlockSpec((1, block_len), lambda h, i: (0, i)),
             pl.BlockSpec((1, length), lambda h, i: (0, 0)),
             gain_block,
@@ -177,6 +178,7 @@
         ],
         out_specs=pl.BlockSpec(memory_space=pltpu.VMEM),
         scratch_shapes=[
+            pltpu.VMEM((length, HEAD_DIM), jnp.bfloat16),
             pltpu.VMEM((length, HEAD_DIM), jnp.bfloat16),
             pltpu.VMEM((heads_here * blocks, block_len, HEAD_DIM), jnp.bfloat16),
             pltpu.VMEM((blocks, heads_here, block_len, HEAD_DIM), jnp.bfloat16),
@@ -189,9 +191,9 @@
             flops=flops, transcendentals=length * length * heads_here, bytes_accessed=12 * length * width
         ),
     )(
-        query_raw.T,
-        key_raw.T,
-        value_half,
+        projected_t,
+        projected_t,
+        projected_t,
         query_rs.reshape(1, length),
         key_rs.reshape(1, length),
         qk_gain[0].reshape(width, 1),
@@ -257,16 +259,8 @@
     row_tokens = lax.all_gather(normed, "seq", axis=0, tiled=True)
     length = row_tokens.shape[0]
     heads_here = qkv_weight.shape[1] // (3 * HEAD_DIM)
-    weight_parts = qkv_weight.reshape(qkv_weight.shape[0], heads_here, 3, HEAD_DIM)
-    query_raw, key_raw, value_raw = (
-        jnp.dot(
-            row_tokens,
-            weight_parts[:, :, c].reshape(qkv_weight.shape[0], heads_here * HEAD_DIM),
-            preferred_element_type=jnp.float32,
-        )
-        for c in range(3)
-    )
-    value_half = value_raw.astype(jnp.bfloat16)
+    projected_t = jnp.dot(row_tokens, qkv_weight, preferred_element_type=jnp.float32).T
+    parts_t = projected_t.reshape(heads_here, 3, HEAD_DIM, length)
     seg_spread = lax.dynamic_update_slice_in_dim(
         jnp.zeros((length,), jnp.float32),
         segment_ids[0].astype(jnp.float32),
@@ -276,8 +270,8 @@
     stats = seq_sum(
         jnp.stack(
             [
-                jnp.sum(query_raw * query_raw, axis=1),
-                jnp.sum(key_raw * key_raw, axis=1),
+                jnp.sum(parts_t[:, 0] * parts_t[:, 0], axis=(0, 1)),
+                jnp.sum(parts_t[:, 1] * parts_t[:, 1], axis=(0, 1)),
                 seg_spread,
             ]
         )
@@ -286,9 +280,7 @@
     norm_width = HEADS * HEAD_DIM
     scale = HEAD_DIM ** (-0.5)
     attended = attend_kernel(
-        query_raw,
-        key_raw,
-        value_half,
+        projected_t,
         lax.rsqrt(query_sq / norm_width + 1e-06),
         lax.rsqrt(key_sq / norm_width + 1e-06),
         qk_gain,

time: 361 us -> 361 us (level)
  waiting for transfers between devices: 185 us -> 202 us
  matrix products: 45.9 us -> 36.2 us
  local copies, waits for them, and re-layouts: 30.4 us -> 21.4 us
    all_gather x1, waiting for transfers between devices: 58.2 us -> 70.1 us  [per_device(): row_tokens = lax.all_gather(normed, 'seq', axis=0, tiled=True)]
    dot_general x3 -> x1, matrix products: 25.2 us -> 15.7 us  [per_device(): jnp.dot(row_tokens, qkv_weight, preferred_element_type=jnp.float32)]
    all_gather x1, waiting for transfers between devices: 8.51 us -> 14.3 us  [per_device(): full_out_weight = lax.all_gather(out_weight, 'seq', axis=0, tiled=False)]
    unnamed x22 -> x21, local copies, waits for them, and re-layouts: 8.02 us -> 3.15 us
    slice x1 -> x0, local copies, waits for them, and re-layouts: 4.38 us -> none  [per_device(): weight_parts[:, :, c].reshape(qkv_weight.shape[0], heads_here * HEAD_DIM)]
  transfers between devices with their start and end apart: 4 -> 4, of which waited for: 4 -> 4; matrix products, arithmetic and copies ran while one was open for 13% -> 7% of each run, Pallas kernels for 13% -> 14%
where the time goes in v4:
time: 361 us; the launch traced here: 360 us
  waiting for transfers between devices  202 us (56%)
  Pallas kernels  61.1 us (17%)
  matrix products  36.2 us (10%)
  local copies, waits for them, and re-layouts  21.4 us (6%)
  other arithmetic  19 us (5%)
  between operations  13.3 us (4%)
  starting transfers between devices  6.91 us (2%)
    reduce_scatter x1, waiting for transfers between devices, per_device(): lax.psum_scatter(partial.reshape(row_count * merged_count, -1), 'rows', s...  93.6 us
    all_gather x1, waiting for transfers between devices, per_device(): row_tokens = lax.all_gather(normed, 'seq', axis=0, tiled=True)  70.1 us
    pallas_call x1, Pallas kernels, attend_kernel(): pl.pallas_call(functools.partial(attention_kernel, scale), out_shape=jax....  37.5 us
    all_to_all x1, waiting for transfers between devices, per_device(): lax.all_to_all(merged_norm, 'rows', split_axis=1, concat_axis=0, tiled=True)  23.4 us
    dot_general x1, matrix products, per_device(): jnp.dot(ordered, fc_weight, preferred_element_type=jnp.float32)  19.2 us
    dot_general x1, matrix products, per_device(): jnp.dot(row_tokens, qkv_weight, preferred_element_type=jnp.float32)  15.7 us
    all_gather x1, waiting for transfers between devices, per_device(): full_out_weight = lax.all_gather(out_weight, 'seq', axis=0, tiled=False)  14.3 us
    pallas_call x1, Pallas kernels, out_proj(): pl.pallas_call(out_proj_kernel, out_shape=jax.ShapeDtypeStruct((tokens, w...  12 us
  transfers between devices with their start and end apart: 4, of which 4 were waited for; matrix products, arithmetic and copies ran while one was open for 7% of the time, Pallas kernels for 14%

profile of v4, /device:TPU:1, one launch (start us, length us, event | category | flops | bytes accessed | tf_op | source)
XLA Modules:
  0.0 359.9 jit_solution(1141855930159905215)
XLA Ops:
  6.5 0.0 copy-start.1
  6.5 0.0 all-gather.4.cloned.1.call-start
  6.5 2.0 fusion.1
  8.5 0.0 copy-done.1
  8.5 2.4 fusion.3
  10.9 0.0 copy-start.6
  10.9 0.0 copy-start.5
  10.9 0.0 copy-start.2
  10.9 0.0 copy-start.3
  10.9 0.0 copy-start.7
  10.9 0.0 all-gather.4.cloned.1.call-update
  10.9 0.0 all-gather.6.cloned.1.call-start
  11.0 0.7 all-gather.6.cloned.1.call-update
  11.7 0.0 copy-done.6
  11.7 0.8 copy.24.qg_ref
  12.5 0.8 copy.25.kg_ref
  13.3 0.0 copy-done.5
  13.3 0.6 reshape.145.ls_ref
  13.9 0.0 copy-done.2
  13.9 0.1 add.79
  14.0 0.0 copy-done.3
  14.0 0.1 mul.110
  14.1 0.0 copy-done.7
  14.2 70.1 %all-gather.4.cloned.1.call-done = bf16[2048,3200]{1,0:T(8,128)(2,1)} async-done(((bf16[256,3200]{1,0:T(8,128)(2,1)}), bf16[2048,3200]{1,0:T(8,128)(2,1)}) %all-gather.4.cloned.1.call-update) | async-done | bytes 13107216 | tf_op jit(solution)/shard_map/all_gather | solution.py:259
  84.2 15.7 %fusion.35 = f32[2048,768]{0,1:T(8,128)S(1)} fusion(bf16[2048,3200]{1,0:T(8,128)(2,1)} %all-gather.4.cloned.1.call-done, bf16[3200,768]{1,0:T(8,128)(2,1)} %param.15), kind=kOutput, calls=%fused_computation.63 | convolution fusion | flops 10066329600 | bytes 24313856 | tf_op jit(solution)/shard_map/dot_general | solution.py:262
  99.9 0.0 copy-start
  99.9 2.6 copy-done
  102.5 0.4 fusion.5
  102.9 0.6 pad_maximum_fusion.part_ref
  103.6 11.6 %shard_map.127 = f32[3,2048]{1,0:T(4,128)} custom-call(f32[3,2048]{1,0:T(4,128)} %pad_maximum_fusion.part_ref), custom_call_target="tpu_custom_call" | custom-call | tf_op jit(solution)/shard_map/pallas_call | solution.py:61
  115.2 1.5 fusion.34
  116.7 1.3 copy.26.qseg_ref
  118.1 37.5 %shard_map.128.att_ref = bf16[8,2,256,128]{3,2,1,0:T(8,128)(2,1)} custom-call(f32[768,2048]{1,0:T(8,128)} %bitcast.40, f32[768,2048]{1,0:T(8,128)} %bitcast.41, f32[768,2048]{1,0:T(8,128)} %bitcast.42, f32[1,2048]{1,0:T(1,128)} %get-tuple-element.10.qrs_ref, f32[1,2048]{1,0:T(1,128)} %get-tuple-element.9.krs_ref, f32[256,1]{1,0:T(8,128)} %copy.24.qg_ref, ...), custom_call_target="tpu_custom_call" | custom-call | flops 4294967296 | bytes 6291456 | tf_op jit(solution)/shard_map/pallas_call | solution.py:164
  155.5 14.3 %all-gather.6.cloned.1.call-done = bf16[2048,3200]{1,0:T(8,128)(2,1)} async-done(((bf16[256,3200]{1,0:T(8,128)(2,1)}), bf16[2048,3200]{1,0:T(8,128)(2,1)}) %all-gather.6.cloned.1.call-update) | async-done | bytes 13107216 | tf_op jit(solution)/shard_map/all_gather | solution.py:291
  169.9 12.0 %shard_map.129 = f32[256,3200]{1,0:T(8,128)} custom-call(bf16[8,2,256,128]{3,2,1,0:T(8,128)(2,1)} %shard_map.128.att_ref, bf16[8,2,128,3200]{3,2,1,0:T(8,128)(2,1)} %bitcast.44, bf16[256,3200]{1,0:T(8,128)(2,1)} %bitcast.43, f32[1,3200]{1,0:T(1,128)} %reshape.145.ls_ref), custom_call_target="tpu_custom_call" | custom-call | flops 3355443200 | bytes 18022400 | tf_op jit(solution)/shard_map/pallas_call | solution.py:218
  181.8 4.0 %reshape.146 = f32[4,2,16,2,3200]{4,3,2,1,0:T(2,128)S(1)} reshape(f32[256,3200]{1,0:T(8,128)} %shard_map.129) | data formatting | bytes 6553600 | tf_op jit(solution)/shard_map/reshape | solution.py:301
  185.8 0.7 fusion.33
  186.6 1.9 multiply_reduce_fusion
  188.5 0.1 div.25
  188.6 2.0 copy.44
  190.6 0.1 rsqrt.31
  190.7 5.8 %reshape.147 = f32[64,16,800]{2,1,0:T(8,128)} reshape(f32[4,16,2,2,3200]{4,3,2,1,0:T(2,128)} %bitcast.45) | data formatting | bytes 6553600 | tf_op jit(solution)/shard_map/reshape | solution.py:301
  196.5 2.7 add_convert_fusion.1
  199.2 1.7 copy.28
  200.9 0.0 copy-start.8
  200.9 6.8 %all-to-all-start = ((bf16[64,16,800]{2,0,1:T(8,128)(2,1)}), bf16[64,16,800]{2,0,1:T(8,128)(2,1)S(1)}, u32[]{:S(2)}, u32[]{:S(2)}) async-start(bf16[64,16,800]{2,0,1:T(8,128)(2,1)} %copy.28), calls=%async_computation | async-start | bytes 3670016 | tf_op jit(solution)/shard_map/all_to_all | solution.py:315
  207.7 0.0 reduce-scatter.2.cloned.1.call-start
  207.8 0.5 broadcast.126
  208.3 0.0 copy-done.8
  208.3 0.7 reduce.9
  209.0 0.1 reshape_squeeze.16
  209.1 0.1 fusion.29
  209.2 0.1 mul.116
  209.3 0.0 copy-done.9
  209.3 0.6 dynamic_slice.3
  209.9 0.6 compare_convert_fusion
  210.5 0.1 broadcast_multiply_fusion
  210.6 23.4 %all-to-all-done = bf16[64,16,800]{2,0,1:T(8,128)(2,1)S(1)} async-done(((bf16[64,16,800]{2,0,1:T(8,128)(2,1)}), bf16[64,16,800]{2,0,1:T(8,128)(2,1)S(1)}, u32[]{:S(2)}, u32[]{:S(2)}) %all-to-all-start) | async-done | bytes 1638432 | tf_op jit(solution)/shard_map/all_to_all | solution.py:315
  234.1 1.3 fusion.10
  235.3 19.2 %add_convert_fusion = bf16[16,64,6144]{2,1,0:T(8,128)(2,1)} fusion(f32[16,64]{1,0:T(8,128)S(1)} %broadcast_multiply_fusion, bf16[800,6144]{1,0:T(8,128)(2,1)} %param.23, bf16[16,64,800]{2,0,1:T(8,128)(2,1)S(1)} %fusion.10), kind=kOutput, calls=%fused_computation | convolution fusion | flops 10078912512 | bytes 24055808 | tf_op jit(solution)/shard_map/dot_general | solution.py:326
  254.6 0.0 reduce-scatter.2.cloned.1.call-update
  254.6 93.6 %reduce-scatter.2.cloned.1.call-done = bf16[64,6144]{1,0:T(8,128)(2,1)} async-done(((bf16[1024,6144]{1,0:T(8,128)(2,1)}), bf16[64,6144]{1,0:T(8,128)(2,1)}) %reduce-scatter.2.cloned.1.call-update) | async-done | bytes 786448 | tf_op jit(solution)/shard_map/reduce_scatter | solution.py:332
  348.2 0.0 copy-done.4
  348.2 5.2 %fusion.26 = bf16[1,64,6144]{2,1,0:T(8,128)(2,1)} fusion(bf16[64,6144]{1,0:T(8,128)(2,1)} %reduce-scatter.2.cloned.1.call-done, f32[6144]{0:T(1024)S(1)} %copy-done.4), kind=kLoop, calls=%fused_computation.41 | loop fusion | flops 26345472 | bytes 1597440 | tf_op jit(solution)/shard_map/broadcast_in_dim | solution.py:339
  (8 shorter events, 0.0 us)
Async XLA Ops:
  6.5 2.0 copy-start.1
  6.5 77.7 %all-gather.4.cloned.1.call-start = ((), (), s32[]{:S(2)}) async-start(), calls=%async_computation.2 | async-start | bytes 14745600 | tf_op jit(solution)/shard_map/all_gather | solution.py:259
  10.9 0.8 copy-start.6
  10.9 2.4 copy-start.5
  10.9 3.0 copy-start.2
  10.9 3.1 copy-start.3
  10.9 3.2 copy-start.7
  10.9 159.0 %all-gather.6.cloned.1.call-start = ((), (), s32[]{:S(2)}) async-start(), calls=%async_computation.4 | async-start | bytes 14745600 | tf_op jit(solution)/shard_map/all_gather | solution.py:291
  99.9 2.6 copy-start
  200.9 7.4 %copy-start.8 = (s32[1,256]{1,0:T(1,128)S(1)}, s32[1,256]{1,0:T(1,128)}, u32[]{:S(2)}) copy-start(s32[1,256]{1,0:T(1,128)} %param.20) | copy-start | bytes 3076
  200.9 8.4 %copy-start.9 = (s32[16]{0:T(128)S(1)}, s32[16]{0:T(128)}, u32[]{:S(2)}) copy-start(s32[16]{0:T(128)} %param.25) | copy-start | bytes 196
  200.9 33.1 %all-to-all-start = ((bf16[64,16,800]{2,0,1:T(8,128)(2,1)}), bf16[64,16,800]{2,0,1:T(8,128)(2,1)S(1)}, u32[]{:S(2)}, u32[]{:S(2)}) async-start(bf16[64,16,800]{2,0,1:T(8,128)(2,1)} %copy.28), calls=%async_computation | async-start | bytes 3670016 | tf_op jit(solution)/shard_map/all_to_all | solution.py:315
  207.7 140.5 %reduce-scatter.2.cloned.1.call-start = ((), (), s32[]{:S(2)}) async-start(), calls=%async_computation.3 | async-start | bytes 13369344 | tf_op jit(solution)/shard_map/reduce_scatter | solution.py:332
  254.6 93.7 %copy-start.4 = (f32[6144]{0:T(1024)S(1)}, f32[6144]{0:T(1024)}, u32[]{:S(2)}) copy-start(f32[6144]{0:T(1024)} %param.24) | copy-start | bytes 73732
Sparse Core Ops, SparseCore 0:
  11.1 73.1 all-gather.3
  85.9 83.9 all-gather.5
  254.7 93.4 reduce-scatter.1

commit v5 on v4

--- a/solution.py
+++ b/solution.py
@@ -204,10 +204,13 @@
 
 
 def out_proj_kernel(att_ref, w_ref, res_ref, ls_ref, o_ref):
+    n = att_ref.shape[0]
+    me = lax.axis_index("seq")
     total = jnp.zeros(o_ref.shape, jnp.float32)
-    for g in range(att_ref.shape[0]):
-        term = jnp.dot(att_ref[g, 0], w_ref[g, 0], preferred_element_type=jnp.float32)
-        term = term + jnp.dot(att_ref[g, 1], w_ref[g, 1], preferred_element_type=jnp.float32)
+    for k in range(n):
+        g = lax.rem(me + n - k, n)
+        term = jnp.dot(att_ref[g, 0], w_ref[k, 0], preferred_element_type=jnp.float32)
+        term = term + jnp.dot(att_ref[g, 1], w_ref[k, 1], preferred_element_type=jnp.float32)
         total = total + term.astype(jnp.bfloat16).astype(jnp.float32)
     o_ref[...] = res_ref[...].astype(jnp.float32) + ls_ref[...] * total
 
@@ -288,7 +291,15 @@
         256,
         scale,
     )
-    full_out_weight = lax.all_gather(out_weight, "seq", axis=0, tiled=False)
+    full_out_weight = jnp.stack(
+        [out_weight]
+        + [
+            lax.ppermute(
+                out_weight, "seq", [(src, (src + k) % seq_count) for src in range(seq_count)]
+            )
+            for k in range(1, seq_count)
+        ]
+    )
     hidden = out_proj(
         attended,
         full_out_weight.reshape(seq_count, heads_here, HEAD_DIM, -1),

time: 361 us -> 479 us (1.33)
  waiting for transfers between devices: 202 us -> 300 us
  local copies, waits for them, and re-layouts: 21.4 us -> 39 us
  starting transfers between devices: 6.91 us -> 15.8 us
  Pallas kernels: 61.1 us -> 55 us
    ppermute x0 -> x7, waiting for transfers between devices: none -> 179 us  [per_device(): lax.ppermute(out_weight, 'seq', [(src, (src + k) % seq_count) for src in...]
    all_gather x1, waiting for transfers between devices: 70.1 us -> 0.57 us  [per_device(): row_tokens = lax.all_gather(normed, 'seq', axis=0, tiled=True)]
    unnamed x21 -> x30, local copies, waits for them, and re-layouts: 3.15 us -> 19.4 us
    all_gather x1 -> x0, waiting for transfers between devices: 14.3 us -> none  [per_device(): full_out_weight = lax.all_gather(out_weight, 'seq', axis=0, tiled=False)]
    ppermute x0 -> x7, starting transfers between devices: none -> 7.92 us  [per_device(): lax.ppermute(out_weight, 'seq', [(src, (src + k) % seq_count) for src in...]
  transfers between devices with their start and end apart: 4 -> 10, of which waited for: 4 -> 7; matrix products, arithmetic and copies ran while one was open for 7% -> 4% of each run, Pallas kernels for 14% -> 0%
where the time goes in v5:
time: 479 us; the launch traced here: 478 us
  waiting for transfers between devices  300 us (63%)
  Pallas kernels  55 us (11%)
  local copies, waits for them, and re-layouts  39 us (8%)
  matrix products  36.1 us (8%)
  other arithmetic  18.9 us (4%)
  starting transfers between devices  15.8 us (3%)
  between operations  13.6 us (3%)
    ppermute x7, waiting for transfers between devices, per_device(): lax.ppermute(out_weight, 'seq', [(src, (src + k) % seq_count) for src in...  179 us
    reduce_scatter x1, waiting for transfers between devices, per_device(): lax.psum_scatter(partial.reshape(row_count * merged_count, -1), 'rows', s...  97.5 us
    pallas_call x1, Pallas kernels, attend_kernel(): pl.pallas_call(functools.partial(attention_kernel, scale), out_shape=jax....  34.6 us
    all_to_all x1, waiting for transfers between devices, per_device(): lax.all_to_all(merged_norm, 'rows', split_axis=1, concat_axis=0, tiled=True)  22.5 us
    unnamed x30, local copies, waits for them, and re-layouts  19.4 us
    dot_general x1, matrix products, per_device(): jnp.dot(ordered, fc_weight, preferred_element_type=jnp.float32)  19.2 us
    dot_general x1, matrix products, per_device(): jnp.dot(row_tokens, qkv_weight, preferred_element_type=jnp.float32)  15.7 us
    pallas_call x1, Pallas kernels, out_proj(): pl.pallas_call(out_proj_kernel, out_shape=jax.ShapeDtypeStruct((tokens, w...  12 us
  transfers between devices with their start and end apart: 10, of which 7 were waited for; matrix products, arithmetic and copies ran while one was open for 4% of the time, Pallas kernels for 0%

profile of v5, /device:TPU:1, one launch (start us, length us, event | category | flops | bytes accessed | tf_op | source)
XLA Modules:
  0.0 477.9 jit_solution(14761412343461060558)
XLA Ops:
  6.5 2.0 fusion.1
  8.5 0.0 copy-start.7
  8.5 2.4 fusion.3
  10.9 0.0 all-gather.2.cloned.1.call-update
  10.9 1.4 copy-done.2
  12.3 2.6 collective-permute-start
  14.9 1.2 collective-permute-start.1
  16.1 1.6 collective-permute-start.2
  17.7 0.5 collective-permute-start.3
  18.2 1.9 collective-permute-start.4
  20.1 0.8 copy.24.qg_ref
  20.9 0.8 copy.25.kg_ref
  21.7 0.6 reshape.158.ls_ref
  22.3 0.1 add.79
  22.4 0.1 mul.110
  22.5 0.0 copy-start.8
  22.5 1.3 constant_dynamic-update-slice_fusion.7
  23.9 50.0 %collective-permute-done = bf16[256,3200]{1,0:T(8,128)(2,1)} collective-permute-done((bf16[256,3200]{1,0:T(8,128)(2,1)S(1)}, bf16[256,3200]{1,0:T(8,128)(2,1)}, u32[]{:S(2)}, u32[]{:S(2)}) %collective-permute-start) | collective-permute-done | bytes 1638432 | tf_op jit(solution)/shard_map/ppermute | solution.py:297
  73.9 0.1 collective-permute-start.5
  74.0 2.8 constant_dynamic-update-slice_fusion.6
  76.8 61.0 %collective-permute-done.1 = bf16[256,3200]{1,0:T(8,128)(2,1)} collective-permute-done((bf16[256,3200]{1,0:T(8,128)(2,1)S(1)}, bf16[256,3200]{1,0:T(8,128)(2,1)}, u32[]{:S(2)}, u32[]{:S(2)}) %collective-permute-start.1) | collective-permute-done | bytes 1638432 | tf_op jit(solution)/shard_map/ppermute | solution.py:297
  137.8 2.7 constant_dynamic-update-slice_fusion.5
  140.5 32.4 %collective-permute-done.2 = bf16[256,3200]{1,0:T(8,128)(2,1)} collective-permute-done((bf16[256,3200]{1,0:T(8,128)(2,1)S(1)}, bf16[256,3200]{1,0:T(8,128)(2,1)}, u32[]{:S(2)}, u32[]{:S(2)}) %collective-permute-start.2) | collective-permute-done | bytes 1638432 | tf_op jit(solution)/shard_map/ppermute | solution.py:297
  172.9 2.7 constant_dynamic-update-slice_fusion.4
  175.6 35.4 %collective-permute-done.3 = bf16[256,3200]{1,0:T(8,128)(2,1)} collective-permute-done((bf16[256,3200]{1,0:T(8,128)(2,1)S(1)}, bf16[256,3200]{1,0:T(8,128)(2,1)}, u32[]{:S(2)}, u32[]{:S(2)}) %collective-permute-start.3) | collective-permute-done | bytes 1638432 | tf_op jit(solution)/shard_map/ppermute | solution.py:297
  211.1 2.7 constant_dynamic-update-slice_fusion.3
  213.8 1.3 constant_dynamic-update-slice_fusion.2
  215.1 1.3 constant_dynamic-update-slice_fusion.1
  216.4 1.4 constant_dynamic-update-slice_fusion.w_ref
  217.7 0.6 all-gather.2.cloned.1.call-done
  218.3 15.7 %fusion.35 = f32[2048,768]{0,1:T(8,128)S(1)} fusion(bf16[2048,3200]{1,0:T(8,128)(2,1)} %all-gather.2.cloned.1.call-done, bf16[3200,768]{1,0:T(8,128)(2,1)} %param.15), kind=kOutput, calls=%fused_computation.71 | convolution fusion | flops 10066329600 | bytes 24313856 | tf_op jit(solution)/shard_map/dot_general | solution.py:265
  234.0 2.6 copy-done
  236.7 0.4 fusion.5
  237.1 0.6 pad_maximum_fusion.part_ref
  237.7 8.4 %shard_map.127 = f32[3,2048]{1,0:T(4,128)} custom-call(f32[3,2048]{1,0:T(4,128)} %pad_maximum_fusion.part_ref), custom_call_target="tpu_custom_call" | custom-call | tf_op jit(solution)/shard_map/pallas_call | solution.py:61
  246.1 1.5 fusion.34
  247.7 1.4 copy.26.qseg_ref
  249.0 34.6 %shard_map.128.att_ref = bf16[8,2,256,128]{3,2,1,0:T(8,128)(2,1)} custom-call(f32[768,2048]{1,0:T(8,128)} %bitcast.47, f32[768,2048]{1,0:T(8,128)} %bitcast.48, f32[768,2048]{1,0:T(8,128)} %bitcast.49, f32[1,2048]{1,0:T(1,128)} %get-tuple-element.10.qrs_ref, f32[1,2048]{1,0:T(1,128)} %get-tuple-element.9.krs_ref, f32[256,1]{1,0:T(8,128)} %copy.24.qg_ref, ...), custom_call_target="tpu_custom_call" | custom-call | flops 4294967296 | bytes 6291456 | tf_op jit(solution)/shard_map/pallas_call | solution.py:164
  283.6 12.0 %shard_map.129 = f32[256,3200]{1,0:T(8,128)} custom-call(bf16[8,2,256,128]{3,2,1,0:T(8,128)(2,1)} %shard_map.128.att_ref, bf16[8,2,128,3200]{3,2,1,0:T(8,128)(2,1)} %constant_dynamic-update-slice_fusion.w_ref, bf16[256,3200]{1,0:T(8,128)(2,1)} %bitcast.50, f32[1,3200]{1,0:T(1,128)} %reshape.158.ls_ref), custom_call_target="tpu_custom_call" | custom-call | flops 3355443200 | bytes 18022400 | tf_op jit(solution)/shard_map/pallas_call | solution.py:221
  295.6 4.0 reshape.159
  299.6 0.7 fusion.33
  300.4 1.9 multiply_reduce_fusion
  302.3 0.1 div.25
  302.4 2.0 copy.44
  304.4 0.1 rsqrt.31
  304.5 5.8 %reshape.160 = f32[64,16,800]{2,1,0:T(8,128)} reshape(f32[4,16,2,2,3200]{4,3,2,1,0:T(2,128)} %bitcast.51) | data formatting | bytes 6553600 | tf_op jit(solution)/shard_map/reshape | solution.py:312
  310.3 2.7 add_convert_fusion.1
  313.0 1.7 copy.28
  314.7 7.8 %all-to-all-start = ((bf16[64,16,800]{2,0,1:T(8,128)(2,1)}), bf16[64,16,800]{2,0,1:T(8,128)(2,1)S(1)}, u32[]{:S(2)}, u32[]{:S(2)}) async-start(bf16[64,16,800]{2,0,1:T(8,128)(2,1)} %copy.28), calls=%async_computation | async-start | bytes 3670016 | tf_op jit(solution)/shard_map/all_to_all | solution.py:326
  322.5 0.0 reduce-scatter.2.cloned.1.call-start
  322.6 0.5 broadcast.126
  323.1 0.7 reduce.9
  323.8 0.1 reshape_squeeze.16
  323.9 0.1 fusion.29
  324.0 0.1 mul.116
  324.1 0.6 dynamic_slice.3
  324.7 0.6 compare_convert_fusion
  325.3 0.1 broadcast_multiply_fusion
  325.4 22.5 %all-to-all-done = bf16[64,16,800]{2,0,1:T(8,128)(2,1)S(1)} async-done(((bf16[64,16,800]{2,0,1:T(8,128)(2,1)}), bf16[64,16,800]{2,0,1:T(8,128)(2,1)S(1)}, u32[]{:S(2)}, u32[]{:S(2)}) %all-to-all-start) | async-done | bytes 1638432 | tf_op jit(solution)/shard_map/all_to_all | solution.py:326
  347.9 1.3 fusion.10
  349.2 19.2 %add_convert_fusion = bf16[16,64,6144]{2,1,0:T(8,128)(2,1)} fusion(f32[16,64]{1,0:T(8,128)S(1)} %broadcast_multiply_fusion, bf16[800,6144]{1,0:T(8,128)(2,1)} %param.23, bf16[16,64,800]{2,0,1:T(8,128)(2,1)S(1)} %fusion.10), kind=kOutput, calls=%fused_computation | convolution fusion | flops 10078912512 | bytes 24055808 | tf_op jit(solution)/shard_map/dot_general | solution.py:337
  368.4 0.0 reduce-scatter.2.cloned.1.call-update
  368.4 97.5 %reduce-scatter.2.cloned.1.call-done = bf16[64,6144]{1,0:T(8,128)(2,1)} async-done(((bf16[1024,6144]{1,0:T(8,128)(2,1)}), bf16[64,6144]{1,0:T(8,128)(2,1)}) %reduce-scatter.2.cloned.1.call-update) | async-done | bytes 786448 | tf_op jit(solution)/shard_map/reduce_scatter | solution.py:343
  465.9 5.2 %fusion.26 = bf16[1,64,6144]{2,1,0:T(8,128)(2,1)} fusion(bf16[64,6144]{1,0:T(8,128)(2,1)} %reduce-scatter.2.cloned.1.call-done, f32[6144]{0:T(1024)S(1)} %copy-done.5), kind=kLoop, calls=%fused_computation.41 | loop fusion | flops 26345472 | bytes 1597440 | tf_op jit(solution)/shard_map/broadcast_in_dim | solution.py:350
  (29 shorter events, 0.1 us)
Async XLA Ops:
  6.5 2.0 copy-start.1
  6.5 211.8 %all-gather.2.cloned.1.call-start = ((), (), s32[]{:S(2)}) async-start(), calls=%async_computation.2 | async-start | bytes 14745600 | tf_op jit(solution)/shard_map/all_gather | solution.py:262
  8.5 11.6 %copy-start.7 = (f32[2,256]{1,0:T(2,128)S(1)}, f32[2,256]{1,0:T(2,128)}, u32[]{:S(2)}) copy-start(f32[2,256]{1,0:T(2,128)} %param.16) | copy-start | bytes 6148
  10.9 1.4 copy-start.2
  10.9 10.8 %copy-start.6 = (f32[3200]{0:T(1024)S(1)}, f32[3200]{0:T(1024)}, u32[]{:S(2)}) copy-start(f32[3200]{0:T(1024)} %param.18) | copy-start | bytes 38404
  10.9 11.4 %copy-start.3 = (f32[12800]{0:T(1024)S(1)}, f32[12800]{0:T(1024)}, u32[]{:S(2)}) copy-start(f32[12800]{0:T(1024)} %param.22) | copy-start | bytes 153604
  10.9 11.5 %copy-start.4 = (f32[12800]{0:T(1024)S(1)}, f32[12800]{0:T(1024)}, u32[]{:S(2)}) copy-start(f32[12800]{0:T(1024)} %param.21) | copy-start | bytes 153604
  12.3 61.6 %collective-permute-start = (bf16[256,3200]{1,0:T(8,128)(2,1)S(1)}, bf16[256,3200]{1,0:T(8,128)(2,1)}, u32[]{:S(2)}, u32[]{:S(2)}) collective-permute-start(bf16[256,3200]{1,0:T(8,128)(2,1)S(1)} %copy-done.2), channel_id=1, source_target_pairs={{0,1},{1,2},{2,3},{3,4},{4,5},{5,6},{6,7},{7,0},{8,9},{9,10},{10,1... | collective-permute-start | bytes 4915208 | tf_op jit(solution)/shard_map/ppermute | solution.py:297
  14.9 122.8 %collective-permute-start.1 = (bf16[256,3200]{1,0:T(8,128)(2,1)S(1)}, bf16[256,3200]{1,0:T(8,128)(2,1)}, u32[]{:S(2)}, u32[]{:S(2)}) collective-permute-start(bf16[256,3200]{1,0:T(8,128)(2,1)S(1)} %copy-done.2), channel_id=1, source_target_pairs={{0,2},{1,3},{2,4},{3,5},{4,6},{5,7},{6,0},{7,1},{8,10},{9,11},{10,... | collective-permute-start | bytes 4915208 | tf_op jit(solution)/shard_map/ppermute | solution.py:297
  16.1 156.8 %collective-permute-start.2 = (bf16[256,3200]{1,0:T(8,128)(2,1)S(1)}, bf16[256,3200]{1,0:T(8,128)(2,1)}, u32[]{:S(2)}, u32[]{:S(2)}) collective-permute-start(bf16[256,3200]{1,0:T(8,128)(2,1)S(1)} %copy-done.2), channel_id=1, source_target_pairs={{0,3},{1,4},{2,5},{3,6},{4,7},{5,0},{6,1},{7,2},{8,11},{9,12},{10,... | collective-permute-start | bytes 4915208 | tf_op jit(solution)/shard_map/ppermute | solution.py:297
  17.7 193.4 %collective-permute-start.3 = (bf16[256,3200]{1,0:T(8,128)(2,1)S(1)}, bf16[256,3200]{1,0:T(8,128)(2,1)}, u32[]{:S(2)}, u32[]{:S(2)}) collective-permute-start(bf16[256,3200]{1,0:T(8,128)(2,1)S(1)} %copy-done.2), channel_id=1, source_target_pairs={{0,4},{1,5},{2,6},{3,7},{4,0},{5,1},{6,2},{7,3},{8,12},{9,13},{10,... | collective-permute-start | bytes 4915208 | tf_op jit(solution)/shard_map/ppermute | solution.py:297
  18.2 195.6 %collective-permute-start.4 = (bf16[256,3200]{1,0:T(8,128)(2,1)S(1)}, bf16[256,3200]{1,0:T(8,128)(2,1)S(1)}, u32[]{:S(2)}, u32[]{:S(2)}) collective-permute-start(bf16[256,3200]{1,0:T(8,128)(2,1)S(1)} %copy-done.2), channel_id=1, source_target_pairs={{0,5},{1,6},{2,7},{3,0},{4,1},{5,2},{6,3},{7,4},{8,13},{9,14},{10,... | collective-permute-start | bytes 4915208 | tf_op jit(solution)/shard_map/ppermute | solution.py:297
  22.5 1.3 copy-start.8
  73.9 141.2 %collective-permute-start.5 = (bf16[256,3200]{1,0:T(8,128)(2,1)S(1)}, bf16[256,3200]{1,0:T(8,128)(2,1)S(1)}, u32[]{:S(2)}, u32[]{:S(2)}) collective-permute-start(bf16[256,3200]{1,0:T(8,128)(2,1)S(1)} %copy-done.2), channel_id=1, source_target_pairs={{0,6},{1,7},{2,0},{3,1},{4,2},{5,3},{6,4},{7,5},{8,14},{9,15},{10,... | collective-permute-start | bytes 4915208 | tf_op jit(solution)/shard_map/ppermute | solution.py:297
  137.8 78.6 %collective-permute-start.6 = (bf16[256,3200]{1,0:T(8,128)(2,1)S(1)}, bf16[256,3200]{1,0:T(8,128)(2,1)S(1)}, u32[]{:S(2)}, u32[]{:S(2)}) collective-permute-start(bf16[256,3200]{1,0:T(8,128)(2,1)S(1)} %copy-done.2), channel_id=1, source_target_pairs={{0,7},{1,0},{2,1},{3,2},{4,3},{5,4},{6,5},{7,6},{8,15},{9,8},{10,9... | collective-permute-start | bytes 4915208 | tf_op jit(solution)/shard_map/ppermute | solution.py:297
  234.0 2.6 copy-start
  314.7 8.4 %copy-start.9 = (s32[1,256]{1,0:T(1,128)S(1)}, s32[1,256]{1,0:T(1,128)}, u32[]{:S(2)}) copy-start(s32[1,256]{1,0:T(1,128)} %param.20) | copy-start | bytes 3076
  314.7 9.4 %copy-start.10 = (s32[16]{0:T(128)S(1)}, s32[16]{0:T(128)}, u32[]{:S(2)}) copy-start(s32[16]{0:T(128)} %param.25) | copy-start | bytes 196
  314.7 33.2 %all-to-all-start = ((bf16[64,16,800]{2,0,1:T(8,128)(2,1)}), bf16[64,16,800]{2,0,1:T(8,128)(2,1)S(1)}, u32[]{:S(2)}, u32[]{:S(2)}) async-start(bf16[64,16,800]{2,0,1:T(8,128)(2,1)} %copy.28), calls=%async_computation | async-start | bytes 3670016 | tf_op jit(solution)/shard_map/all_to_all | solution.py:326
  322.5 143.4 %reduce-scatter.2.cloned.1.call-start = ((), (), s32[]{:S(2)}) async-start(), calls=%async_computation.3 | async-start | bytes 13369344 | tf_op jit(solution)/shard_map/reduce_scatter | solution.py:343
  368.4 97.5 %copy-start.5 = (f32[6144]{0:T(1024)S(1)}, f32[6144]{0:T(1024)}, u32[]{:S(2)}) copy-start(f32[6144]{0:T(1024)} %param.24) | copy-start | bytes 73732
Sparse Core Ops, SparseCore 0:
  11.0 207.2 all-gather.1
  368.5 97.3 reduce-scatter.1

commit v6 on v4

--- a/solution.py
+++ b/solution.py
@@ -289,18 +289,25 @@
         scale,
     )
     full_out_weight = lax.all_gather(out_weight, "seq", axis=0, tiled=False)
-    hidden = out_proj(
-        attended,
-        full_out_weight.reshape(seq_count, heads_here, HEAD_DIM, -1),
-        residual_in[0],
-        layer_scale,
-    )
     half_grid = GRID // 2
     lines = shard_rows // (2 * GRID)
     merged_count = shard_rows // 4
-    merged = jnp.transpose(hidden.reshape(lines, 2, half_grid, 2, D), (0, 2, 1, 3, 4)).reshape(
-        merged_count, 4 * D
-    )
+
+    def shuffle_rows(x, axis):
+        shape = x.shape
+        split = shape[:axis] + (lines, 2, half_grid, 2) + shape[axis + 1:]
+        order = list(range(axis)) + [axis, axis + 2, axis + 1, axis + 3] + list(
+            range(axis + 4, len(split))
+        )
+        return jnp.transpose(x.reshape(split), order).reshape(shape)
+
+    hidden = out_proj(
+        shuffle_rows(attended, 2),
+        full_out_weight.reshape(seq_count, heads_here, HEAD_DIM, -1),
+        shuffle_rows(residual_in[0], 0),
+        layer_scale,
+    )
+    merged = hidden.reshape(merged_count, 4 * D)
     centre = merged - jnp.mean(merged, axis=-1, keepdims=True)
     spread = jnp.mean(centre * centre, axis=-1, keepdims=True)
     merged_norm = (centre * lax.rsqrt(spread + 1e-05) * ln_weight + ln_bias).astype(jnp.bfloat16)

time: 361 us -> 353 us (0.978)
  waiting for transfers between devices: 202 us -> 196 us
    reshape x3, local copies, waits for them, and re-layouts: 11.8 us -> 7.84 us  [the longest x2 4.66 us: shuffle_rows(): return jnp.transpose(x.reshape(split), order).reshape(shape)]
  transfers between devices with their start and end apart: 4 -> 4, of which waited for: 4 -> 4; matrix products, arithmetic and copies ran while one was open for 7% -> 9% of each run, Pallas kernels for 14% -> 14%
where the time goes in v6:
time: 353 us
  waiting for transfers between devices  196 us (56%)
  Pallas kernels  61.1 us (17%)
  matrix products  36.2 us (10%)
  other arithmetic  21.3 us (6%)
  local copies, waits for them, and re-layouts  18.3 us (5%)
  between operations  13.3 us (4%)
  starting transfers between devices  6.91 us (2%)
    reduce_scatter x1, waiting for transfers between devices, per_device(): lax.psum_scatter(partial.reshape(row_count * merged_count, -1), 'rows', s...  93.5 us
    all_gather x1, waiting for transfers between devices, per_device(): row_tokens = lax.all_gather(normed, 'seq', axis=0, tiled=True)  66.7 us
    pallas_call x1, Pallas kernels, attend_kernel(): pl.pallas_call(functools.partial(attention_kernel, scale), out_shape=jax....  37.5 us
    all_to_all x1, waiting for transfers between devices, per_device(): lax.all_to_all(merged_norm, 'rows', split_axis=1, concat_axis=0, tiled=True)  23.4 us
    dot_general x1, matrix products, per_device(): jnp.dot(ordered, fc_weight, preferred_element_type=jnp.float32)  19.2 us
    dot_general x1, matrix products, per_device(): jnp.dot(row_tokens, qkv_weight, preferred_element_type=jnp.float32)  15.7 us
    pallas_call x1, Pallas kernels, out_proj(): pl.pallas_call(out_proj_kernel, out_shape=jax.ShapeDtypeStruct((tokens, w...  12 us
    pallas_call x1, Pallas kernels, seq_sum(): pl.pallas_call(seq_sum_kernel, out_shape=jax.ShapeDtypeStruct(part.shape,...  11.6 us
  transfers between devices with their start and end apart: 4, of which 4 were waited for; matrix products, arithmetic and copies ran while one was open for 9% of the time, Pallas kernels for 14%

profile of v6, /device:TPU:1, one launch (start us, length us, event | category | flops | bytes accessed | tf_op | source)
XLA Modules:
  0.0 352.7 jit_solution(17827351611982268752)
XLA Ops:
  6.5 0.0 all-gather.4.cloned.1.call-start
  6.5 2.0 fusion.5
  8.5 0.0 copy-done.2
  8.5 2.4 fusion.7
  10.9 0.0 all-gather.4.cloned.1.call-update
  10.9 0.0 all-gather.6.cloned.1.call-start
  11.0 0.7 all-gather.6.cloned.1.call-update
  11.7 0.0 copy-start.7
  11.7 0.7 reshape_squeeze.19
  12.4 0.0 copy-done.7
  12.4 0.8 copy.28.qg_ref
  13.2 0.8 copy.29.kg_ref
  14.0 1.1 copy.54
  15.1 0.0 copy-start.6
  15.1 0.0 copy-start.3
  15.1 0.0 copy-start.4
  15.1 0.0 copy-start.8
  15.1 1.6 reshape.138.res_ref
  16.7 0.0 copy-done.6
  16.7 0.6 reshape.139.ls_ref
  17.3 0.0 copy-done.3
  17.3 0.1 add.78
  17.4 0.0 copy-done.4
  17.4 0.1 mul.110
  17.5 0.0 copy-done.8
  17.6 66.7 %all-gather.4.cloned.1.call-done = bf16[2048,3200]{1,0:T(8,128)(2,1)} async-done(((bf16[256,3200]{1,0:T(8,128)(2,1)}), bf16[2048,3200]{1,0:T(8,128)(2,1)}) %all-gather.4.cloned.1.call-update) | async-done | bytes 13107216 | tf_op jit(solution)/shard_map/all_gather | solution.py:259
  84.2 15.7 %fusion.38 = f32[2048,768]{0,1:T(8,128)S(1)} fusion(bf16[2048,3200]{1,0:T(8,128)(2,1)} %all-gather.4.cloned.1.call-done, bf16[3200,768]{1,0:T(8,128)(2,1)} %param.15), kind=kOutput, calls=%fused_computation.66 | convolution fusion | flops 10066329600 | bytes 24313856 | tf_op jit(solution)/shard_map/dot_general | solution.py:262
  99.9 2.6 copy-done
  102.5 0.4 fusion.9
  102.9 0.6 pad_maximum_fusion.part_ref
  103.5 11.6 %shard_map.127 = f32[3,2048]{1,0:T(4,128)} custom-call(f32[3,2048]{1,0:T(4,128)} %pad_maximum_fusion.part_ref), custom_call_target="tpu_custom_call" | custom-call | tf_op jit(solution)/shard_map/pallas_call | solution.py:61
  115.2 1.5 fusion.37
  116.7 1.3 copy.30.qseg_ref
  118.0 37.5 %shard_map.128 = bf16[8,2,256,128]{3,2,1,0:T(8,128)(2,1)} custom-call(f32[768,2048]{1,0:T(8,128)} %bitcast.41, f32[768,2048]{1,0:T(8,128)} %bitcast.42, f32[768,2048]{1,0:T(8,128)} %bitcast.43, f32[1,2048]{1,0:T(1,128)} %get-tuple-element.10.qrs_ref, f32[1,2048]{1,0:T(1,128)} %get-tuple-element.9.krs_ref, f32[256,1]{1,0:T(8,128)} %copy.28.qg_ref, ...), custom_call_target="tpu_custom_call" | custom-call | flops 4294967296 | bytes 6291456 | tf_op jit(solution)/shard_map/pallas_call | solution.py:164
  155.5 3.1 copy.31
  158.6 11.3 %all-gather.6.cloned.1.call-done = bf16[2048,3200]{1,0:T(8,128)(2,1)} async-done(((bf16[256,3200]{1,0:T(8,128)(2,1)}), bf16[2048,3200]{1,0:T(8,128)(2,1)}) %all-gather.6.cloned.1.call-update) | async-done | bytes 13107216 | tf_op jit(solution)/shard_map/all_gather | solution.py:291
  169.9 12.0 %shard_map.129 = f32[256,3200]{1,0:T(8,128)} custom-call(bf16[8,2,256,128]{3,2,1,0:T(8,128)(2,1)} %bitcast.48, bf16[8,2,128,3200]{3,2,1,0:T(8,128)(2,1)} %bitcast.44, bf16[256,3200]{1,0:T(8,128)(2,1)} %reshape.138.res_ref, f32[1,3200]{1,0:T(1,128)} %reshape.139.ls_ref), custom_call_target="tpu_custom_call" | custom-call | flops 3355443200 | bytes 18022400 | tf_op jit(solution)/shard_map/pallas_call | solution.py:218
  181.8 2.3 reduce_sum.62
  184.1 0.6 copy-done.1
  184.7 3.2 reshape.140
  187.9 0.1 reduce_sum.63
  188.0 0.1 reduce_sum.64
  188.1 0.1 sub.24
  188.2 0.1 sub.25
  188.3 0.5 multiply_reduce_fusion
  188.8 0.1 reduce_sum.66
  188.9 0.1 reduce_sum.67
  189.1 4.7 %fusion.4 = bf16[64,16,800]{2,0,1:T(8,128)(2,1)} fusion(f32[64,16,800]{2,1,0:T(8,128)} %reshape.140, f32[16,800]{1,0:T(8,128)S(1)} %add.78, f32[16,800]{1,0:T(8,128)S(1)} %mul.110, f32[64]{0:T(128)S(1)} %add_rsqrt_fusion.3, f32[64]{0:T(128)S(1)} %broadcast_multiply_fusion.1), kind=kLoop, calls=%fused_computation.8 | loop fusion | flops 4096000 | bytes 5018112 | tf_op jit(solution)/shard_map/convert_element_type | solution.py:313
  193.7 6.8 %all-to-all-start = ((bf16[64,16,800]{2,0,1:T(8,128)(2,1)}), bf16[64,16,800]{2,0,1:T(8,128)(2,1)S(1)}, u32[]{:S(2)}, u32[]{:S(2)}) async-start(bf16[64,16,800]{2,0,1:T(8,128)(2,1)} %fusion.4), calls=%async_computation | async-start | bytes 3670016 | tf_op jit(solution)/shard_map/all_to_all | solution.py:322
  200.6 0.0 reduce-scatter.2.cloned.1.call-start
  200.6 0.5 broadcast.118
  201.1 0.7 reduce.11
  201.8 0.1 reshape_squeeze.20
  201.9 0.1 fusion.33
  202.0 0.1 mul.116
  202.1 0.6 dynamic_slice.3
  202.7 0.6 compare_convert_fusion
  203.4 0.1 broadcast_multiply_fusion
  203.4 23.4 %all-to-all-done = bf16[64,16,800]{2,0,1:T(8,128)(2,1)S(1)} async-done(((bf16[64,16,800]{2,0,1:T(8,128)(2,1)}), bf16[64,16,800]{2,0,1:T(8,128)(2,1)S(1)}, u32[]{:S(2)}, u32[]{:S(2)}) %all-to-all-start) | async-done | bytes 1638432 | tf_op jit(solution)/shard_map/all_to_all | solution.py:322
  226.9 1.3 fusion.14
  228.1 19.2 %add_convert_fusion = bf16[16,64,6144]{2,1,0:T(8,128)(2,1)} fusion(f32[16,64]{1,0:T(8,128)S(1)} %broadcast_multiply_fusion, bf16[800,6144]{1,0:T(8,128)(2,1)} %param.23, bf16[16,64,800]{2,0,1:T(8,128)(2,1)S(1)} %fusion.14), kind=kOutput, calls=%fused_computation | convolution fusion | flops 10078912512 | bytes 24055808 | tf_op jit(solution)/shard_map/dot_general | solution.py:333
  247.4 0.0 reduce-scatter.2.cloned.1.call-update
  247.4 93.5 %reduce-scatter.2.cloned.1.call-done = bf16[64,6144]{1,0:T(8,128)(2,1)} async-done(((bf16[1024,6144]{1,0:T(8,128)(2,1)}), bf16[64,6144]{1,0:T(8,128)(2,1)}) %reduce-scatter.2.cloned.1.call-update) | async-done | bytes 786448 | tf_op jit(solution)/shard_map/reduce_scatter | solution.py:339
  341.0 5.2 %fusion.30 = bf16[1,64,6144]{2,1,0:T(8,128)(2,1)} fusion(bf16[64,6144]{1,0:T(8,128)(2,1)} %reduce-scatter.2.cloned.1.call-done, f32[6144]{0:T(1024)S(1)} %copy-done.5), kind=kLoop, calls=%fused_computation.45 | loop fusion | flops 26345472 | bytes 1597440 | tf_op jit(solution)/shard_map/broadcast_in_dim | solution.py:346
  (15 shorter events, 0.1 us)
Async XLA Ops:
  6.5 2.0 copy-start.2
  6.5 77.7 %all-gather.4.cloned.1.call-start = ((), (), s32[]{:S(2)}) async-start(), calls=%async_computation.2 | async-start | bytes 14745600 | tf_op jit(solution)/shard_map/all_gather | solution.py:259
  10.9 159.0 %all-gather.6.cloned.1.call-start = ((), (), s32[]{:S(2)}) async-start(), calls=%async_computation.4 | async-start | bytes 14745600 | tf_op jit(solution)/shard_map/all_gather | solution.py:291
  11.7 0.7 copy-start.7
  15.1 1.6 copy-start.6
  15.1 2.2 copy-start.3
  15.1 2.3 copy-start.4
  15.1 2.4 copy-start.8
  99.9 2.6 copy-start
  181.8 2.9 copy-start.1
  193.7 7.4 %copy-start.9 = (s32[1,256]{1,0:T(1,128)S(1)}, s32[1,256]{1,0:T(1,128)}, u32[]{:S(2)}) copy-start(s32[1,256]{1,0:T(1,128)} %param.20) | copy-start | bytes 3076
  193.7 8.4 %copy-start.10 = (s32[16]{0:T(128)S(1)}, s32[16]{0:T(128)}, u32[]{:S(2)}) copy-start(s32[16]{0:T(128)} %param.25) | copy-start | bytes 196
  193.7 33.1 %all-to-all-start = ((bf16[64,16,800]{2,0,1:T(8,128)(2,1)}), bf16[64,16,800]{2,0,1:T(8,128)(2,1)S(1)}, u32[]{:S(2)}, u32[]{:S(2)}) async-start(bf16[64,16,800]{2,0,1:T(8,128)(2,1)} %fusion.4), calls=%async_computation | async-start | bytes 3670016 | tf_op jit(solution)/shard_map/all_to_all | solution.py:322
  200.6 140.4 %reduce-scatter.2.cloned.1.call-start = ((), (), s32[]{:S(2)}) async-start(), calls=%async_computation.3 | async-start | bytes 13369344 | tf_op jit(solution)/shard_map/reduce_scatter | solution.py:339
  247.4 93.6 %copy-start.5 = (f32[6144]{0:T(1024)S(1)}, f32[6144]{0:T(1024)}, u32[]{:S(2)}) copy-start(f32[6144]{0:T(1024)} %param.24) | copy-start | bytes 73732
Sparse Core Ops, SparseCore 0:
  11.0 73.1 all-gather.3
  85.9 83.9 all-gather.5
  247.5 93.3 reduce-scatter.1

commit v7 on v6

--- a/solution.py
+++ b/solution.py
@@ -95,20 +95,27 @@
         )
         value_half[...] = jnp.transpose(v_ref[...].astype(jnp.bfloat16))
 
-    query_norm = jnp.transpose((q_ref[...] * qrs_ref[...] * qg_ref[...]).astype(jnp.bfloat16))
+    dest = lax.rem(me + 1 + block, blocks)
+    width = slots.shape[1]
+    start = pl.multiple_of(dest * width, width)
+    query_norm = jnp.transpose(
+        (q_ref[:, pl.ds(start, width)] * qrs_ref[:, pl.ds(start, width)] * qg_ref[...]).astype(
+            jnp.bfloat16
+        )
+    )
     scores = (
         lax.dot_general(
             query_norm, key_norm[...], (((1,), (1,)), ((), ())), preferred_element_type=jnp.float32
         )
         * scale
     )
-    scores = jnp.where(qseg_ref[...] == kseg_ref[...], scores, -1e30)
+    scores = jnp.where(qseg_ref[pl.ds(start, width), :] == kseg_ref[...], scores, -1e30)
     peak_val = jnp.max(scores, axis=-1, keepdims=True)
     exp_terms = jnp.exp(scores - peak_val)
     total = jnp.sum(exp_terms, axis=-1, keepdims=True)
     probs = (exp_terms / total).astype(jnp.bfloat16)
     step = head * blocks + block
-    slots[step] = jnp.dot(probs, value_half[...], preferred_element_type=jnp.float32).astype(
+    slots[head * blocks + dest] = jnp.dot(probs, value_half[...], preferred_element_type=jnp.float32).astype(
         slots.dtype
     )
 
@@ -127,11 +134,11 @@
             slots.at[h * blocks + me], landing.at[me, h], local_sem.at[h]
         )
 
-    @pl.when(block != me)
-    def _():
-        remote(head, block).start()
-
-    @pl.when(block == me)
+    @pl.when(dest != me)
+    def _():
+        remote(head, dest).start()
+
+    @pl.when(dest == me)
     def _():
         local(head).start()
 
@@ -166,14 +173,14 @@
         out_shape=jax.ShapeDtypeStruct((blocks, heads_here, block_len, HEAD_DIM), jnp.bfloat16),
         grid=(heads_here, blocks),
         in_specs=[
-            pl.BlockSpec((HEAD_DIM, block_len), lambda h, i: (3 * h, i)),
+            pl.BlockSpec((HEAD_DIM, length), lambda h, i: (3 * h, 0)),
             pl.BlockSpec((HEAD_DIM, length), lambda h, i: (3 * h + 1, 0)),
             pl.BlockSpec((HEAD_DIM, length), lambda h, i: (3 * h + 2, 0)),
-            pl.BlockSpec((1, block_len), lambda h, i: (0, i)),
+            pl.BlockSpec((1, length), lambda h, i: (0, 0)),
             pl.BlockSpec((1, length), lambda h, i: (0, 0)),
             gain_block,
             gain_block,
-            pl.BlockSpec((block_len, 1), lambda h, i: (i, 0)),
+            pl.BlockSpec((length, 1), lambda h, i: (0, 0)),
             pl.BlockSpec((1, length), lambda h, i: (0, 0)),
         ],
         out_specs=pl.BlockSpec(memory_space=pltpu.VMEM),

time: 353 us -> 353 us (level)
  no operation moved by 1% of the time
where the time goes in v7:
time: 353 us
  waiting for transfers between devices  196 us (56%)
  Pallas kernels  60.6 us (17%)
  matrix products  36.2 us (10%)
  other arithmetic  21.3 us (6%)
  local copies, waits for them, and re-layouts  18.3 us (5%)
  between operations  13.3 us (4%)
  starting transfers between devices  6.91 us (2%)
    reduce_scatter x1, waiting for transfers between devices, per_device(): lax.psum_scatter(partial.reshape(row_count * merged_count, -1), 'rows', s...  93.5 us
    all_gather x1, waiting for transfers between devices, per_device(): row_tokens = lax.all_gather(normed, 'seq', axis=0, tiled=True)  66.7 us
    pallas_call x1, Pallas kernels, attend_kernel(): pl.pallas_call(functools.partial(attention_kernel, scale), out_shape=jax....  37 us
    all_to_all x1, waiting for transfers between devices, per_device(): lax.all_to_all(merged_norm, 'rows', split_axis=1, concat_axis=0, tiled=True)  23.4 us
    dot_general x1, matrix products, per_device(): jnp.dot(ordered, fc_weight, preferred_element_type=jnp.float32)  19.2 us
    dot_general x1, matrix products, per_device(): jnp.dot(row_tokens, qkv_weight, preferred_element_type=jnp.float32)  15.7 us
    pallas_call x1, Pallas kernels, out_proj(): pl.pallas_call(out_proj_kernel, out_shape=jax.ShapeDtypeStruct((tokens, w...  12 us
    all_gather x1, waiting for transfers between devices, per_device(): full_out_weight = lax.all_gather(out_weight, 'seq', axis=0, tiled=False)  11.7 us
  transfers between devices with their start and end apart: 4, of which 4 were waited for; matrix products, arithmetic and copies ran while one was open for 9% of the time, Pallas kernels for 14%

profile of v7, /device:TPU:1, one launch (start us, length us, event | category | flops | bytes accessed | tf_op | source)
XLA Modules:
  0.0 352.7 jit_solution(16168267127258722584)
XLA Ops:
  6.5 0.0 all-gather.4.cloned.1.call-start
  6.5 2.0 fusion.5
  8.5 0.0 copy-done.2
  8.5 2.4 fusion.7
  10.9 0.0 all-gather.4.cloned.1.call-update
  10.9 0.0 all-gather.6.cloned.1.call-start
  11.0 0.7 all-gather.6.cloned.1.call-update
  11.7 0.0 copy-start.7
  11.7 0.7 reshape_squeeze.19
  12.4 0.0 copy-done.7
  12.4 0.8 copy.28.qg_ref
  13.2 0.8 copy.29.kg_ref
  14.0 1.1 copy.54
  15.1 0.0 copy-start.6
  15.1 0.0 copy-start.3
  15.1 0.0 copy-start.4
  15.1 0.0 copy-start.8
  15.1 1.6 reshape.138.res_ref
  16.7 0.0 copy-done.6
  16.7 0.6 reshape.139.ls_ref
  17.3 0.0 copy-done.3
  17.3 0.1 add.78
  17.4 0.0 copy-done.4
  17.4 0.1 mul.110
  17.5 0.0 copy-done.8
  17.6 66.7 %all-gather.4.cloned.1.call-done = bf16[2048,3200]{1,0:T(8,128)(2,1)} async-done(((bf16[256,3200]{1,0:T(8,128)(2,1)}), bf16[2048,3200]{1,0:T(8,128)(2,1)}) %all-gather.4.cloned.1.call-update) | async-done | bytes 13107216 | tf_op jit(solution)/shard_map/all_gather | solution.py:266
  84.2 15.7 %fusion.38 = f32[2048,768]{0,1:T(8,128)S(1)} fusion(bf16[2048,3200]{1,0:T(8,128)(2,1)} %all-gather.4.cloned.1.call-done, bf16[3200,768]{1,0:T(8,128)(2,1)} %param.15), kind=kOutput, calls=%fused_computation.66 | convolution fusion | flops 10066329600 | bytes 24313856 | tf_op jit(solution)/shard_map/dot_general | solution.py:269
  99.9 2.6 copy-done
  102.5 0.4 fusion.9
  102.9 0.6 pad_maximum_fusion.part_ref
  103.5 11.6 %shard_map.127 = f32[3,2048]{1,0:T(4,128)} custom-call(f32[3,2048]{1,0:T(4,128)} %pad_maximum_fusion.part_ref), custom_call_target="tpu_custom_call" | custom-call | tf_op jit(solution)/shard_map/pallas_call | solution.py:61
  115.2 1.5 fusion.37
  116.7 1.3 copy.30.qseg_ref
  118.0 37.0 %shard_map.128 = bf16[8,2,256,128]{3,2,1,0:T(8,128)(2,1)} custom-call(f32[768,2048]{1,0:T(8,128)} %bitcast.41, f32[768,2048]{1,0:T(8,128)} %bitcast.42, f32[768,2048]{1,0:T(8,128)} %bitcast.43, f32[1,2048]{1,0:T(1,128)} %get-tuple-element.10.qrs_ref, f32[1,2048]{1,0:T(1,128)} %get-tuple-element.9.krs_ref, f32[256,1]{1,0:T(8,128)} %copy.28.qg_ref, ...), custom_call_target="tpu_custom_call" | custom-call | flops 4294967296 | bytes 6291456 | tf_op jit(solution)/shard_map/pallas_call | solution.py:171
  155.0 3.1 copy.31
  158.1 11.7 %all-gather.6.cloned.1.call-done = bf16[2048,3200]{1,0:T(8,128)(2,1)} async-done(((bf16[256,3200]{1,0:T(8,128)(2,1)}), bf16[2048,3200]{1,0:T(8,128)(2,1)}) %all-gather.6.cloned.1.call-update) | async-done | bytes 13107216 | tf_op jit(solution)/shard_map/all_gather | solution.py:298
  169.9 12.0 %shard_map.129 = f32[256,3200]{1,0:T(8,128)} custom-call(bf16[8,2,256,128]{3,2,1,0:T(8,128)(2,1)} %bitcast.48, bf16[8,2,128,3200]{3,2,1,0:T(8,128)(2,1)} %bitcast.44, bf16[256,3200]{1,0:T(8,128)(2,1)} %reshape.138.res_ref, f32[1,3200]{1,0:T(1,128)} %reshape.139.ls_ref), custom_call_target="tpu_custom_call" | custom-call | flops 3355443200 | bytes 18022400 | tf_op jit(solution)/shard_map/pallas_call | solution.py:225
  181.8 2.3 reduce_sum.62
  184.1 0.6 copy-done.1
  184.7 3.2 reshape.140
  187.9 0.1 reduce_sum.63
  188.0 0.1 reduce_sum.64
  188.1 0.1 sub.24
  188.2 0.1 sub.25
  188.3 0.5 multiply_reduce_fusion
  188.8 0.1 reduce_sum.66
  188.9 0.1 reduce_sum.67
  189.1 4.7 %fusion.4 = bf16[64,16,800]{2,0,1:T(8,128)(2,1)} fusion(f32[64,16,800]{2,1,0:T(8,128)} %reshape.140, f32[16,800]{1,0:T(8,128)S(1)} %add.78, f32[16,800]{1,0:T(8,128)S(1)} %mul.110, f32[64]{0:T(128)S(1)} %add_rsqrt_fusion.3, f32[64]{0:T(128)S(1)} %broadcast_multiply_fusion.1), kind=kLoop, calls=%fused_computation.8 | loop fusion | flops 4096000 | bytes 5018112 | tf_op jit(solution)/shard_map/convert_element_type | solution.py:320
  193.7 6.8 %all-to-all-start = ((bf16[64,16,800]{2,0,1:T(8,128)(2,1)}), bf16[64,16,800]{2,0,1:T(8,128)(2,1)S(1)}, u32[]{:S(2)}, u32[]{:S(2)}) async-start(bf16[64,16,800]{2,0,1:T(8,128)(2,1)} %fusion.4), calls=%async_computation | async-start | bytes 3670016 | tf_op jit(solution)/shard_map/all_to_all | solution.py:329
  200.6 0.0 reduce-scatter.2.cloned.1.call-start
  200.6 0.5 broadcast.118
  201.1 0.7 reduce.11
  201.8 0.1 reshape_squeeze.20
  201.9 0.1 fusion.33
  202.0 0.1 mul.116
  202.1 0.6 dynamic_slice.3
  202.7 0.6 compare_convert_fusion
  203.4 0.1 broadcast_multiply_fusion
  203.4 23.4 %all-to-all-done = bf16[64,16,800]{2,0,1:T(8,128)(2,1)S(1)} async-done(((bf16[64,16,800]{2,0,1:T(8,128)(2,1)}), bf16[64,16,800]{2,0,1:T(8,128)(2,1)S(1)}, u32[]{:S(2)}, u32[]{:S(2)}) %all-to-all-start) | async-done | bytes 1638432 | tf_op jit(solution)/shard_map/all_to_all | solution.py:329
  226.9 1.3 fusion.14
  228.1 19.2 %add_convert_fusion = bf16[16,64,6144]{2,1,0:T(8,128)(2,1)} fusion(f32[16,64]{1,0:T(8,128)S(1)} %broadcast_multiply_fusion, bf16[800,6144]{1,0:T(8,128)(2,1)} %param.23, bf16[16,64,800]{2,0,1:T(8,128)(2,1)S(1)} %fusion.14), kind=kOutput, calls=%fused_computation | convolution fusion | flops 10078912512 | bytes 24055808 | tf_op jit(solution)/shard_map/dot_general | solution.py:340
  247.4 0.0 reduce-scatter.2.cloned.1.call-update
  247.4 93.5 %reduce-scatter.2.cloned.1.call-done = bf16[64,6144]{1,0:T(8,128)(2,1)} async-done(((bf16[1024,6144]{1,0:T(8,128)(2,1)}), bf16[64,6144]{1,0:T(8,128)(2,1)}) %reduce-scatter.2.cloned.1.call-update) | async-done | bytes 786448 | tf_op jit(solution)/shard_map/reduce_scatter | solution.py:346
  341.0 5.2 %fusion.30 = bf16[1,64,6144]{2,1,0:T(8,128)(2,1)} fusion(bf16[64,6144]{1,0:T(8,128)(2,1)} %reduce-scatter.2.cloned.1.call-done, f32[6144]{0:T(1024)S(1)} %copy-done.5), kind=kLoop, calls=%fused_computation.45 | loop fusion | flops 26345472 | bytes 1597440 | tf_op jit(solution)/shard_map/broadcast_in_dim | solution.py:353
  (15 shorter events, 0.1 us)
Async XLA Ops:
  6.5 2.0 copy-start.2
  6.5 77.7 %all-gather.4.cloned.1.call-start = ((), (), s32[]{:S(2)}) async-start(), calls=%async_computation.2 | async-start | bytes 14745600 | tf_op jit(solution)/shard_map/all_gather | solution.py:266
  10.9 159.0 %all-gather.6.cloned.1.call-start = ((), (), s32[]{:S(2)}) async-start(), calls=%async_computation.4 | async-start | bytes 14745600 | tf_op jit(solution)/shard_map/all_gather | solution.py:298
  11.7 0.7 copy-start.7
  15.1 1.6 copy-start.6
  15.1 2.2 copy-start.3
  15.1 2.3 copy-start.4
  15.1 2.4 copy-start.8
  99.9 2.6 copy-start
  181.8 2.9 copy-start.1
  193.7 7.4 %copy-start.9 = (s32[1,256]{1,0:T(1,128)S(1)}, s32[1,256]{1,0:T(1,128)}, u32[]{:S(2)}) copy-start(s32[1,256]{1,0:T(1,128)} %param.20) | copy-start | bytes 3076
  193.7 8.4 %copy-start.10 = (s32[16]{0:T(128)S(1)}, s32[16]{0:T(128)}, u32[]{:S(2)}) copy-start(s32[16]{0:T(128)} %param.25) | copy-start | bytes 196
  193.7 33.1 %all-to-all-start = ((bf16[64,16,800]{2,0,1:T(8,128)(2,1)}), bf16[64,16,800]{2,0,1:T(8,128)(2,1)S(1)}, u32[]{:S(2)}, u32[]{:S(2)}) async-start(bf16[64,16,800]{2,0,1:T(8,128)(2,1)} %fusion.4), calls=%async_computation | async-start | bytes 3670016 | tf_op jit(solution)/shard_map/all_to_all | solution.py:329
  200.6 140.4 %reduce-scatter.2.cloned.1.call-start = ((), (), s32[]{:S(2)}) async-start(), calls=%async_computation.3 | async-start | bytes 13369344 | tf_op jit(solution)/shard_map/reduce_scatter | solution.py:346
  247.4 93.6 %copy-start.5 = (f32[6144]{0:T(1024)S(1)}, f32[6144]{0:T(1024)}, u32[]{:S(2)}) copy-start(f32[6144]{0:T(1024)} %param.24) | copy-start | bytes 73732
Sparse Core Ops, SparseCore 0:
  11.0 73.1 all-gather.3
  85.9 83.9 all-gather.5
  247.5 93.3 reduce-scatter.1

commit v8 on v7

--- a/solution.py
+++ b/solution.py
@@ -213,8 +213,9 @@
 def out_proj_kernel(att_ref, w_ref, res_ref, ls_ref, o_ref):
     total = jnp.zeros(o_ref.shape, jnp.float32)
     for g in range(att_ref.shape[0]):
-        term = jnp.dot(att_ref[g, 0], w_ref[g, 0], preferred_element_type=jnp.float32)
-        term = term + jnp.dot(att_ref[g, 1], w_ref[g, 1], preferred_element_type=jnp.float32)
+        heads = jnp.concatenate([att_ref[g, 0], att_ref[g, 1]], axis=1)
+        weights = w_ref[g].reshape(2 * HEAD_DIM, w_ref.shape[-1])
+        term = jnp.dot(heads, weights, preferred_element_type=jnp.float32)
         total = total + term.astype(jnp.bfloat16).astype(jnp.float32)
     o_ref[...] = res_ref[...].astype(jnp.float32) + ls_ref[...] * total
 

time: 353 us -> 352 us (level)
  no operation moved by 1% of the time
where the time goes in v8:
time: 352 us; the launch traced here: 351 us
  waiting for transfers between devices  196 us (56%)
  Pallas kernels  59.4 us (17%)
  matrix products  36.2 us (10%)
  other arithmetic  21.3 us (6%)
  local copies, waits for them, and re-layouts  18.3 us (5%)
  between operations  13.3 us (4%)
  starting transfers between devices  6.91 us (2%)
    reduce_scatter x1, waiting for transfers between devices, per_device(): lax.psum_scatter(partial.reshape(row_count * merged_count, -1), 'rows', s...  93.5 us
    all_gather x1, waiting for transfers between devices, per_device(): row_tokens = lax.all_gather(normed, 'seq', axis=0, tiled=True)  66.7 us
    pallas_call x1, Pallas kernels, attend_kernel(): pl.pallas_call(functools.partial(attention_kernel, scale), out_shape=jax....  37 us
    all_to_all x1, waiting for transfers between devices, per_device(): lax.all_to_all(merged_norm, 'rows', split_axis=1, concat_axis=0, tiled=True)  23.5 us
    dot_general x1, matrix products, per_device(): jnp.dot(ordered, fc_weight, preferred_element_type=jnp.float32)  19.2 us
    dot_general x1, matrix products, per_device(): jnp.dot(row_tokens, qkv_weight, preferred_element_type=jnp.float32)  15.7 us
    all_gather x1, waiting for transfers between devices, per_device(): full_out_weight = lax.all_gather(out_weight, 'seq', axis=0, tiled=False)  11.7 us
    pallas_call x1, Pallas kernels, seq_sum(): pl.pallas_call(seq_sum_kernel, out_shape=jax.ShapeDtypeStruct(part.shape,...  11.6 us
  transfers between devices with their start and end apart: 4, of which 4 were waited for; matrix products, arithmetic and copies ran while one was open for 9% of the time, Pallas kernels for 14%

profile of v8, /device:TPU:1, one launch (start us, length us, event | category | flops | bytes accessed | tf_op | source)
XLA Modules:
  0.0 351.4 jit_solution(3224713529347429443)
XLA Ops:
  6.5 0.0 all-gather.4.cloned.1.call-start
  6.5 2.0 fusion.5
  8.5 0.0 copy-done.2
  8.5 2.4 fusion.7
  10.9 0.0 all-gather.4.cloned.1.call-update
  10.9 0.0 all-gather.6.cloned.1.call-start
  11.0 0.7 all-gather.6.cloned.1.call-update
  11.7 0.0 copy-start.7
  11.7 0.7 reshape_squeeze.19
  12.4 0.0 copy-done.7
  12.4 0.8 copy.28.qg_ref
  13.2 0.8 copy.29.kg_ref
  14.0 1.1 copy.54
  15.1 0.0 copy-start.6
  15.1 0.0 copy-start.3
  15.1 0.0 copy-start.4
  15.1 0.0 copy-start.8
  15.1 1.6 reshape.138.res_ref
  16.7 0.0 copy-done.6
  16.7 0.6 reshape.139.ls_ref
  17.3 0.0 copy-done.3
  17.3 0.1 add.78
  17.4 0.0 copy-done.4
  17.4 0.1 mul.110
  17.6 66.7 %all-gather.4.cloned.1.call-done = bf16[2048,3200]{1,0:T(8,128)(2,1)} async-done(((bf16[256,3200]{1,0:T(8,128)(2,1)}), bf16[2048,3200]{1,0:T(8,128)(2,1)}) %all-gather.4.cloned.1.call-update) | async-done | bytes 13107216 | tf_op jit(solution)/shard_map/all_gather | solution.py:267
  84.2 15.7 %fusion.38 = f32[2048,768]{0,1:T(8,128)S(1)} fusion(bf16[2048,3200]{1,0:T(8,128)(2,1)} %all-gather.4.cloned.1.call-done, bf16[3200,768]{1,0:T(8,128)(2,1)} %param.15), kind=kOutput, calls=%fused_computation.66 | convolution fusion | flops 10066329600 | bytes 24313856 | tf_op jit(solution)/shard_map/dot_general | solution.py:270
  99.9 2.6 copy-done
  102.5 0.4 fusion.9
  102.9 0.6 pad_maximum_fusion.part_ref
  103.5 11.6 %shard_map.127 = f32[3,2048]{1,0:T(4,128)} custom-call(f32[3,2048]{1,0:T(4,128)} %pad_maximum_fusion.part_ref), custom_call_target="tpu_custom_call" | custom-call | tf_op jit(solution)/shard_map/pallas_call | solution.py:61
  115.2 1.5 fusion.37
  116.7 1.3 copy.30.qseg_ref
  118.0 37.0 %shard_map.128 = bf16[8,2,256,128]{3,2,1,0:T(8,128)(2,1)} custom-call(f32[768,2048]{1,0:T(8,128)} %bitcast.41, f32[768,2048]{1,0:T(8,128)} %bitcast.42, f32[768,2048]{1,0:T(8,128)} %bitcast.43, f32[1,2048]{1,0:T(1,128)} %get-tuple-element.10.qrs_ref, f32[1,2048]{1,0:T(1,128)} %get-tuple-element.9.krs_ref, f32[256,1]{1,0:T(8,128)} %copy.28.qg_ref, ...), custom_call_target="tpu_custom_call" | custom-call | flops 4294967296 | bytes 6291456 | tf_op jit(solution)/shard_map/pallas_call | solution.py:171
  155.0 3.1 copy.31
  158.1 11.7 %all-gather.6.cloned.1.call-done = bf16[2048,3200]{1,0:T(8,128)(2,1)} async-done(((bf16[256,3200]{1,0:T(8,128)(2,1)}), bf16[2048,3200]{1,0:T(8,128)(2,1)}) %all-gather.6.cloned.1.call-update) | async-done | bytes 13107216 | tf_op jit(solution)/shard_map/all_gather | solution.py:299
  169.9 10.7 %shard_map.129 = f32[256,3200]{1,0:T(8,128)} custom-call(bf16[8,2,256,128]{3,2,1,0:T(8,128)(2,1)} %bitcast.48, bf16[8,2,128,3200]{3,2,1,0:T(8,128)(2,1)} %bitcast.44, bf16[256,3200]{1,0:T(8,128)(2,1)} %reshape.138.res_ref, f32[1,3200]{1,0:T(1,128)} %reshape.139.ls_ref), custom_call_target="tpu_custom_call" | custom-call | flops 3355443200 | bytes 18022400 | tf_op jit(solution)/shard_map/pallas_call | solution.py:226
  180.6 2.3 reduce_sum.62
  182.9 0.6 copy-done.1
  183.5 3.2 reshape.140
  186.7 0.1 reduce_sum.63
  186.8 0.1 reduce_sum.64
  186.9 0.1 sub.24
  187.0 0.1 sub.25
  187.1 0.5 multiply_reduce_fusion
  187.6 0.1 reduce_sum.66
  187.7 0.1 reduce_sum.67
  187.8 4.7 %fusion.4 = bf16[64,16,800]{2,0,1:T(8,128)(2,1)} fusion(f32[64,16,800]{2,1,0:T(8,128)} %reshape.140, f32[16,800]{1,0:T(8,128)S(1)} %add.78, f32[16,800]{1,0:T(8,128)S(1)} %mul.110, f32[64]{0:T(128)S(1)} %add_rsqrt_fusion.3, f32[64]{0:T(128)S(1)} %broadcast_multiply_fusion.1), kind=kLoop, calls=%fused_computation.8 | loop fusion | flops 4096000 | bytes 5018112 | tf_op jit(solution)/shard_map/convert_element_type | solution.py:321
  192.5 6.8 %all-to-all-start = ((bf16[64,16,800]{2,0,1:T(8,128)(2,1)}), bf16[64,16,800]{2,0,1:T(8,128)(2,1)S(1)}, u32[]{:S(2)}, u32[]{:S(2)}) async-start(bf16[64,16,800]{2,0,1:T(8,128)(2,1)} %fusion.4), calls=%async_computation | async-start | bytes 3670016 | tf_op jit(solution)/shard_map/all_to_all | solution.py:330
  199.3 0.0 reduce-scatter.2.cloned.1.call-start
  199.4 0.5 broadcast.118
  199.9 0.0 copy-done.9
  199.9 0.7 reduce.11
  200.6 0.1 reshape_squeeze.20
  200.7 0.1 fusion.33
  200.8 0.1 mul.116
  200.9 0.6 dynamic_slice.3
  201.5 0.6 compare_convert_fusion
  202.1 0.1 broadcast_multiply_fusion
  202.2 23.5 %all-to-all-done = bf16[64,16,800]{2,0,1:T(8,128)(2,1)S(1)} async-done(((bf16[64,16,800]{2,0,1:T(8,128)(2,1)}), bf16[64,16,800]{2,0,1:T(8,128)(2,1)S(1)}, u32[]{:S(2)}, u32[]{:S(2)}) %all-to-all-start) | async-done | bytes 1638432 | tf_op jit(solution)/shard_map/all_to_all | solution.py:330
  225.7 1.3 fusion.14
  226.9 19.2 %add_convert_fusion = bf16[16,64,6144]{2,1,0:T(8,128)(2,1)} fusion(f32[16,64]{1,0:T(8,128)S(1)} %broadcast_multiply_fusion, bf16[800,6144]{1,0:T(8,128)(2,1)} %param.23, bf16[16,64,800]{2,0,1:T(8,128)(2,1)S(1)} %fusion.14), kind=kOutput, calls=%fused_computation | convolution fusion | flops 10078912512 | bytes 24055808 | tf_op jit(solution)/shard_map/dot_general | solution.py:341
  246.2 0.0 reduce-scatter.2.cloned.1.call-update
  246.2 93.5 %reduce-scatter.2.cloned.1.call-done = bf16[64,6144]{1,0:T(8,128)(2,1)} async-done(((bf16[1024,6144]{1,0:T(8,128)(2,1)}), bf16[64,6144]{1,0:T(8,128)(2,1)}) %reduce-scatter.2.cloned.1.call-update) | async-done | bytes 786448 | tf_op jit(solution)/shard_map/reduce_scatter | solution.py:347
  339.7 5.2 %fusion.30 = bf16[1,64,6144]{2,1,0:T(8,128)(2,1)} fusion(bf16[64,6144]{1,0:T(8,128)(2,1)} %reduce-scatter.2.cloned.1.call-done, f32[6144]{0:T(1024)S(1)} %copy-done.5), kind=kLoop, calls=%fused_computation.45 | loop fusion | flops 26345472 | bytes 1597440 | tf_op jit(solution)/shard_map/broadcast_in_dim | solution.py:354
  (15 shorter events, 0.1 us)
Async XLA Ops:
  6.5 2.0 copy-start.2
  6.5 77.7 %all-gather.4.cloned.1.call-start = ((), (), s32[]{:S(2)}) async-start(), calls=%async_computation.2 | async-start | bytes 14745600 | tf_op jit(solution)/shard_map/all_gather | solution.py:267
  10.9 159.0 %all-gather.6.cloned.1.call-start = ((), (), s32[]{:S(2)}) async-start(), calls=%async_computation.4 | async-start | bytes 14745600 | tf_op jit(solution)/shard_map/all_gather | solution.py:299
  11.7 0.7 copy-start.7
  15.1 1.6 copy-start.6
  15.1 2.2 copy-start.3
  15.1 2.3 copy-start.4
  15.1 2.4 copy-start.8
  99.9 2.6 copy-start
  180.6 2.9 copy-start.1
  192.5 7.4 %copy-start.9 = (s32[1,256]{1,0:T(1,128)S(1)}, s32[1,256]{1,0:T(1,128)}, u32[]{:S(2)}) copy-start(s32[1,256]{1,0:T(1,128)} %param.20) | copy-start | bytes 3076
  192.5 8.4 %copy-start.10 = (s32[16]{0:T(128)S(1)}, s32[16]{0:T(128)}, u32[]{:S(2)}) copy-start(s32[16]{0:T(128)} %param.25) | copy-start | bytes 196
  192.5 33.2 %all-to-all-start = ((bf16[64,16,800]{2,0,1:T(8,128)(2,1)}), bf16[64,16,800]{2,0,1:T(8,128)(2,1)S(1)}, u32[]{:S(2)}, u32[]{:S(2)}) async-start(bf16[64,16,800]{2,0,1:T(8,128)(2,1)} %fusion.4), calls=%async_computation | async-start | bytes 3670016 | tf_op jit(solution)/shard_map/all_to_all | solution.py:330
  199.3 140.4 %reduce-scatter.2.cloned.1.call-start = ((), (), s32[]{:S(2)}) async-start(), calls=%async_computation.3 | async-start | bytes 13369344 | tf_op jit(solution)/shard_map/reduce_scatter | solution.py:347
  246.2 93.5 %copy-start.5 = (f32[6144]{0:T(1024)S(1)}, f32[6144]{0:T(1024)}, u32[]{:S(2)}) copy-start(f32[6144]{0:T(1024)} %param.24) | copy-start | bytes 73732
Sparse Core Ops, SparseCore 0:
  11.0 73.1 all-gather.3
  85.9 83.9 all-gather.5
  246.3 93.2 reduce-scatter.1

commit v9 on v8

--- a/solution.py
+++ b/solution.py
@@ -350,7 +350,8 @@
         scatter_dimension=0,
         tiled=True,
     ).astype(jnp.float32)
-    result = jax.nn.gelu(summed + fc_bias, approximate=False)
+    pre = summed + fc_bias
+    result = pre * (1.0 + lax.erf(pre * (2.0 ** -0.5))) * 0.5
     return result.astype(jnp.bfloat16)[None]
 
 

time: 352 us -> 350 us (level)
  no operation moved by 1% of the time
where the time goes in v9:
time: 350 us; the launch traced here: 349 us
  waiting for transfers between devices  196 us (56%)
  Pallas kernels  59.4 us (17%)
  matrix products  36.2 us (10%)
  other arithmetic  19.2 us (5%)
  local copies, waits for them, and re-layouts  18.3 us (5%)
  between operations  13.3 us (4%)
  starting transfers between devices  6.92 us (2%)
    reduce_scatter x1, waiting for transfers between devices, per_device(): lax.psum_scatter(partial.reshape(row_count * merged_count, -1), 'rows', s...  93.5 us
    all_gather x1, waiting for transfers between devices, per_device(): row_tokens = lax.all_gather(normed, 'seq', axis=0, tiled=True)  66.7 us
    pallas_call x1, Pallas kernels, attend_kernel(): pl.pallas_call(functools.partial(attention_kernel, scale), out_shape=jax....  37 us
    all_to_all x1, waiting for transfers between devices, per_device(): lax.all_to_all(merged_norm, 'rows', split_axis=1, concat_axis=0, tiled=True)  23.5 us
    dot_general x1, matrix products, per_device(): jnp.dot(ordered, fc_weight, preferred_element_type=jnp.float32)  19.2 us
    dot_general x1, matrix products, per_device(): jnp.dot(row_tokens, qkv_weight, preferred_element_type=jnp.float32)  15.7 us
    all_gather x1, waiting for transfers between devices, per_device(): full_out_weight = lax.all_gather(out_weight, 'seq', axis=0, tiled=False)  11.7 us
    pallas_call x1, Pallas kernels, seq_sum(): pl.pallas_call(seq_sum_kernel, out_shape=jax.ShapeDtypeStruct(part.shape,...  11.6 us
  transfers between devices with their start and end apart: 4, of which 4 were waited for; matrix products, arithmetic and copies ran while one was open for 9% of the time, Pallas kernels for 14%

profile of v9, /device:TPU:1, one launch (start us, length us, event | category | flops | bytes accessed | tf_op | source)
XLA Modules:
  0.0 349.4 jit_solution(15109234748464525390)
XLA Ops:
  6.5 0.0 all-gather.4.cloned.1.call-start
  6.5 1.8 fusion.5
  8.4 0.0 copy-start.2
  8.4 3.2 fusion.7
  11.6 0.0 all-gather.4.cloned.1.call-update
  11.6 0.0 all-gather.6.cloned.1.call-start
  11.7 0.7 all-gather.6.cloned.1.call-update
  12.4 0.0 copy-done.2
  12.4 0.7 reshape_squeeze.19
  13.1 0.0 copy-done.7
  13.1 0.8 copy.28.qg_ref
  13.9 0.8 copy.29.kg_ref
  14.7 1.1 copy.54
  15.8 1.6 reshape.138.res_ref
  17.4 0.0 copy-done.6
  17.4 0.6 reshape.139.ls_ref
  18.0 0.0 copy-done.3
  18.0 0.1 add.84
  18.1 0.0 copy-done.4
  18.1 0.1 mul.110
  18.2 0.0 copy-done.8
  18.2 66.7 %all-gather.4.cloned.1.call-done = bf16[2048,3200]{1,0:T(8,128)(2,1)} async-done(((bf16[256,3200]{1,0:T(8,128)(2,1)}), bf16[2048,3200]{1,0:T(8,128)(2,1)}) %all-gather.4.cloned.1.call-update) | async-done | bytes 13107216 | tf_op jit(solution)/shard_map/all_gather | solution.py:267
  84.9 15.7 %fusion.25 = f32[2048,768]{0,1:T(8,128)S(1)} fusion(bf16[2048,3200]{1,0:T(8,128)(2,1)} %all-gather.4.cloned.1.call-done, bf16[3200,768]{1,0:T(8,128)(2,1)} %param.15), kind=kOutput, calls=%fused_computation.45 | convolution fusion | flops 10066329600 | bytes 24313856 | tf_op jit(solution)/shard_map/dot_general | solution.py:270
  100.6 0.0 copy-start
  100.6 2.6 copy-done
  103.2 0.4 fusion.9
  103.6 0.6 pad_maximum_fusion.part_ref
  104.3 11.6 %shard_map.127 = f32[3,2048]{1,0:T(4,128)} custom-call(f32[3,2048]{1,0:T(4,128)} %pad_maximum_fusion.part_ref), custom_call_target="tpu_custom_call" | custom-call | tf_op jit(solution)/shard_map/pallas_call | solution.py:61
  115.9 1.5 fusion.24
  117.4 1.3 copy.30.qseg_ref
  118.7 37.0 %shard_map.128 = bf16[8,2,256,128]{3,2,1,0:T(8,128)(2,1)} custom-call(f32[768,2048]{1,0:T(8,128)} %bitcast.41, f32[768,2048]{1,0:T(8,128)} %bitcast.42, f32[768,2048]{1,0:T(8,128)} %bitcast.43, f32[1,2048]{1,0:T(1,128)} %get-tuple-element.10.qrs_ref, f32[1,2048]{1,0:T(1,128)} %get-tuple-element.9.krs_ref, f32[256,1]{1,0:T(8,128)} %copy.28.qg_ref, ...), custom_call_target="tpu_custom_call" | custom-call | flops 4294967296 | bytes 6291456 | tf_op jit(solution)/shard_map/pallas_call | solution.py:171
  155.7 3.1 copy.31
  158.9 11.7 %all-gather.6.cloned.1.call-done = bf16[2048,3200]{1,0:T(8,128)(2,1)} async-done(((bf16[256,3200]{1,0:T(8,128)(2,1)}), bf16[2048,3200]{1,0:T(8,128)(2,1)}) %all-gather.6.cloned.1.call-update) | async-done | bytes 13107216 | tf_op jit(solution)/shard_map/all_gather | solution.py:299
  170.6 10.7 %shard_map.129 = f32[256,3200]{1,0:T(8,128)} custom-call(bf16[8,2,256,128]{3,2,1,0:T(8,128)(2,1)} %bitcast.48, bf16[8,2,128,3200]{3,2,1,0:T(8,128)(2,1)} %bitcast.44, bf16[256,3200]{1,0:T(8,128)(2,1)} %reshape.138.res_ref, f32[1,3200]{1,0:T(1,128)} %reshape.139.ls_ref), custom_call_target="tpu_custom_call" | custom-call | flops 3355443200 | bytes 18022400 | tf_op jit(solution)/shard_map/pallas_call | solution.py:226
  181.3 2.3 reduce_sum.62
  183.6 0.6 copy-done.1
  184.2 3.2 reshape.140
  187.4 0.1 reduce_sum.63
  187.5 0.1 reduce_sum.64
  187.6 0.1 sub.24
  187.7 0.1 sub.25
  187.8 0.5 multiply_reduce_fusion
  188.3 0.1 reduce_sum.66
  188.4 0.1 reduce_sum.67
  188.5 0.0 copy-start.9
  188.6 4.7 %fusion.4 = bf16[64,16,800]{2,0,1:T(8,128)(2,1)} fusion(f32[64,16,800]{2,1,0:T(8,128)} %reshape.140, f32[16,800]{1,0:T(8,128)S(1)} %add.84, f32[16,800]{1,0:T(8,128)S(1)} %mul.110, f32[64]{0:T(128)S(1)} %add_rsqrt_fusion.3, f32[64]{0:T(128)S(1)} %broadcast_multiply_fusion.1), kind=kLoop, calls=%fused_computation.8 | loop fusion | flops 4096000 | bytes 5018112 | tf_op jit(solution)/shard_map/convert_element_type | solution.py:321
  193.2 6.8 %all-to-all-start = ((bf16[64,16,800]{2,0,1:T(8,128)(2,1)}), bf16[64,16,800]{2,0,1:T(8,128)(2,1)S(1)}, u32[]{:S(2)}, u32[]{:S(2)}) async-start(bf16[64,16,800]{2,0,1:T(8,128)(2,1)} %fusion.4), calls=%async_computation | async-start | bytes 3670016 | tf_op jit(solution)/shard_map/all_to_all | solution.py:330
  200.1 0.0 reduce-scatter.2.cloned.1.call-start
  200.1 0.5 broadcast.113
  200.6 0.0 copy-done.9
  200.6 0.7 reduce.11
  201.3 0.1 reshape_squeeze.20
  201.4 0.1 fusion.20
  201.5 0.1 mul.116
  201.6 0.0 copy-done.10
  201.6 0.6 dynamic_slice.3
  202.2 0.6 compare_convert_fusion
  202.9 0.1 broadcast_multiply_fusion
  202.9 23.5 %all-to-all-done = bf16[64,16,800]{2,0,1:T(8,128)(2,1)S(1)} async-done(((bf16[64,16,800]{2,0,1:T(8,128)(2,1)}), bf16[64,16,800]{2,0,1:T(8,128)(2,1)S(1)}, u32[]{:S(2)}, u32[]{:S(2)}) %all-to-all-start) | async-done | bytes 1638432 | tf_op jit(solution)/shard_map/all_to_all | solution.py:330
  226.4 1.3 fusion.14
  227.7 19.2 %add_convert_fusion = bf16[16,64,6144]{2,1,0:T(8,128)(2,1)} fusion(f32[16,64]{1,0:T(8,128)S(1)} %broadcast_multiply_fusion, bf16[800,6144]{1,0:T(8,128)(2,1)} %param.23, bf16[16,64,800]{2,0,1:T(8,128)(2,1)S(1)} %fusion.14), kind=kOutput, calls=%fused_computation | convolution fusion | flops 10078912512 | bytes 24055808 | tf_op jit(solution)/shard_map/dot_general | solution.py:341
  246.9 0.0 reduce-scatter.2.cloned.1.call-update
  247.0 93.5 %reduce-scatter.2.cloned.1.call-done = bf16[64,6144]{1,0:T(8,128)(2,1)} async-done(((bf16[1024,6144]{1,0:T(8,128)(2,1)}), bf16[64,6144]{1,0:T(8,128)(2,1)}) %reduce-scatter.2.cloned.1.call-update) | async-done | bytes 786448 | tf_op jit(solution)/shard_map/reduce_scatter | solution.py:347
  340.4 2.4 fusion.17
  (15 shorter events, 0.1 us)
Async XLA Ops:
  6.5 78.4 %all-gather.4.cloned.1.call-start = ((), (), s32[]{:S(2)}) async-start(), calls=%async_computation.2 | async-start | bytes 14745600 | tf_op jit(solution)/shard_map/all_gather | solution.py:267
  8.4 4.0 %copy-start.2 = (bf16[1,256,3200]{2,1,0:T(8,128)(2,1)S(1)}, bf16[1,256,3200]{2,1,0:T(8,128)(2,1)}, u32[]{:S(2)}) copy-start(bf16[1,256,3200]{2,1,0:T(8,128)(2,1)} %param.13) | copy-start | bytes 4915204
  11.6 1.5 copy-start.7
  11.6 159.0 %all-gather.6.cloned.1.call-start = ((), (), s32[]{:S(2)}) async-start(), calls=%async_computation.4 | async-start | bytes 14745600 | tf_op jit(solution)/shard_map/all_gather | solution.py:299
  14.7 2.7 copy-start.6
  14.7 3.3 copy-start.3
  14.7 3.4 copy-start.4
  14.7 3.5 %copy-start.8 = (s32[1,256]{1,0:T(1,128)S(1)}, s32[1,256]{1,0:T(1,128)}, u32[]{:S(2)}) copy-start(s32[1,256]{1,0:T(1,128)} %param.19) | copy-start | bytes 3076
  100.6 2.6 copy-start
  181.3 2.9 copy-start.1
  188.5 12.1 %copy-start.9 = (s32[1,256]{1,0:T(1,128)S(1)}, s32[1,256]{1,0:T(1,128)}, u32[]{:S(2)}) copy-start(s32[1,256]{1,0:T(1,128)} %param.20) | copy-start | bytes 3076
  193.2 8.4 %copy-start.10 = (s32[16]{0:T(128)S(1)}, s32[16]{0:T(128)}, u32[]{:S(2)}) copy-start(s32[16]{0:T(128)} %param.25) | copy-start | bytes 196
  193.2 33.2 %all-to-all-start = ((bf16[64,16,800]{2,0,1:T(8,128)(2,1)}), bf16[64,16,800]{2,0,1:T(8,128)(2,1)S(1)}, u32[]{:S(2)}, u32[]{:S(2)}) async-start(bf16[64,16,800]{2,0,1:T(8,128)(2,1)} %fusion.4), calls=%async_computation | async-start | bytes 3670016 | tf_op jit(solution)/shard_map/all_to_all | solution.py:330
  200.1 140.4 %reduce-scatter.2.cloned.1.call-start = ((), (), s32[]{:S(2)}) async-start(), calls=%async_computation.3 | async-start | bytes 13369344 | tf_op jit(solution)/shard_map/reduce_scatter | solution.py:347
  246.9 93.5 %copy-start.5 = (f32[6144]{0:T(1024)S(1)}, f32[6144]{0:T(1024)}, u32[]{:S(2)}) copy-start(f32[6144]{0:T(1024)} %param.24) | copy-start | bytes 73732
Sparse Core Ops, SparseCore 0:
  11.7 73.1 all-gather.3
  86.6 83.9 all-gather.5
  247.1 93.3 reduce-scatter.1

commit v10 on v9

--- a/solution.py
+++ b/solution.py
@@ -210,14 +210,21 @@
     )
 
 
-def out_proj_kernel(att_ref, w_ref, res_ref, ls_ref, o_ref):
+def out_proj_kernel(att_ref, w_ref, res_ref, ls_ref, o_ref, sum_ref):
     total = jnp.zeros(o_ref.shape, jnp.float32)
     for g in range(att_ref.shape[0]):
         heads = jnp.concatenate([att_ref[g, 0], att_ref[g, 1]], axis=1)
         weights = w_ref[g].reshape(2 * HEAD_DIM, w_ref.shape[-1])
         term = jnp.dot(heads, weights, preferred_element_type=jnp.float32)
         total = total + term.astype(jnp.bfloat16).astype(jnp.float32)
-    o_ref[...] = res_ref[...].astype(jnp.float32) + ls_ref[...] * total
+    hidden = res_ref[...].astype(jnp.float32) + ls_ref[...] * total
+    o_ref[...] = hidden
+
+    @pl.when(pl.program_id(0) == 0)
+    def _():
+        sum_ref[...] = jnp.zeros(sum_ref.shape, jnp.float32)
+
+    sum_ref[...] += jnp.sum(hidden, axis=1, keepdims=True)
 
 
 def out_proj(attended, out_weight_groups, residual, layer_scale, tile=640):
@@ -225,7 +232,10 @@
     width = out_weight_groups.shape[-1]
     return pl.pallas_call(
         out_proj_kernel,
-        out_shape=jax.ShapeDtypeStruct((tokens, width), jnp.float32),
+        out_shape=(
+            jax.ShapeDtypeStruct((tokens, width), jnp.float32),
+            jax.ShapeDtypeStruct((tokens, 1), jnp.float32),
+        ),
         grid=(width // tile,),
         in_specs=[
             pl.BlockSpec(attended.shape, lambda j: (0, 0, 0, 0)),
@@ -233,7 +243,10 @@
             pl.BlockSpec((tokens, tile), lambda j: (0, j)),
             pl.BlockSpec((1, tile), lambda j: (0, j)),
         ],
-        out_specs=pl.BlockSpec((tokens, tile), lambda j: (0, j)),
+        out_specs=(
+            pl.BlockSpec((tokens, tile), lambda j: (0, j)),
+            pl.BlockSpec((tokens, 1), lambda j: (0, 0)),
+        ),
         cost_estimate=pl.CostEstimate(
             flops=2 * tokens * groups * heads_here * HEAD_DIM * width,
             transcendentals=0,
@@ -309,14 +322,14 @@
         )
         return jnp.transpose(x.reshape(split), order).reshape(shape)
 
-    hidden = out_proj(
+    hidden, row_sums = out_proj(
         shuffle_rows(attended, 2),
         full_out_weight.reshape(seq_count, heads_here, HEAD_DIM, -1),
         shuffle_rows(residual_in[0], 0),
         layer_scale,
     )
     merged = hidden.reshape(merged_count, 4 * D)
-    centre = merged - jnp.mean(merged, axis=-1, keepdims=True)
+    centre = merged - jnp.sum(row_sums.reshape(merged_count, 4), axis=1, keepdims=True) / (4 * D)
     spread = jnp.mean(centre * centre, axis=-1, keepdims=True)
     merged_norm = (centre * lax.rsqrt(spread + 1e-05) * ln_weight + ln_bias).astype(jnp.bfloat16)
     merged_mask = (

time: 350 us -> 350 us (level)
  no operation moved by 1% of the time
where the time goes in v10:
time: 350 us; the launch traced here: 349 us
  waiting for transfers between devices  196 us (56%)
  Pallas kernels  59 us (17%)
  matrix products  36.2 us (10%)
  local copies, waits for them, and re-layouts  20.1 us (6%)
  other arithmetic  17.9 us (5%)
  between operations  13.3 us (4%)
  starting transfers between devices  6.92 us (2%)
    reduce_scatter x1, waiting for transfers between devices, per_device(): lax.psum_scatter(partial.reshape(row_count * merged_count, -1), 'rows', s...  93.4 us
    all_gather x1, waiting for transfers between devices, per_device(): row_tokens = lax.all_gather(normed, 'seq', axis=0, tiled=True)  66.7 us
    pallas_call x1, Pallas kernels, attend_kernel(): pl.pallas_call(functools.partial(attention_kernel, scale), out_shape=jax....  37 us
    all_to_all x1, waiting for transfers between devices, per_device(): lax.all_to_all(merged_norm, 'rows', split_axis=1, concat_axis=0, tiled=True)  23.5 us
    dot_general x1, matrix products, per_device(): jnp.dot(ordered, fc_weight, preferred_element_type=jnp.float32)  19.2 us
    dot_general x1, matrix products, per_device(): jnp.dot(row_tokens, qkv_weight, preferred_element_type=jnp.float32)  15.7 us
    all_gather x1, waiting for transfers between devices, per_device(): full_out_weight = lax.all_gather(out_weight, 'seq', axis=0, tiled=False)  11.7 us
    pallas_call x1, Pallas kernels, seq_sum(): pl.pallas_call(seq_sum_kernel, out_shape=jax.ShapeDtypeStruct(part.shape,...  11.6 us
  transfers between devices with their start and end apart: 4, of which 4 were waited for; matrix products, arithmetic and copies ran while one was open for 9% of the time, Pallas kernels for 14%

profile of v10, /device:TPU:1, one launch (start us, length us, event | category | flops | bytes accessed | tf_op | source)
XLA Modules:
  0.0 349.4 jit_solution(12574589772655192471)
XLA Ops:
  6.5 0.0 all-gather.4.cloned.1.call-start
  6.5 1.8 fusion.5
  8.4 0.0 copy-start.1
  8.4 3.2 fusion.7
  11.6 0.0 all-gather.4.cloned.1.call-update
  11.6 0.0 all-gather.6.cloned.1.call-start
  11.7 0.7 all-gather.6.cloned.1.call-update
  12.4 0.0 copy-done.1
  12.4 0.7 reshape_squeeze.19
  13.1 0.0 copy-done.7
  13.1 0.8 copy.28.qg_ref
  13.9 0.8 copy.29.kg_ref
  14.7 1.1 copy.54
  15.8 1.6 reshape.140.res_ref
  17.4 0.0 copy-done.6
  17.4 0.6 reshape.141.ls_ref
  18.0 0.0 copy-done.3
  18.0 0.1 add.84
  18.1 0.0 copy-done.4
  18.1 0.1 mul.110
  18.2 0.0 copy-done.8
  18.2 66.7 %all-gather.4.cloned.1.call-done = bf16[2048,3200]{1,0:T(8,128)(2,1)} async-done(((bf16[256,3200]{1,0:T(8,128)(2,1)}), bf16[2048,3200]{1,0:T(8,128)(2,1)}) %all-gather.4.cloned.1.call-update) | async-done | bytes 13107216 | tf_op jit(solution)/shard_map/all_gather | solution.py:280
  84.9 15.7 %fusion.25 = f32[2048,768]{0,1:T(8,128)S(1)} fusion(bf16[2048,3200]{1,0:T(8,128)(2,1)} %all-gather.4.cloned.1.call-done, bf16[3200,768]{1,0:T(8,128)(2,1)} %param.15), kind=kOutput, calls=%fused_computation.45 | convolution fusion | flops 10066329600 | bytes 24313856 | tf_op jit(solution)/shard_map/dot_general | solution.py:283
  100.6 0.0 copy-start
  100.6 2.6 copy-done
  103.2 0.4 fusion.9
  103.6 0.6 pad_maximum_fusion.part_ref
  104.3 11.6 %shard_map.127 = f32[3,2048]{1,0:T(4,128)} custom-call(f32[3,2048]{1,0:T(4,128)} %pad_maximum_fusion.part_ref), custom_call_target="tpu_custom_call" | custom-call | tf_op jit(solution)/shard_map/pallas_call | solution.py:61
  115.9 1.5 fusion.24
  117.4 1.3 copy.30.qseg_ref
  118.7 37.0 %shard_map.128 = bf16[8,2,256,128]{3,2,1,0:T(8,128)(2,1)} custom-call(f32[768,2048]{1,0:T(8,128)} %bitcast.41, f32[768,2048]{1,0:T(8,128)} %bitcast.42, f32[768,2048]{1,0:T(8,128)} %bitcast.43, f32[1,2048]{1,0:T(1,128)} %get-tuple-element.14.qrs_ref, f32[1,2048]{1,0:T(1,128)} %get-tuple-element.13.krs_ref, f32[256,1]{1,0:T(8,128)} %copy.28.qg_ref, ...), custom_call_target="tpu_custom_call" | custom-call | flops 4294967296 | bytes 6291456 | tf_op jit(solution)/shard_map/pallas_call | solution.py:171
  155.7 3.1 copy.31
  158.9 11.7 %all-gather.6.cloned.1.call-done = bf16[2048,3200]{1,0:T(8,128)(2,1)} async-done(((bf16[256,3200]{1,0:T(8,128)(2,1)}), bf16[2048,3200]{1,0:T(8,128)(2,1)}) %all-gather.6.cloned.1.call-update) | async-done | bytes 13107216 | tf_op jit(solution)/shard_map/all_gather | solution.py:312
  170.6 10.4 %shard_map.129 = (f32[256,3200]{1,0:T(8,128)}, f32[256,1]{1,0:T(8,128)}) custom-call(bf16[8,2,256,128]{3,2,1,0:T(8,128)(2,1)} %bitcast.47, bf16[8,2,128,3200]{3,2,1,0:T(8,128)(2,1)} %bitcast.44, bf16[256,3200]{1,0:T(8,128)(2,1)} %reshape.140.res_ref, f32[1,3200]{1,0:T(1,128)} %reshape.141.ls_ref), custom_call_target="tpu_custom_call" | custom-call | flops 3355443200 | bytes 18022400 | tf_op jit(solution)/shard_map/pallas_call | solution.py:233
  181.0 1.0 reduce.4
  182.0 0.1 reshape.143
  182.1 0.1 reduce_sum.55
  182.2 0.1 sub.24
  182.3 0.1 sub.25
  182.4 0.0 copy-start.2
  182.4 5.5 %reshape.142 = f32[64,16,800]{2,1,0:T(8,128)} reshape(f32[256,3200]{1,0:T(8,128)} %get-tuple-element.7) | data formatting | bytes 6553600 | tf_op jit(solution)/shard_map/reshape | solution.py:331
  188.0 0.5 multiply_reduce_fusion
  188.4 0.1 reduce_sum.57
  188.5 0.1 reduce_sum.58
  188.7 0.0 copy-start.9
  188.7 4.7 %fusion.4 = bf16[64,16,800]{2,0,1:T(8,128)(2,1)} fusion(f32[64,16,800]{2,1,0:T(8,128)} %reshape.142, f32[16,800]{1,0:T(8,128)S(1)} %add.84, f32[16,800]{1,0:T(8,128)S(1)} %mul.110, f32[64]{0:T(128)S(1)} %add_rsqrt_fusion.3, f32[64]{0:T(128)S(1)} %broadcast_multiply_fusion.1), kind=kLoop, calls=%fused_computation.8 | loop fusion | flops 4096000 | bytes 5018112 | tf_op jit(solution)/shard_map/convert_element_type | solution.py:334
  193.4 6.8 %all-to-all-start = ((bf16[64,16,800]{2,0,1:T(8,128)(2,1)}), bf16[64,16,800]{2,0,1:T(8,128)(2,1)S(1)}, u32[]{:S(2)}, u32[]{:S(2)}) async-start(bf16[64,16,800]{2,0,1:T(8,128)(2,1)} %fusion.4), calls=%async_computation | async-start | bytes 3670016 | tf_op jit(solution)/shard_map/all_to_all | solution.py:343
  200.2 0.0 reduce-scatter.2.cloned.1.call-start
  200.2 0.5 broadcast.114
  200.8 0.0 copy-done.9
  200.8 0.7 reduce.10
  201.4 0.1 reshape_squeeze.20
  201.6 0.1 fusion.20
  201.7 0.1 mul.116
  201.7 0.6 dynamic_slice.3
  202.3 0.6 compare_convert_fusion
  203.0 0.1 broadcast_multiply_fusion
  203.1 23.5 %all-to-all-done = bf16[64,16,800]{2,0,1:T(8,128)(2,1)S(1)} async-done(((bf16[64,16,800]{2,0,1:T(8,128)(2,1)}), bf16[64,16,800]{2,0,1:T(8,128)(2,1)S(1)}, u32[]{:S(2)}, u32[]{:S(2)}) %all-to-all-start) | async-done | bytes 1638432 | tf_op jit(solution)/shard_map/all_to_all | solution.py:343
  226.5 1.3 fusion.14
  227.8 19.2 %add_convert_fusion = bf16[16,64,6144]{2,1,0:T(8,128)(2,1)} fusion(f32[16,64]{1,0:T(8,128)S(1)} %broadcast_multiply_fusion, bf16[800,6144]{1,0:T(8,128)(2,1)} %param.23, bf16[16,64,800]{2,0,1:T(8,128)(2,1)S(1)} %fusion.14), kind=kOutput, calls=%fused_computation | convolution fusion | flops 10078912512 | bytes 24055808 | tf_op jit(solution)/shard_map/dot_general | solution.py:354
  247.1 0.0 reduce-scatter.2.cloned.1.call-update
  247.1 93.4 %reduce-scatter.2.cloned.1.call-done = bf16[64,6144]{1,0:T(8,128)(2,1)} async-done(((bf16[1024,6144]{1,0:T(8,128)(2,1)}), bf16[64,6144]{1,0:T(8,128)(2,1)}) %reduce-scatter.2.cloned.1.call-update) | async-done | bytes 786448 | tf_op jit(solution)/shard_map/reduce_scatter | solution.py:360
  340.5 0.0 copy-done.5
  340.5 2.4 fusion.17
  (15 shorter events, 0.1 us)
Async XLA Ops:
  6.5 78.4 %all-gather.4.cloned.1.call-start = ((), (), s32[]{:S(2)}) async-start(), calls=%async_computation.2 | async-start | bytes 14745600 | tf_op jit(solution)/shard_map/all_gather | solution.py:280
  8.4 4.0 %copy-start.1 = (bf16[1,256,3200]{2,1,0:T(8,128)(2,1)S(1)}, bf16[1,256,3200]{2,1,0:T(8,128)(2,1)}, u32[]{:S(2)}) copy-start(bf16[1,256,3200]{2,1,0:T(8,128)(2,1)} %param.13) | copy-start | bytes 4915204
  11.6 1.5 copy-start.7
  11.6 159.0 %all-gather.6.cloned.1.call-start = ((), (), s32[]{:S(2)}) async-start(), calls=%async_computation.4 | async-start | bytes 14745600 | tf_op jit(solution)/shard_map/all_gather | solution.py:312
  14.7 2.7 copy-start.6
  14.7 3.3 copy-start.3
  14.7 3.4 copy-start.4
  14.7 3.5 %copy-start.8 = (s32[1,256]{1,0:T(1,128)S(1)}, s32[1,256]{1,0:T(1,128)}, u32[]{:S(2)}) copy-start(s32[1,256]{1,0:T(1,128)} %param.19) | copy-start | bytes 3076
  100.6 2.6 copy-start
  182.4 5.6 %copy-start.2 = (f32[256,3200]{1,0:T(8,128)S(1)}, f32[256,3200]{1,0:T(8,128)}, u32[]{:S(2)}) copy-start(f32[256,3200]{1,0:T(8,128)} %get-tuple-element.7) | copy-start | bytes 9830404
  188.7 12.1 %copy-start.9 = (s32[1,256]{1,0:T(1,128)S(1)}, s32[1,256]{1,0:T(1,128)}, u32[]{:S(2)}) copy-start(s32[1,256]{1,0:T(1,128)} %param.20) | copy-start | bytes 3076
  193.4 8.4 %copy-start.10 = (s32[16]{0:T(128)S(1)}, s32[16]{0:T(128)}, u32[]{:S(2)}) copy-start(s32[16]{0:T(128)} %param.25) | copy-start | bytes 196
  193.4 33.2 %all-to-all-start = ((bf16[64,16,800]{2,0,1:T(8,128)(2,1)}), bf16[64,16,800]{2,0,1:T(8,128)(2,1)S(1)}, u32[]{:S(2)}, u32[]{:S(2)}) async-start(bf16[64,16,800]{2,0,1:T(8,128)(2,1)} %fusion.4), calls=%async_computation | async-start | bytes 3670016 | tf_op jit(solution)/shard_map/all_to_all | solution.py:343
  200.2 140.3 %reduce-scatter.2.cloned.1.call-start = ((), (), s32[]{:S(2)}) async-start(), calls=%async_computation.3 | async-start | bytes 13369344 | tf_op jit(solution)/shard_map/reduce_scatter | solution.py:360
  247.1 93.4 %copy-start.5 = (f32[6144]{0:T(1024)S(1)}, f32[6144]{0:T(1024)}, u32[]{:S(2)}) copy-start(f32[6144]{0:T(1024)} %param.24) | copy-start | bytes 73732
Sparse Core Ops, SparseCore 0:
  11.7 73.1 all-gather.3
  86.6 83.9 all-gather.5
  247.2 93.2 reduce-scatter.1

commit v11 on v10

--- a/solution.py
+++ b/solution.py
@@ -332,6 +332,7 @@
     centre = merged - jnp.sum(row_sums.reshape(merged_count, 4), axis=1, keepdims=True) / (4 * D)
     spread = jnp.mean(centre * centre, axis=-1, keepdims=True)
     merged_norm = (centre * lax.rsqrt(spread + 1e-05) * ln_weight + ln_bias).astype(jnp.bfloat16)
+    merged_norm = lax.optimization_barrier(merged_norm)
     merged_mask = (
         pad_mask[0]
         .reshape(lines, 2, half_grid, 2)[:, 0, :, 0]

time: 350 us -> 351 us (level)
    all_to_all x0 -> x2, local copies, waits for them, and re-layouts: none -> 4.42 us  [per_device(): lax.all_to_all(merged_norm, 'rows', split_axis=1, concat_axis=0, tiled=True)]
where the time goes in v11:
time: 351 us
  waiting for transfers between devices  196 us (56%)
  Pallas kernels  59 us (17%)
  matrix products  36.2 us (10%)
  local copies, waits for them, and re-layouts  23.5 us (7%)
  other arithmetic  15.7 us (4%)
  between operations  13.3 us (4%)
  starting transfers between devices  6.78 us (2%)
    reduce_scatter x1, waiting for transfers between devices, per_device(): lax.psum_scatter(partial.reshape(row_count * merged_count, -1), 'rows', s...  93.3 us
    all_gather x1, waiting for transfers between devices, per_device(): row_tokens = lax.all_gather(normed, 'seq', axis=0, tiled=True)  66.9 us
    pallas_call x1, Pallas kernels, attend_kernel(): pl.pallas_call(functools.partial(attention_kernel, scale), out_shape=jax....  37 us
    all_to_all x1, waiting for transfers between devices, per_device(): lax.all_to_all(merged_norm, 'rows', split_axis=1, concat_axis=0, tiled=True)  23.5 us
    dot_general x1, matrix products, per_device(): jnp.dot(ordered, fc_weight, preferred_element_type=jnp.float32)  19.2 us
    dot_general x1, matrix products, per_device(): jnp.dot(row_tokens, qkv_weight, preferred_element_type=jnp.float32)  15.7 us
    all_gather x1, waiting for transfers between devices, per_device(): full_out_weight = lax.all_gather(out_weight, 'seq', axis=0, tiled=False)  11.7 us
    pallas_call x1, Pallas kernels, seq_sum(): pl.pallas_call(seq_sum_kernel, out_shape=jax.ShapeDtypeStruct(part.shape,...  11.6 us
  transfers between devices with their start and end apart: 4, of which 4 were waited for; matrix products, arithmetic and copies ran while one was open for 9% of the time, Pallas kernels for 14%

profile of v11, /device:TPU:1, one launch (start us, length us, event | category | flops | bytes accessed | tf_op | source)
XLA Modules:
  0.0 350.7 jit_solution(17839722971740803301)
XLA Ops:
  6.5 0.0 all-gather.4.cloned.1.call-start
  6.5 1.8 fusion.1
  8.4 0.0 copy-start.1
  8.4 3.2 fusion.3
  11.6 0.0 all-gather.4.cloned.1.call-update
  11.6 0.0 all-gather.6.cloned.1.call-start
  11.7 0.7 all-gather.6.cloned.1.call-update
  12.4 0.0 copy-done.1
  12.4 0.7 reshape_squeeze.19
  13.1 0.0 copy-done.7
  13.1 0.8 copy.35.qg_ref
  13.9 0.8 copy.36.kg_ref
  14.7 1.1 copy.52
  15.8 1.6 reshape.119.res_ref
  17.4 0.0 copy-done.6
  17.4 0.6 reshape.120.ls_ref
  18.0 0.0 copy-done.8
  18.0 66.9 %all-gather.4.cloned.1.call-done = bf16[2048,3200]{1,0:T(8,128)(2,1)} async-done(((bf16[256,3200]{1,0:T(8,128)(2,1)}), bf16[2048,3200]{1,0:T(8,128)(2,1)}) %all-gather.4.cloned.1.call-update) | async-done | bytes 13107216 | tf_op jit(solution)/shard_map/all_gather | solution.py:280
  84.9 15.7 %fusion.21 = f32[2048,768]{0,1:T(8,128)S(1)} fusion(bf16[2048,3200]{1,0:T(8,128)(2,1)} %all-gather.4.cloned.1.call-done, bf16[3200,768]{1,0:T(8,128)(2,1)} %param.15), kind=kOutput, calls=%fused_computation.41 | convolution fusion | flops 10066329600 | bytes 24313856 | tf_op jit(solution)/shard_map/dot_general | solution.py:283
  100.6 0.0 copy-start
  100.6 2.6 copy-done
  103.2 0.4 fusion.5
  103.6 0.6 pad_maximum_fusion.part_ref
  104.3 11.6 %shard_map.127 = f32[3,2048]{1,0:T(4,128)} custom-call(f32[3,2048]{1,0:T(4,128)} %pad_maximum_fusion.part_ref), custom_call_target="tpu_custom_call" | custom-call | tf_op jit(solution)/shard_map/pallas_call | solution.py:61
  115.9 1.5 fusion.20
  117.4 1.3 copy.37.qseg_ref
  118.7 37.0 %shard_map.128 = bf16[8,2,256,128]{3,2,1,0:T(8,128)(2,1)} custom-call(f32[768,2048]{1,0:T(8,128)} %bitcast.41, f32[768,2048]{1,0:T(8,128)} %bitcast.42, f32[768,2048]{1,0:T(8,128)} %bitcast.43, f32[1,2048]{1,0:T(1,128)} %get-tuple-element.14.qrs_ref, f32[1,2048]{1,0:T(1,128)} %get-tuple-element.13.krs_ref, f32[256,1]{1,0:T(8,128)} %copy.35.qg_ref, ...), custom_call_target="tpu_custom_call" | custom-call | flops 4294967296 | bytes 6291456 | tf_op jit(solution)/shard_map/pallas_call | solution.py:171
  155.7 3.1 copy.38
  158.9 11.7 %all-gather.6.cloned.1.call-done = bf16[2048,3200]{1,0:T(8,128)(2,1)} async-done(((bf16[256,3200]{1,0:T(8,128)(2,1)}), bf16[2048,3200]{1,0:T(8,128)(2,1)}) %all-gather.6.cloned.1.call-update) | async-done | bytes 13107216 | tf_op jit(solution)/shard_map/all_gather | solution.py:312
  170.6 10.4 %shard_map.129 = (f32[256,3200]{1,0:T(8,128)}, f32[256,1]{1,0:T(8,128)}) custom-call(bf16[8,2,256,128]{3,2,1,0:T(8,128)(2,1)} %bitcast.47, bf16[8,2,128,3200]{3,2,1,0:T(8,128)(2,1)} %bitcast.44, bf16[256,3200]{1,0:T(8,128)(2,1)} %reshape.119.res_ref, f32[1,3200]{1,0:T(1,128)} %reshape.120.ls_ref), custom_call_target="tpu_custom_call" | custom-call | flops 3355443200 | bytes 18022400 | tf_op jit(solution)/shard_map/pallas_call | solution.py:233
  181.0 1.0 reduce.4
  182.0 0.1 reshape.122
  182.1 0.1 reduce_sum.55
  182.2 0.1 sub.23
  182.3 0.1 sub.24
  182.4 0.0 copy-start.2
  182.4 4.6 %reshape.121 = f32[64,12800]{1,0:T(8,128)} reshape(f32[256,3200]{1,0:T(8,128)} %get-tuple-element.7) | data formatting | bytes 6553600 | tf_op jit(solution)/shard_map/reshape | solution.py:331
  187.1 0.5 multiply_reduce_fusion
  187.5 0.1 reduce_sum.57
  187.7 0.1 reduce_sum.58
  187.8 0.1 copy-done.3
  187.9 0.0 copy-done.4
  187.9 2.5 add_convert_fusion.1
  190.4 2.8 all_to_all.12
  193.2 0.0 copy-start.9
  193.2 0.0 copy-start.10
  193.2 1.7 copy.40
  194.9 6.7 %all-to-all-start = ((bf16[64,16,800]{2,0,1:T(8,128)(2,1)}), bf16[64,16,800]{2,0,1:T(8,128)(2,1)S(1)}, u32[]{:S(2)}, u32[]{:S(2)}) async-start(bf16[64,16,800]{2,0,1:T(8,128)(2,1)} %copy.40), calls=%async_computation | async-start | bytes 3670016 | tf_op jit(solution)/shard_map/all_to_all | solution.py:344
  201.6 0.0 reduce-scatter.2.cloned.1.call-start
  201.6 0.5 broadcast.104
  202.1 0.7 reduce.10
  202.8 0.1 reshape_squeeze.20
  202.9 0.1 fusion.16
  203.0 0.1 mul.111
  203.1 0.0 copy-done.10
  203.1 0.6 dynamic_slice.3
  203.7 0.6 compare_convert_fusion
  204.4 0.1 broadcast_multiply_fusion
  204.4 23.5 %all-to-all-done = bf16[64,16,800]{2,0,1:T(8,128)(2,1)S(1)} async-done(((bf16[64,16,800]{2,0,1:T(8,128)(2,1)}), bf16[64,16,800]{2,0,1:T(8,128)(2,1)S(1)}, u32[]{:S(2)}, u32[]{:S(2)}) %all-to-all-start) | async-done | bytes 1638432 | tf_op jit(solution)/shard_map/all_to_all | solution.py:344
  227.9 1.3 fusion.10
  229.2 19.2 %add_convert_fusion = bf16[16,64,6144]{2,1,0:T(8,128)(2,1)} fusion(f32[16,64]{1,0:T(8,128)S(1)} %broadcast_multiply_fusion, bf16[800,6144]{1,0:T(8,128)(2,1)} %param.23, bf16[16,64,800]{2,0,1:T(8,128)(2,1)S(1)} %fusion.10), kind=kOutput, calls=%fused_computation | convolution fusion | flops 10078912512 | bytes 24055808 | tf_op jit(solution)/shard_map/dot_general | solution.py:355
  248.4 0.0 reduce-scatter.2.cloned.1.call-update
  248.5 93.3 %reduce-scatter.2.cloned.1.call-done = bf16[64,6144]{1,0:T(8,128)(2,1)} async-done(((bf16[1024,6144]{1,0:T(8,128)(2,1)}), bf16[64,6144]{1,0:T(8,128)(2,1)}) %reduce-scatter.2.cloned.1.call-update) | async-done | bytes 786448 | tf_op jit(solution)/shard_map/reduce_scatter | solution.py:361
  341.8 2.4 fusion.13
  (15 shorter events, 0.1 us)
Async XLA Ops:
  6.5 78.4 %all-gather.4.cloned.1.call-start = ((), (), s32[]{:S(2)}) async-start(), calls=%async_computation.2 | async-start | bytes 14745600 | tf_op jit(solution)/shard_map/all_gather | solution.py:280
  8.4 4.0 %copy-start.1 = (bf16[1,256,3200]{2,1,0:T(8,128)(2,1)S(1)}, bf16[1,256,3200]{2,1,0:T(8,128)(2,1)}, u32[]{:S(2)}) copy-start(bf16[1,256,3200]{2,1,0:T(8,128)(2,1)} %param.13) | copy-start | bytes 4915204
  11.6 1.5 copy-start.7
  11.6 159.0 %all-gather.6.cloned.1.call-start = ((), (), s32[]{:S(2)}) async-start(), calls=%async_computation.4 | async-start | bytes 14745600 | tf_op jit(solution)/shard_map/all_gather | solution.py:312
  14.7 2.7 copy-start.6
  14.7 3.3 copy-start.8
  100.6 2.6 copy-start
  182.4 4.7 %copy-start.2 = (f32[256,3200]{1,0:T(8,128)S(1)}, f32[256,3200]{1,0:T(8,128)}, u32[]{:S(2)}) copy-start(f32[256,3200]{1,0:T(8,128)} %get-tuple-element.7) | copy-start | bytes 9830404
  187.1 0.8 copy-start.3
  187.1 0.8 copy-start.4
  193.2 9.0 %copy-start.9 = (s32[1,256]{1,0:T(1,128)S(1)}, s32[1,256]{1,0:T(1,128)}, u32[]{:S(2)}) copy-start(s32[1,256]{1,0:T(1,128)} %param.20) | copy-start | bytes 3076
  193.2 9.9 %copy-start.10 = (s32[16]{0:T(128)S(1)}, s32[16]{0:T(128)}, u32[]{:S(2)}) copy-start(s32[16]{0:T(128)} %param.25) | copy-start | bytes 196
  194.9 33.1 %all-to-all-start = ((bf16[64,16,800]{2,0,1:T(8,128)(2,1)}), bf16[64,16,800]{2,0,1:T(8,128)(2,1)S(1)}, u32[]{:S(2)}, u32[]{:S(2)}) async-start(bf16[64,16,800]{2,0,1:T(8,128)(2,1)} %copy.40), calls=%async_computation | async-start | bytes 3670016 | tf_op jit(solution)/shard_map/all_to_all | solution.py:344
  201.6 140.2 %reduce-scatter.2.cloned.1.call-start = ((), (), s32[]{:S(2)}) async-start(), calls=%async_computation.3 | async-start | bytes 13369344 | tf_op jit(solution)/shard_map/reduce_scatter | solution.py:361
  248.4 93.4 %copy-start.5 = (f32[6144]{0:T(1024)S(1)}, f32[6144]{0:T(1024)}, u32[]{:S(2)}) copy-start(f32[6144]{0:T(1024)} %param.24) | copy-start | bytes 73732
Sparse Core Ops, SparseCore 0:
  11.7 73.1 all-gather.3
  86.6 83.9 all-gather.5
  248.6 93.1 reduce-scatter.1
